TPU v7x, 32 devices: a whole 2x2x4 slice. The times are simulated.
32 devices in a mesh: tm: 2 (over x), diamond: 2 (over y), tile: 8 (over z, core).
Axes of the slice: x: 2, y: 2, z: 4, core: 2. Of those that a mesh axis runs over, the one named last changes fastest.
Arguments:
- activations: bfloat16 [8, 2, 32, 64, 256], P('tm', 'diamond', 'tile'), may hold values from -6 to 6
- upstream: bfloat16 [8, 2, 32, 64, 256], P('tm', 'diamond', 'tile'), may hold values from -16 to 16
- hex_weight: bfloat16 [7, 64, 64], replicated, may hold values from -0.25 to 0.25
- time_weight: bfloat16 [3, 64, 64], replicated, may hold values from -0.4375 to 0.4375
- left_map: int32 [2, 32], replicated, may hold values from 0 to 31, each once within a row
- right_map: int32 [2, 32], replicated, may hold values from 0 to 31, each once within a row
Outputs:
- grad_input: bfloat16 [8, 2, 32, 64, 256], P('tm', 'diamond', 'tile')
- grad_hex: float32 [7, 64, 64], replicated
- grad_time: float32 [3, 64, 64], replicated
Inputs may be any that keep to these rules, and one draw needn't show every extreme that they name: Each row of left_map holds every number of 0 to 31 once. Each row of right_map holds every number of 0 to 31 once.
All inputs are finite; a program needn't handle non-finite values.
Results may differ from a plain program's by a relative error of at most 0.0035.
Values may be sent and summed in bfloat16 or wider, within the bound.
A program may use at most 64 MiB of HBM per device.

v0:
```python
import jax
import jax.numpy as jnp
from jax import lax
from jax.sharding import PartitionSpec as P

OFFSETS = ((0, 0), (0, 1), (0, -1), (1, 0), (-1, 0), (1, -1), (-1, 1))


def from_behind(block, axis, distance):
    devices = range(lax.axis_size(axis))
    route = [((i - distance) % len(devices), i) for i in devices]
    return lax.ppermute(block, axis, route)


def with_halo(x, sides, width):
    for axis, dim in sides:
        size, length = (lax.axis_size(axis), x.shape[dim])
        up = [(i, (i + 1) % size) for i in range(size - 1)]
        down = [(j, i) for i, j in up]
        last = lax.slice_in_dim(x, length - width, length, axis=dim)
        initial = lax.slice_in_dim(x, 0, width, axis=dim)
        before = lax.ppermute(last, axis, up)
        after = lax.ppermute(initial, axis, down)
        x = jnp.concatenate([before, x, after], axis=dim)
    return x


def passed_along(block, axis, distance):
    devices = range(lax.axis_size(axis))
    route = [(i - distance, i) for i in devices if i - distance in devices]
    return lax.ppermute(block, axis, route)


def silu_slope(hidden):
    sigmoid = jax.nn.sigmoid(hidden)
    return sigmoid * (1.0 + hidden * (1.0 - sigmoid))


def shards(activations, upstream, hex_weight, time_weight, left_map, right_map):
    field = activations[:, 0]
    cotangent = upstream[:, 0]
    frames, tile_rows, channels, columns = field.shape
    chart = lax.axis_index("diamond")
    first_row = lax.axis_index("tile") * tile_rows
    chart_rows = tile_rows * lax.axis_size("tile")
    own_left = lax.dynamic_slice(left_map, (chart, first_row), (1, tile_rows))[0]
    own_right = lax.dynamic_slice(right_map, (chart, first_row), (1, tile_rows))[0]
    strips = (
        lax.all_gather(field[..., 0], "tile", axis=1, tiled=True),
        lax.all_gather(field[..., columns - 1], "tile", axis=1, tiled=True),
    )
    prev_right = from_behind(strips[1], "diamond", 1)
    next_left = from_behind(strips[0], "diamond", -1)
    ghost_left = jnp.take(prev_right, own_left, axis=1)
    ghost_right = jnp.take(next_left, own_right, axis=1)
    widened = jnp.concatenate([ghost_left[..., None], field, ghost_right[..., None]], axis=-1)
    depth = 1
    margin = depth - 1
    span_rows = tile_rows + 2 * margin
    padded = with_halo(widened, (("tile", 1),), depth)
    hidden = jnp.zeros((frames, span_rows, channels, columns), jnp.float32)
    for number, (step_row, step_col) in enumerate(OFFSETS):
        window = padded[
            :, 1 + step_row : 1 + step_row + span_rows, :, 1 + step_col : 1 + step_col + columns
        ]
        hidden = hidden + jnp.einsum(
            "frcx,cd->frdx", window, hex_weight[number], preferred_element_type=jnp.float32
        )
    active = jax.nn.silu(hidden).astype(jnp.bfloat16)
    framed = with_halo(cotangent, (("tm", 0),), 1)
    grad_act = jnp.zeros((frames, span_rows, channels, columns), jnp.float32)
    time_terms = []
    for number in range(3):
        shifted = framed[2 - number : 2 - number + frames]
        grad_act = grad_act + jnp.einsum(
            "frdx,cd->frcx", shifted, time_weight[number], preferred_element_type=jnp.float32
        )
        time_terms.append(
            jnp.einsum("frcx,frdx->cd", active, shifted, preferred_element_type=jnp.float32)
        )
    grad_wide = (grad_act * silu_slope(hidden)).astype(jnp.bfloat16)
    hex_terms = []
    for number, (step_row, step_col) in enumerate(OFFSETS):
        begin = 1 + margin + step_row
        window = padded[:, begin : begin + tile_rows, :, 1 + step_col : 1 + step_col + columns]
        hex_terms.append(
            jnp.einsum("frcx,frdx->cd", window, grad_wide, preferred_element_type=jnp.float32)
        )
    spread = jnp.zeros((frames, tile_rows + 2, channels, columns + 2), jnp.float32)
    for number, (step_row, step_col) in enumerate(OFFSETS):
        spread = spread.at[
            :, 1 + step_row : 1 + step_row + tile_rows, :, 1 + step_col : 1 + step_col + columns
        ].add(
            jnp.einsum(
                "frdx,cd->frcx", grad_wide, hex_weight[number], preferred_element_type=jnp.float32
            )
        )
    from_below = passed_along(spread[:, 0].astype(jnp.bfloat16), "tile", -1).astype(jnp.float32)
    from_above = passed_along(spread[:, tile_rows + 1].astype(jnp.bfloat16), "tile", 1).astype(
        jnp.float32
    )
    owned = spread[:, 1 : tile_rows + 1]
    owned = owned.at[:, 0].add(from_above)
    owned = owned.at[:, tile_rows - 1].add(from_below)
    total = cotangent.astype(jnp.float32) + owned[..., 1 : columns + 1]
    left_grad = owned[..., 0]
    right_grad = owned[..., columns + 1]
    strip_left = (
        jnp.zeros((frames, chart_rows, channels), jnp.float32).at[:, own_left].set(left_grad)
    )
    strip_right = (
        jnp.zeros((frames, chart_rows, channels), jnp.float32).at[:, own_right].set(right_grad)
    )
    moved_left = from_behind(strip_left.astype(jnp.bfloat16), "diamond", -1).astype(
        strip_left.dtype
    )
    moved_right = from_behind(strip_right.astype(jnp.bfloat16), "diamond", 1).astype(
        strip_right.dtype
    )
    into_last, into_first = (
        lax.psum_scatter(
            moved_left.astype(jnp.bfloat16), "tile", scatter_dimension=1, tiled=True
        ).astype(jnp.float32),
        lax.psum_scatter(
            moved_right.astype(jnp.bfloat16), "tile", scatter_dimension=1, tiled=True
        ).astype(jnp.float32),
    )
    total = total.at[..., columns - 1].add(into_last)
    total = total.at[..., 0].add(into_first)
    hex_local = jnp.stack(hex_terms)
    time_local = jnp.stack(time_terms)
    grad_hex, grad_time = lax.psum((hex_local, time_local), ("tm", "diamond", "tile"))
    return (total.astype(jnp.bfloat16)[:, None], grad_hex, grad_time)


def solution(mesh):
    in_specs = (
        P("tm", "diamond", "tile", None, None),
        P("tm", "diamond", "tile", None, None),
        P(),
        P(),
        P(),
        P(),
    )
    out_specs = (P("tm", "diamond", "tile", None, None), P(), P())
    return jax.shard_map(shards, mesh=mesh, in_specs=in_specs, out_specs=out_specs, check_vma=False)
```

profile of v0, /device:TPU:1, one launch (start us, length us, event | category | flops | bytes accessed | tf_op | source)
XLA Modules:
  0.0 313.1 jit_solution(10565177064639616680)
XLA Ops:
  8.4 25.0 %all-gather = bf16[4,32,64,1]{3,2,1,0:T(8,128)(2,1)S(1)} all-gather(bf16[4,4,64,1]{3,2,1,0:T(8,128)(2,1)S(1)} %get-tuple-element.164), channel_id=2, replica_groups=mesh['tm'=2,'diamond'=2,'tile'=8] {'tile'}, dimensions={1}, use_global_device_ids=true | all-gather | bytes 18432 | tf_op jit(solution)/shard_map/all_gather | solution.py:49
  34.5 1.3 collective-permute-start.2
  35.8 23.0 %all-gather.1 = bf16[4,32,64,1]{3,2,1,0:T(8,128)(2,1)S(1)} all-gather(bf16[4,4,64,1]{3,2,1,0:T(8,128)(2,1)S(1)} %get-tuple-element.163), channel_id=3, replica_groups=mesh['tm'=2,'diamond'=2,'tile'=8] {'tile'}, dimensions={1}, use_global_device_ids=true | all-gather | bytes 18432 | tf_op jit(solution)/shard_map/all_gather | solution.py:50
  60.8 3.9 %collective-permute-start.1 = (bf16[1,4,64,256]{3,2,1,0:T(8,128)(2,1)}, bf16[1,4,64,256]{3,2,1,0:T(8,128)(2,1)}, u32[]{:S(2)}, u32[]{:S(2)}) collective-permute-start(bf16[1,4,64,256]{3,2,1,0:T(8,128)(2,1)} %get-tuple-element.162), channel_id=1, source_target_pairs={{0,16},{1,17},{2,18},{3,19},{4,20},{5,21},{6,22},{7,23},{8,24},{9,... | collective-permute-start | bytes 393224 | tf_op jit(solution)/shard_map/ppermute | solution.py:22
  64.7 1.3 collective-permute-start
  68.5 2.7 and_reduce_fusion
  75.6 2.8 collective-permute-start.4
  78.4 3.1 collective-permute-start.5
  85.9 1.5 multiply_convert_fusion
  87.4 1.5 fusion.15
  90.1 1.4 fusion.9
  91.9 7.1 %scatter-add.39 = f32[4,6,64,258]{3,2,0,1:T(8,128)S(1)} dynamic-update-slice(f32[4,6,64,258]{3,2,0,1:T(8,128)S(1)} %scatter-add.36, f32[4,4,64,256]{3,2,0,1:T(8,128)} %fusion.9, s32[]{:T(128)} %constant.332.clone.1, s32[]{:T(128)} %constant.338.clone.1, s32[]{:T(128)} %constant.332.clone.1, s32[]{:T(128)} %constant.333.clone.1) | dynamic-update-slice | bytes 2097156 | tf_op jit(solution)/shard_map/scatter-add | solution.py:93
  99.3 1.3 fusion.12
  100.7 7.1 %scatter-add.41 = f32[4,6,64,258]{3,2,0,1:T(8,128)S(1)} dynamic-update-slice(f32[4,6,64,258]{3,2,0,1:T(8,128)S(1)} %fusion.11, f32[4,4,64,256]{3,2,0,1:T(8,128)} %fusion.12, s32[]{:T(128)} %constant.332.clone.1, s32[]{:T(128)} %constant.333.clone.1, s32[]{:T(128)} %constant.332.clone.1, s32[]{:T(128)} %constant.338.clone.1) | dynamic-update-slice | bytes 2097156 | tf_op jit(solution)/shard_map/scatter-add | solution.py:93
  107.7 2.7 add_select_fusion.1
  110.4 7.8 %scatter-add.44 = f32[4,6,64,258]{3,2,0,1:T(8,128)S(1)} dynamic-update-slice(f32[4,6,64,258]{3,2,0,1:T(8,128)S(1)} %scatter-add.41, f32[4,4,64,256]{3,2,0,1:T(8,128)} %add_select_fusion.1, s32[]{:T(128)} %constant.332.clone.1, s32[]{:T(128)S(1)} %bitcast.366, s32[]{:T(128)} %constant.332.clone.1, s32[]{:T(128)} %bitcast.61) | dynamic-update-slice | bytes 2097156 | tf_op jit(solution)/shard_map/scatter-add | solution.py:93
  118.5 3.2 %add_select_fusion = f32[4,4,64,256]{3,2,0,1:T(8,128)} fusion(f32[4,6,64,258]{3,2,0,1:T(8,128)S(1)} %fusion.14, s32[]{:T(128)} %bitcast.66, s32[]{:T(128)} %bitcast.67, pred[]{:T(512)} %get-tuple-element.147, bf16[4,4,64,256]{3,2,1,0:T(8,128)(2,1)S(1)} %fusion.15, bf16[7,64,64]{2,1,0:T(8,128)(2,1)S(1)} %copy-done.12), kind=kOutput, calls=%fused_computation.4 | convolution fusion | flops 34078720 | bytes 2637833 | tf_op jit(solution)/shard_map/frdx,cd->frcx/dot_general | solution.py:94
  121.7 8.4 %scatter-add.46 = f32[4,6,64,258]{3,2,0,1:T(8,128)S(1)} dynamic-update-slice(f32[4,6,64,258]{3,2,0,1:T(8,128)S(1)} %fusion.14, f32[4,4,64,256]{3,2,0,1:T(8,128)} %add_select_fusion, s32[]{:T(128)} %constant.332.clone.1, s32[]{:T(128)} %bitcast.66, s32[]{:T(128)} %constant.332.clone.1, s32[]{:T(128)} %bitcast.67) | dynamic-update-slice | bytes 2097156 | tf_op jit(solution)/shard_map/scatter-add | solution.py:93
  131.3 1.3 slice.528
  138.6 1.4 convolution_bitcast_fusion.18
  140.0 1.8 slice_bitcast_fusion.1
  141.8 4.4 %collective-permute-start.6 = (bf16[4,64,258]{2,1,0:T(8,128)(2,1)}, bf16[4,64,258]{2,1,0:T(8,128)(2,1)}, u32[]{:S(2)}, u32[]{:S(2)}) collective-permute-start(bf16[4,64,258]{2,1,0:T(8,128)(2,1)} %get-tuple-element.156), channel_id=1, source_target_pairs={{0,1},{1,2},{2,3},{3,4},{4,5},{5,6},{6,7},{8,9},{9,10},{10,11},{11... | collective-permute-start | bytes 396296 | tf_op jit(solution)/shard_map/ppermute | solution.py:31
  146.1 1.9 collective-permute-start.7
  148.1 1.4 convolution_bitcast_fusion.17
  150.7 42.3 %psum.15 = f32[3,64,64]{2,1,0:T(8,128)} all-reduce(f32[3,64,64]{2,1,0:T(8,128)S(1)} %pad_maximum_fusion.16), channel_id=1, replica_groups=mesh['tm'=2,'diamond'=2,'tile'=8] {'tm','diamond','tile'}, use_global_device_ids=true, to_apply=%region_7.9 | all-reduce | flops 12288 | bytes 98304 | tf_op jit(solution)/shard_map/psum | solution.py:132
  192.9 73.2 %all-reduce.6.cloned.1.call-done = f32[7,64,64]{1,2,0:T(8,128)} async-done(((f32[7,64,64]{1,2,0:T(8,128)}), f32[7,64,64]{1,2,0:T(8,128)}) %all-reduce.6.cloned.1.call-update) | async-done | bytes 114704 | tf_op jit(solution)/shard_map/psum | solution.py:132
  266.1 1.8 copy.133
  267.8 1.7 fusion.33
  269.5 1.5 copy.119
  276.8 1.4 collective-permute-done.9
  278.1 23.9 %all-reduce.3 = (bf16[4,32,64]{2,0,1:T(4,128)(2,1)S(1)}, bf16[4,32,64]{2,0,1:T(4,128)(2,1)S(1)}) all-reduce(bf16[4,32,64]{2,0,1:T(4,128)(2,1)S(1)} %collective-permute-done.8, bf16[4,32,64]{2,0,1:T(4,128)(2,1)S(1)} %collective-permute-done.9), channel_id=4, replica_groups=mesh['tm'=2,'diamond'=2,'tile'=8] {'tile'}, use_global_device_ids=true, to_apply=%region_3.5.clone | all-reduce | flops 16384 | bytes 65536
  302.8 1.9 scatter-add.51
  (116 shorter events, 33.3 us)
Async XLA Ops:
  7.2 258.9 %all-reduce.6.cloned.1.call-start = ((), (), s32[]{:S(2)}) async-start(), calls=%async_computation | async-start | bytes 458752 | tf_op jit(solution)/shard_map/psum | solution.py:132
  34.5 38.1 %collective-permute-start.2 = (bf16[4,32,64]{2,0,1:T(4,128)(2,1)S(1)}, bf16[4,32,64]{2,0,1:T(4,128)(2,1)S(1)}, u32[]{:S(2)}, u32[]{:S(2)}) collective-permute-start(bf16[4,32,64]{2,0,1:T(4,128)(2,1)S(1)} %bitcast.359), channel_id=1, source_target_pairs={{8,0},{0,8},{9,1},{1,9},{10,2},{2,10},{11,3},{3,11},{12,4},{4,12},... | collective-permute-start | bytes 49160 | tf_op jit(solution)/shard_map/ppermute | solution.py:12
  35.8 24.3 %copy-start.1 = (bf16[4,1,4,64,256]{4,3,2,1,0:T(8,128)(2,1)S(1)}, bf16[4,1,4,64,256]{4,3,2,1,0:T(8,128)(2,1)}, u32[]{:S(2)}) copy-start(bf16[4,1,4,64,256]{4,3,2,1,0:T(8,128)(2,1)} %param.31) | copy-start | bytes 1572868
  35.8 30.3 %copy-start.14 = (s32[2,32]{1,0:T(2,128)S(1)}, s32[2,32]{1,0:T(2,128)}, u32[]{:S(2)}) copy-start(s32[2,32]{1,0:T(2,128)} %param.35) | copy-start | bytes 772
  35.8 30.4 %copy-start.15 = (s32[2,32]{1,0:T(2,128)S(1)}, s32[2,32]{1,0:T(2,128)}, u32[]{:S(2)}) copy-start(s32[2,32]{1,0:T(2,128)} %param.34) | copy-start | bytes 772
  58.8 9.7 %copy-start.16 = (s32[4]{0:T(128)S(1)}, s32[4]{0:T(128)}, u32[]{:S(2)}) copy-start(s32[4]{0:T(128)} %constant.340.clone.1) | copy-start | bytes 52
  58.8 12.5 %copy-start.17 = (u32[32]{0:T(128)S(1)}, u32[32]{0:T(128)}, u32[]{:S(2)}) copy-start(u32[32]{0:T(128)} %constant.350) | copy-start | bytes 388
  58.8 15.7 %copy-start = (bf16[4,1,4,64,256]{4,3,2,1,0:T(8,128)(2,1)S(1)}, bf16[4,1,4,64,256]{4,3,2,1,0:T(8,128)(2,1)}, u32[]{:S(2)}) copy-start(bf16[4,1,4,64,256]{4,3,2,1,0:T(8,128)(2,1)} %param.30) | copy-start | bytes 1572868
  59.8 13.7 %collective-permute-start.3 = (bf16[4,32,64]{2,0,1:T(4,128)(2,1)S(1)}, bf16[4,32,64]{2,0,1:T(4,128)(2,1)S(1)}, u32[]{:S(2)}, u32[]{:S(2)}) collective-permute-start(bf16[4,32,64]{2,0,1:T(4,128)(2,1)S(1)} %bitcast.358), channel_id=1, source_target_pairs={{8,0},{0,8},{9,1},{1,9},{10,2},{2,10},{11,3},{3,11},{12,4},{4,12},... | collective-permute-start | bytes 49160 | tf_op jit(solution)/shard_map/ppermute | solution.py:12
  60.8 13.9 %copy-start.12 = (bf16[7,64,64]{2,1,0:T(8,128)(2,1)S(1)}, bf16[7,64,64]{2,1,0:T(8,128)(2,1)}, u32[]{:S(2)}) copy-start(bf16[7,64,64]{2,1,0:T(8,128)(2,1)} %param.32) | copy-start | bytes 172036
  60.8 21.0 %collective-permute-start.1 = (bf16[1,4,64,256]{3,2,1,0:T(8,128)(2,1)}, bf16[1,4,64,256]{3,2,1,0:T(8,128)(2,1)}, u32[]{:S(2)}, u32[]{:S(2)}) collective-permute-start(bf16[1,4,64,256]{3,2,1,0:T(8,128)(2,1)} %get-tuple-element.162), channel_id=1, source_target_pairs={{0,16},{1,17},{2,18},{3,19},{4,20},{5,21},{6,22},{7,23},{8,24},{9,... | collective-permute-start | bytes 393224 | tf_op jit(solution)/shard_map/ppermute | solution.py:22
  64.7 22.7 %collective-permute-start = (bf16[1,4,64,256]{3,2,1,0:T(8,128)(2,1)}, bf16[1,4,64,256]{3,2,1,0:T(8,128)(2,1)}, u32[]{:S(2)}, u32[]{:S(2)}) collective-permute-start(bf16[1,4,64,256]{3,2,1,0:T(8,128)(2,1)} %get-tuple-element.161), channel_id=1, source_target_pairs={{16,0},{17,1},{18,2},{19,3},{20,4},{21,5},{22,6},{23,7},{24,8},{25... | collective-permute-start | bytes 393224 | tf_op jit(solution)/shard_map/ppermute | solution.py:23
  73.5 10.4 %copy-start.7 = (bf16[4,4,64,1]{3,2,1,0:T(8,128)(2,1)}, bf16[4,4,64,1]{3,2,1,0:T(8,128)(2,1)S(1)}, u32[]{:S(2)}) copy-start(bf16[4,4,64,1]{3,2,1,0:T(8,128)(2,1)S(1)} %copy.92) | copy-start | bytes 6148
  74.4 9.5 %copy-start.9 = (bf16[4,4,64,1]{3,2,1,0:T(8,128)(2,1)}, bf16[4,4,64,1]{3,2,1,0:T(8,128)(2,1)S(1)}, u32[]{:S(2)}) copy-start(bf16[4,4,64,1]{3,2,1,0:T(8,128)(2,1)S(1)} %copy.96) | copy-start | bytes 6148
  75.6 6.2 %copy-start.13 = (bf16[3,64,64]{2,1,0:T(8,128)(2,1)S(1)}, bf16[3,64,64]{2,1,0:T(8,128)(2,1)}, u32[]{:S(2)}) copy-start(bf16[3,64,64]{2,1,0:T(8,128)(2,1)} %param.33) | copy-start | bytes 73732
  75.6 7.4 %collective-permute-start.4 = (bf16[4,1,64,258]{3,2,1,0:T(8,128)(2,1)S(1)}, bf16[4,1,64,258]{3,2,1,0:T(8,128)(2,1)S(1)}, u32[]{:S(2)}, u32[]{:S(2)}) collective-permute-start(bf16[4,1,64,258]{3,2,1,0:T(8,128)(2,1)S(1)} %get-tuple-element.159), channel_id=1, source_target_pairs={{1,0},{2,1},{3,2},{4,3},{5,4},{6,5},{7,6},{9,8},{10,9},{11,10},{12... | collective-permute-start | bytes 396296 | tf_op jit(solution)/shard_map/ppermute | solution.py:23
  78.4 5.5 %collective-permute-start.5 = (bf16[4,1,64,258]{3,2,1,0:T(8,128)(2,1)S(1)}, bf16[4,1,64,258]{3,2,1,0:T(8,128)(2,1)S(1)}, u32[]{:S(2)}, u32[]{:S(2)}) collective-permute-start(bf16[4,1,64,258]{3,2,1,0:T(8,128)(2,1)S(1)} %get-tuple-element.160), channel_id=1, source_target_pairs={{0,1},{1,2},{2,3},{3,4},{4,5},{5,6},{6,7},{8,9},{9,10},{10,11},{11... | collective-permute-start | bytes 396296 | tf_op jit(solution)/shard_map/ppermute | solution.py:22
  84.6 1.1 copy-start.3
  84.6 1.3 copy-start.5
  131.3 1.3 copy-start.8
  131.3 2.3 copy-start.10
  132.6 2.0 copy-start.6
  132.6 3.0 copy-start.4
  135.6 2.9 copy-start.2
  138.5 10.9 %copy-start.11 = (bf16[4,4,64,256]{3,2,1,0:T(8,128)(2,1)S(1)}, bf16[4,4,64,256]{3,2,1,0:T(8,128)(2,1)}, u32[]{:S(2)}) copy-start(bf16[4,4,64,256]{3,2,1,0:T(8,128)(2,1)} %get-tuple-element.167) | copy-start | bytes 1572868
  141.8 126.1 %collective-permute-start.6 = (bf16[4,64,258]{2,1,0:T(8,128)(2,1)}, bf16[4,64,258]{2,1,0:T(8,128)(2,1)}, u32[]{:S(2)}, u32[]{:S(2)}) collective-permute-start(bf16[4,64,258]{2,1,0:T(8,128)(2,1)} %get-tuple-element.156), channel_id=1, source_target_pairs={{0,1},{1,2},{2,3},{3,4},{4,5},{5,6},{6,7},{8,9},{9,10},{10,11},{11... | collective-permute-start | bytes 396296 | tf_op jit(solution)/shard_map/ppermute | solution.py:31
  146.1 124.9 %collective-permute-start.7 = (bf16[4,64,258]{2,1,0:T(8,128)(2,1)}, bf16[4,64,258]{2,1,0:T(8,128)(2,1)}, u32[]{:S(2)}, u32[]{:S(2)}) collective-permute-start(bf16[4,64,258]{2,1,0:T(8,128)(2,1)} %get-tuple-element.155), channel_id=1, source_target_pairs={{1,0},{2,1},{3,2},{4,3},{5,4},{6,5},{7,6},{9,8},{10,9},{11,10},{12... | collective-permute-start | bytes 396296 | tf_op jit(solution)/shard_map/ppermute | solution.py:31
  273.4 3.4 %collective-permute-start.8 = (bf16[4,32,64]{2,0,1:T(4,128)(2,1)S(1)}, bf16[4,32,64]{2,0,1:T(4,128)(2,1)S(1)}, u32[]{:S(2)}, u32[]{:S(2)}) collective-permute-start(bf16[4,32,64]{2,0,1:T(4,128)(2,1)S(1)} %convert_element_type.38), channel_id=1, source_target_pairs={{8,0},{0,8},{9,1},{1,9},{10,2},{2,10},{11,3},{3,11},{12,4},{4,12},... | collective-permute-start | bytes 49160 | tf_op jit(solution)/shard_map/ppermute | solution.py:12
  275.3 2.8 collective-permute-start.9
Sparse Core Ops, SparseCore 0:
  138.7 127.3 all-reduce.5
where the time goes:
time: 318 us; the launch traced here: 313 us
  blocking collectives  114 us (36%)
  waiting for transfers between devices  76.2 us (24%)
  local copies, waits for them, and re-layouts  49.8 us (16%)
  matrix products  27.6 us (9%)
  starting transfers between devices  20.6 us (6%)
  between operations  15.2 us (5%)
  other arithmetic  9.59 us (3%)
    psum x1, waiting for transfers between devices, shards(): lax.psum((hex_local, time_local), ('tm', 'diamond', 'tile'))  73.2 us
    psum x1, blocking collectives, shards(): lax.psum((hex_local, time_local), ('tm', 'diamond', 'tile'))  42.3 us
    scatter-add x5, local copies, waits for them, and re-layouts, shards(): spread = spread.at[:, 1 + step_row:1 + step_row + tile_rows, :, 1 + step_...  30.8 us
    all_gather x1, blocking collectives, shards(): lax.all_gather(field[..., 0], 'tile', axis=1, tiled=True)  25 us
    unnamed x1, blocking collectives  23.9 us
    all_gather x1, blocking collectives, shards(): lax.all_gather(field[..., columns - 1], 'tile', axis=1, tiled=True)  23 us
    dot_general x7, matrix products, shards(): jnp.einsum('frdx,cd->frcx', grad_wide, hex_weight[number], preferred_elem...  9.43 us
    ppermute x2, starting transfers between devices, with_halo(): before = lax.ppermute(last, axis, up)  7.02 us
  transfers between devices with their start and end apart: 11, of which 4 were waited for; matrix products, arithmetic and copies ran while one was open for 9% of the time, Pallas kernels for 0%

commit v1 on v0

v1 whole, which is shorter than its diff:
```python
import jax
import jax.numpy as jnp
from jax import lax
from jax.experimental import pallas as pl
from jax.experimental.pallas import tpu as pltpu
from jax.sharding import PartitionSpec as P

OFFSETS = ((0, 0), (0, 1), (0, -1), (1, 0), (-1, 0), (1, -1), (-1, 1))
ANY = pl.BlockSpec(memory_space=pl.ANY)
VMEM = pl.BlockSpec(memory_space=pltpu.VMEM)


def remote(src, dst, send_sem, recv_sem, device_id):
    return pltpu.make_async_remote_copy(
        src_ref=src,
        dst_ref=dst,
        send_sem=send_sem,
        recv_sem=recv_sem,
        device_id=device_id,
        device_id_type=pl.DeviceIdType.MESH,
    )


def line_copies(axis, to_next, at_next, to_prev, at_prev, send, recv):
    me, size = lax.axis_index(axis), lax.axis_size(axis)
    up = remote(to_next, at_next, send.at[0], recv.at[0], {axis: lax.rem(me + 1, size)})
    down = remote(to_prev, at_prev, send.at[1], recv.at[1], {axis: lax.rem(me + size - 1, size)})

    def start():
        pl.when(me < size - 1)(up.start)
        pl.when(me > 0)(down.start)

    def wait():
        pl.when(me < size - 1)(up.wait_send)
        pl.when(me > 0)(down.wait_send)
        pl.when(me > 0)(up.wait_recv)
        pl.when(me < size - 1)(down.wait_recv)

    return start, wait


def seam_copies(strips, gathered, send, recv):
    me, tiles = lax.axis_index("tile"), lax.axis_size("tile")
    chart, charts = lax.axis_index("diamond"), lax.axis_size("diamond")
    sides = (lax.rem(chart + 1, charts), lax.rem(chart + charts - 1, charts))
    copies = []
    for step in range(tiles):
        other = lax.rem(me + step, tiles)
        for side in range(2):
            copies.append(
                remote(
                    strips.at[side],
                    gathered.at[side, me],
                    send.at[side, step],
                    recv.at[side, me],
                    {"diamond": sides[side], "tile": other},
                )
            )

    def start():
        for copy in copies:
            copy.start()

    def wait():
        for copy in copies:
            copy.wait_send()
        for side in range(2):
            for number in range(tiles):
                remote(
                    strips.at[side],
                    gathered.at[side, number],
                    send.at[side, 0],
                    recv.at[side, number],
                    {"diamond": sides[side], "tile": me},
                ).wait_recv()

    return start, wait


def first_exchange(
    strips, field, cotangent, gathered, above, below, before, after,
    seam_send, seam_recv, row_send, row_recv, frame_send, frame_recv,
):
    rows, frames = field.shape[1], field.shape[0]
    parts = (
        seam_copies(strips, gathered, seam_send, seam_recv),
        line_copies("tile", field.at[:, rows - 1], above, field.at[:, 0], below, row_send, row_recv),
        line_copies(
            "tm", cotangent.at[frames - 1], before, cotangent.at[0], after, frame_send, frame_recv
        ),
    )
    for start, _ in parts:
        start()
    for _, wait in parts:
        wait()


def last_exchange(
    strips, up_row, down_row, terms, gathered, above, below, sums,
    seam_send, seam_recv, row_send, row_recv,
    scattered, scatter_send, scatter_recv, group, group_send, group_recv, out_send, out_recv,
):
    me, tiles = lax.axis_index("tile"), lax.axis_size("tile")
    charts, lines = lax.axis_size("diamond"), lax.axis_size("tm")
    mine = lax.axis_index("tm") * charts + lax.axis_index("diamond")
    size = lines * charts

    def tile_copy(src, dst, send, recv, step):
        return remote(src, dst, send.at[step], recv, {"tile": lax.rem(me + step, tiles)})

    first = [
        tile_copy(
            terms.at[lax.rem(me + step, tiles)], scattered.at[me], scatter_send,
            scatter_recv.at[me], step,
        )
        for step in range(1, tiles)
    ]
    for copy in first:
        copy.start()
    parts = (
        seam_copies(strips, gathered, seam_send, seam_recv),
        line_copies("tile", down_row, above, up_row, below, row_send, row_recv),
    )
    for start, _ in parts:
        start()
    total = terms[me]
    for step in range(1, tiles):
        other = lax.rem(me + step, tiles)
        tile_copy(
            terms.at[other], scattered.at[other], scatter_send, scatter_recv.at[other], step
        ).wait_recv()
        total = total + scattered[other]
    group[mine] = total
    second = []
    for step in range(1, size):
        other = lax.rem(mine + step, size)
        target = {"tm": other // charts, "diamond": lax.rem(other, charts)}
        copy = remote(
            group.at[mine], group.at[mine], group_send.at[step], group_recv.at[mine], target
        )
        copy.start()
        second.append(copy)
    for step in range(1, size):
        other = lax.rem(mine + step, size)
        target = {"tm": other // charts, "diamond": lax.rem(other, charts)}
        remote(
            group.at[other], group.at[other], group_send.at[step], group_recv.at[other], target
        ).wait_recv()
    total = group[0]
    for number in range(1, size):
        total = total + group[number]
    sums[me] = total
    third = [
        tile_copy(sums.at[me], sums.at[me], out_send, out_recv.at[me], step)
        for step in range(1, tiles)
    ]
    for copy in third:
        copy.start()
    for step in range(1, tiles):
        other = lax.rem(me + step, tiles)
        tile_copy(sums.at[other], sums.at[other], out_send, out_recv.at[other], step).wait_recv()
    for copy in first + second + third:
        copy.wait_send()
    for _, wait in parts:
        wait()


def exchange_start(strips, field, cotangent):
    frames, rows, channels, columns = field.shape
    tiles = lax.axis_size("tile")
    dma = pltpu.SemaphoreType.DMA
    kind = field.dtype
    line = jax.ShapeDtypeStruct((frames, channels, columns), kind)
    frame = jax.ShapeDtypeStruct((rows, channels, columns), kind)
    return pl.pallas_call(
        first_exchange,
        out_shape=(
            jax.ShapeDtypeStruct((2, tiles) + strips.shape[1:], kind), line, line, frame, frame,
        ),
        in_specs=[ANY] * 3,
        out_specs=(ANY,) * 5,
        scratch_shapes=[
            dma((2, tiles)), dma((2, tiles)), dma((2,)), dma((2,)), dma((2,)), dma((2,)),
        ],
        compiler_params=pltpu.CompilerParams(has_side_effects=True),
        name="first_exchange",
    )(strips, field, cotangent)


def exchange_end(strips, up_row, down_row, terms):
    tiles = lax.axis_size("tile")
    size = lax.axis_size("tm") * lax.axis_size("diamond")
    dma = pltpu.SemaphoreType.DMA
    line = jax.ShapeDtypeStruct(up_row.shape, up_row.dtype)
    return pl.pallas_call(
        last_exchange,
        out_shape=(
            jax.ShapeDtypeStruct((2, tiles) + strips.shape[1:], strips.dtype), line, line,
            jax.ShapeDtypeStruct(terms.shape, terms.dtype),
        ),
        in_specs=[ANY, ANY, ANY, VMEM],
        out_specs=(ANY, ANY, ANY, VMEM),
        scratch_shapes=[
            dma((2, tiles)), dma((2, tiles)), dma((2,)), dma((2,)),
            pltpu.VMEM(terms.shape, terms.dtype), dma((tiles,)), dma((tiles,)),
            pltpu.VMEM((size,) + terms.shape[1:], terms.dtype), dma((size,)), dma((size,)),
            dma((tiles,)), dma((tiles,)),
        ],
        compiler_params=pltpu.CompilerParams(has_side_effects=True),
        name="last_exchange",
    )(strips, up_row, down_row, terms)


def silu_slope(hidden):
    sigmoid = jax.nn.sigmoid(hidden)
    return sigmoid * (1.0 + hidden * (1.0 - sigmoid))


def local_math(padded, framed, hex_weight, time_weight, frames, tile_rows, channels, columns):
    hidden = jnp.zeros((frames, tile_rows, channels, columns), jnp.float32)
    windows = [
        padded[:, 1 + a : 1 + a + tile_rows, :, 1 + b : 1 + b + columns] for a, b in OFFSETS
    ]
    for number in range(7):
        hidden = hidden + jnp.einsum(
            "frcx,cd->frdx", windows[number], hex_weight[number],
            preferred_element_type=jnp.float32,
        )
    active = jax.nn.silu(hidden).astype(jnp.bfloat16)
    grad_act = jnp.zeros((frames, tile_rows, channels, columns), jnp.float32)
    time_terms = []
    for number in range(3):
        shifted = framed[2 - number : 2 - number + frames]
        grad_act = grad_act + jnp.einsum(
            "frdx,cd->frcx", shifted, time_weight[number], preferred_element_type=jnp.float32
        )
        time_terms.append(
            jnp.einsum("frcx,frdx->cd", active, shifted, preferred_element_type=jnp.float32)
        )
    grad_wide = (grad_act * silu_slope(hidden)).astype(jnp.bfloat16)
    hex_terms = [
        jnp.einsum("frcx,frdx->cd", window, grad_wide, preferred_element_type=jnp.float32)
        for window in windows
    ]
    spread = None
    for number, (a, b) in enumerate(OFFSETS):
        term = jnp.einsum(
            "frdx,cd->frcx", grad_wide, hex_weight[number], preferred_element_type=jnp.float32
        )
        term = jnp.pad(term, ((0, 0), (1 + a, 1 - a), (0, 0), (1 + b, 1 - b)))
        spread = term if spread is None else spread + term
    return spread, jnp.stack(hex_terms + time_terms)


def shards(activations, upstream, hex_weight, time_weight, left_map, right_map):
    field = activations[:, 0]
    cotangent = upstream[:, 0]
    frames, tile_rows, channels, columns = field.shape
    chart, charts = lax.axis_index("diamond"), lax.axis_size("diamond")
    tile, tiles = lax.axis_index("tile"), lax.axis_size("tile")
    line, lines = lax.axis_index("tm"), lax.axis_size("tm")
    first_row = tile * tile_rows
    wide = tile_rows + 2
    strips = jnp.stack([field[..., columns - 1], field[..., 0]]).reshape(
        2, frames * tile_rows, channels
    )
    gathered, above, below, before, after = exchange_start(strips, field, cotangent)
    above = jnp.where(tile > 0, above, 0)
    below = jnp.where(tile < tiles - 1, below, 0)
    before = jnp.where(line > 0, before, 0)
    after = jnp.where(line < lines - 1, after, 0)

    def chart_rows(table, number):
        own = lax.dynamic_slice(table, (number, 0), (1, table.shape[1]))[0]
        return jnp.pad(own, (1, 1), constant_values=-1)

    every = jnp.arange(tiles * tile_rows)

    def ghost(strip, table):
        own = lax.dynamic_slice(chart_rows(table, chart), (first_row,), (wide,))
        pick = (own[:, None] == every[None, :]).astype(jnp.bfloat16)
        pick = pick.reshape(wide, tiles, tile_rows)
        strip = strip.reshape(tiles, frames, tile_rows, channels)
        return jnp.einsum("wtr,tfrc->fwc", pick, strip, preferred_element_type=jnp.float32).astype(
            jnp.bfloat16
        )

    ghost_left = ghost(gathered[0], left_map)
    ghost_right = ghost(gathered[1], right_map)
    rows = jnp.concatenate([above[:, None], field, below[:, None]], axis=1)
    padded = jnp.concatenate([ghost_left[..., None], rows, ghost_right[..., None]], axis=-1)
    framed = jnp.concatenate([before[None], cotangent, after[None]], axis=0)
    spread, terms = local_math(
        padded, framed, hex_weight, time_weight, frames, tile_rows, channels, columns
    )
    sent = spread.astype(jnp.bfloat16)
    strips = jnp.stack([sent[..., columns + 1], sent[..., 0]]).reshape(2, frames * wide, channels)
    count = terms.size // (tiles * 128)
    gathered, above, below, sums = exchange_end(
        strips, sent[:, 0, :, 1 : columns + 1], sent[:, wide - 1, :, 1 : columns + 1],
        terms.reshape(tiles, count, 128),
    )
    sums = sums.reshape(terms.shape)
    total = cotangent.astype(jnp.float32) + spread[:, 1 : tile_rows + 1, :, 1 : columns + 1]
    above = jnp.where(tile > 0, above, 0).astype(jnp.float32)
    below = jnp.where(tile < tiles - 1, below, 0).astype(jnp.float32)
    total = total + jnp.pad(above[:, None], ((0, 0), (0, tile_rows - 1), (0, 0), (0, 0)))
    total = total + jnp.pad(below[:, None], ((0, 0), (tile_rows - 1, 0), (0, 0), (0, 0)))
    own_rows = first_row + jnp.arange(tile_rows)
    source = (jnp.arange(tiles)[:, None] * tile_rows + jnp.arange(wide)[None, :]).reshape(-1)

    def landing(strip, table, number):
        target = jnp.take(chart_rows(table, number), source)
        pick = (own_rows[:, None] == target[None, :]).astype(jnp.bfloat16)
        pick = pick.reshape(tile_rows, tiles, wide)
        strip = strip.reshape(tiles, frames, wide, channels)
        return jnp.einsum("rtw,tfwc->frc", pick, strip, preferred_element_type=jnp.float32)

    into_first = landing(gathered[0], right_map, lax.rem(chart + charts - 1, charts))
    into_last = landing(gathered[1], left_map, lax.rem(chart + 1, charts))
    column = jnp.arange(columns)
    total = total + jnp.where(column == 0, into_first[..., None], 0.0)
    total = total + jnp.where(column == columns - 1, into_last[..., None], 0.0)
    return total.astype(jnp.bfloat16)[:, None], sums[:7], sums[7:]


def solution(mesh):
    whole = P("tm", "diamond", "tile", None, None)
    return jax.shard_map(
        shards,
        mesh=mesh,
        in_specs=(whole, whole, P(), P(), P(), P()),
        out_specs=(whole, P(), P()),
        check_vma=False,
    )
```

time: 318 us -> 73.2 us (0.23); the launches traced: 313 us -> 72.8 us
  blocking collectives: 114 us -> 0 us
  waiting for transfers between devices: 76.2 us -> 0 us
  Pallas kernels: 0 us -> 36.1 us
  local copies, waits for them, and re-layouts: 49.8 us -> 17.3 us
  starting transfers between devices: 20.6 us -> 0 us
  matrix products: 27.6 us -> 11.2 us
  between operations: 15.2 us -> 1.03 us
    psum x1 -> x0, waiting for transfers between devices: 73.2 us -> none  [shards(): lax.psum((hex_local, time_local), ('tm', 'diamond', 'tile'))]
    all_gather x2 -> x0, blocking collectives: 48 us -> none  [the longest x1 25 us: shards(): lax.all_gather(field[..., 0], 'tile', axis=1, tiled=True)]
    psum x1 -> x0, blocking collectives: 42.3 us -> none  [shards(): lax.psum((hex_local, time_local), ('tm', 'diamond', 'tile'))]
    pallas_call x0 -> x2, Pallas kernels: none -> 36.1 us  [the longest x1 22.3 us: exchange_end(): pl.pallas_call(last_exchange, out_shape=(jax.ShapeDtypeStruct((2, tiles)...]
    scatter-add x8 -> x0, local copies, waits for them, and re-layouts: 34.9 us -> none  [the longest x5 30.8 us: shards(): spread = spread.at[:, 1 + step_row:1 + step_row + tile_rows, :, 1 + step_...]
    unnamed x1 -> x0, blocking collectives: 23.9 us -> none
    ppermute x10 -> x0, starting transfers between devices: 20.5 us -> none  [the longest x2 7.02 us: with_halo(): before = lax.ppermute(last, axis, up)]
    dot_general x27 -> x31, matrix products: 27.6 us -> 11.2 us  [the longest x7 4.1 us: local_math(): jnp.einsum('frcx,cd->frdx', windows[number], hex_weight[number], preferre...]
  transfers between devices with their start and end apart: 11 -> 0, of which waited for: 4 -> 0; matrix products, arithmetic and copies ran while one was open for 9% -> 0% of each run, Pallas kernels for 0% -> 0%
where the time goes in v1:
time: 73.2 us; the launch traced here: 72.8 us
  Pallas kernels  36.1 us (49%)
  local copies, waits for them, and re-layouts  17.3 us (24%)
  matrix products  11.2 us (15%)
  other arithmetic  7.14 us (10%)
  between operations  1.03 us (1%)
    pallas_call x1, Pallas kernels, exchange_end(): pl.pallas_call(last_exchange, out_shape=(jax.ShapeDtypeStruct((2, tiles)...  22.3 us
    pallas_call x1, Pallas kernels, exchange_start(): pl.pallas_call(first_exchange, out_shape=(jax.ShapeDtypeStruct((2, tiles)...  13.8 us
    dot_general x7, matrix products, local_math(): jnp.einsum('frcx,cd->frdx', windows[number], hex_weight[number], preferre...  4.1 us
    unnamed x22, local copies, waits for them, and re-layouts  2.79 us
    dot_general x7, matrix products, local_math(): jnp.einsum('frcx,frdx->cd', window, grad_wide, preferred_element_type=jnp...  2.42 us
    slice x2, local copies, waits for them, and re-layouts, shards(): sent[..., columns + 1]  2.22 us
    convert_element_type x1, other arithmetic, shards(): sent = spread.astype(jnp.bfloat16)  2.09 us
    dot_general x7, matrix products, local_math(): jnp.einsum('frdx,cd->frcx', grad_wide, hex_weight[number], preferred_elem...  1.91 us

profile of v1, /device:TPU:1, one launch (start us, length us, event | category | flops | bytes accessed | tf_op | source)
XLA Modules:
  0.0 72.8 jit_solution(13330219208448939444)
XLA Ops:
  0.7 0.8 %fusion.97 = (s32[32]{0:T(128)S(1)}, s32[32]{0:T(128)S(1)}) fusion(s32[2,32]{1,0:T(2,128)} %param.13, s32[]{:T(128)S(6)} %select_n.72, s32[]{:T(128)S(6)} %select_n.68), kind=kLoop, calls=%fused_computation.170 | loop fusion | bytes 520 | tf_op jit(solution)/shard_map/squeeze | solution.py:274
  1.4 0.8 %fusion.98 = (s32[32]{0:T(128)S(1)}, s32[32]{0:T(128)S(1)}) fusion(s32[2,32]{1,0:T(2,128)} %param.12, s32[]{:T(128)S(6)} %select_n.72, s32[]{:T(128)S(6)} %select_n.68), kind=kLoop, calls=%fused_computation.171 | loop fusion | bytes 520 | tf_op jit(solution)/shard_map/squeeze | solution.py:274
  2.5 1.5 %slice_reduce_fusion.1 = (bf16[4,4,64]{2,1,0:T(4,128)(2,1)S(1)}, bf16[4,4,64]{2,1,0:T(4,128)(2,1)S(1)}) fusion(bf16[4,4,64,256]{3,2,1,0:T(8,128)(2,1)} %bitcast.367), kind=kLoop, calls=%fused_computation.95 | loop fusion | bytes 8192 | tf_op jit(solution)/shard_map/slice | solution.py:264
  4.0 0.6 pad_maximum_fusion.11.strips
  4.6 13.8 %first_exchange.1 = (bf16[2,8,16,64]{3,2,1,0:T(8,128)(2,1)}, bf16[4,64,256]{2,1,0:T(8,128)(2,1)}, bf16[4,64,256]{2,1,0:T(8,128)(2,1)}, bf16[4,64,256]{2,1,0:T(8,128)(2,1)}, bf16[4,64,256]{2,1,0:T(8,128)(2,1)}) custom-call(bf16[2,16,64]{2,1,0:T(8,128)(2,1)} %pad_maximum_fusion.11.strips, bf16[4,4,64,256]{3,2,1,0:T(8,128)(2,1)} %bitcast.368, ...), custom_call_target="tpu_custom_call" | custom-call | tf_op jit(solution)/shard_map/first_exchange/pallas_call | solution.py:175
  18.4 0.8 %fusion.110 = (bf16[1,8,16,64]{3,2,1,0:T(8,128)(2,1)S(1)}, bf16[1,8,16,64]{3,2,1,0:T(8,128)(2,1)S(1)}) fusion(bf16[2,8,16,64]{3,2,1,0:T(8,128)(2,1)} %get-tuple-element.17), kind=kLoop, calls=%fused_computation.189 | loop fusion | bytes 65536 | tf_op jit(solution)/shard_map/slice | solution.py:288
  19.7 1.0 %select_bitcast_fusion.2 = (bf16[4,1,64,256]{3,2,1,0:T(8,128)(2,1)S(1)}, bf16[4,1,64,256]{3,2,1,0:T(8,128)(2,1)S(1)}) fusion(bf16[4,64,256]{2,1,0:T(8,128)(2,1)} %get-tuple-element.16, pred[]{:T(512)S(6)} %lt.26, bf16[4,64,256]{2,1,0:T(8,128)(2,1)} %get-tuple-element.15, pred[]{:T(512)S(6)} %gt.8), kind=kLoop, calls=%fused_computation.107 | loop fusion | flops 131072 | bytes 524290 | tf_op jit(solution)/shard_map/broadcast_in_dim | solution.py:290
  20.7 0.4 convolution_bitcast_fusion.11
  21.7 0.5 convolution_bitcast_fusion.12
  22.2 0.5 convolution_bitcast_fusion.7
  23.7 1.8 %multiply_convert_fusion = (bf16[4,4,64,256]{3,2,1,0:T(8,128)(2,1)}, f32[4,4,64,256]{3,2,1,0:T(8,128)}) fusion(f32[4,4,64,256]{3,2,1,0:T(8,128)S(1)} %convolution_bitcast_fusion.7, f32[4,4,64,256]{3,2,1,0:T(8,128)S(1)} %convolution_bitcast_fusion.8, f32[4,4,64,256]{3,2,1,0:T(8,128)S(1)} %convolution_bitcast_fusion.9, ...), kind=kOutput, calls=%fused_computation.64 | convolution fusion | flops 36438016 | bytes 8404992 | tf_op jit(solution)/shard_map/frcx,cd->frdx/dot_general | solution.py:225
  25.6 0.6 copy-done.9
  26.8 0.5 fusion.9
  27.6 0.4 fusion.18
  29.4 0.4 fusion.15
  31.1 0.8 %reshape.98.terms = f32[8,40,128]{2,1,0:T(8,128)} reshape(f32[10,64,64]{2,1,0:T(8,128)S(1)} %copy.115) | data formatting | bytes 327680 | tf_op jit(solution)/shard_map/reshape | solution.py:301
  33.8 2.1 %fusion.107 = (bf16[4,6,64,258]{3,2,0,1:T(8,128)(2,1)S(1)}, f32[4,6,64,258]{3,2,0,1:T(8,128)S(1)}) fusion(f32[4,4,64,256]{3,2,0,1:T(8,128)S(1)} %convolution_bitcast_fusion, f32[4,4,64,256]{3,2,0,1:T(8,128)S(1)} %convolution_bitcast_fusion.1, f32[4,4,64,256]{3,2,0,1:T(8,128)S(1)} %convolution_bitcast_fusion.2, ...), kind=kLoop, calls=%fused_computation.186 | loop fusion | flops 2774016 | bytes 9717760 | tf_op jit(solution)/shard_map/convert_element_type | solution.py:296
  35.9 1.0 %copy-done.2 = bf16[4,6,64,258]{3,2,0,1:T(8,128)(2,1)} copy-done((bf16[4,6,64,258]{3,2,0,1:T(8,128)(2,1)}, bf16[4,6,64,258]{3,2,0,1:T(8,128)(2,1)S(1)}, u32[]{:S(2)}) %copy-start.2) | copy-done | bytes 792600
  36.9 1.0 %fusion.108 = (bf16[4,6,64,1]{3,2,0,1:T(8,128)(2,1)}, bf16[4,6,64,1]{3,2,0,1:T(8,128)(2,1)S(1)}) fusion(bf16[4,6,64,258]{3,2,0,1:T(8,128)(2,1)S(1)} %get-tuple-element.30), kind=kLoop, calls=%fused_computation.187 | loop fusion | bytes 12288 | tf_op jit(solution)/shard_map/slice | solution.py:297
  37.9 1.3 %copy.101 = bf16[4,6,64,1]{2,1,0,3:T(8,128)(2,1)S(1)} copy(bf16[4,6,64,1]{3,2,0,1:T(8,128)(2,1)} %get-tuple-element.34) | data formatting | bytes 6144 | tf_op jit(solution)/shard_map/slice | solution.py:297
  39.5 0.6 pad_maximum_fusion.10.strips
  40.1 1.9 %slice_bitcast_fusion = (bf16[4,64,256]{2,1,0:T(8,128)(2,1)}, bf16[4,64,256]{2,1,0:T(8,128)(2,1)}) fusion(bf16[4,6,64,258]{3,2,0,1:T(8,128)(2,1)} %copy-done.2), kind=kLoop, calls=%fused_computation.103 | loop fusion | bytes 524288 | tf_op jit(solution)/shard_map/squeeze | solution.py:300
  41.9 22.3 %last_exchange.1 = (bf16[2,8,24,64]{3,2,1,0:T(8,128)(2,1)}, bf16[4,64,256]{2,1,0:T(8,128)(2,1)}, bf16[4,64,256]{2,1,0:T(8,128)(2,1)}, f32[8,40,128]{2,1,0:T(8,128)}) custom-call(bf16[2,24,64]{2,1,0:T(8,128)(2,1)} %pad_maximum_fusion.10.strips, bf16[4,64,256]{2,1,0:T(8,128)(2,1)} %get-tuple-element.33.up_row, bf16[4,64,256]{2,1,0:T(8,128)(2,1)} %get-tuple-element.32.down_row, ...), custom_call_target="tpu_custom_call" | custom-call | tf_op jit(solution)/shard_map/last_exchange/pallas_call | solution.py:195
  64.2 0.8 %fusion.109 = (bf16[1,8,24,64]{3,2,1,0:T(8,128)(2,1)S(1)}, bf16[1,8,24,64]{3,2,1,0:T(8,128)(2,1)S(1)}) fusion(bf16[2,8,24,64]{3,2,1,0:T(8,128)(2,1)} %get-tuple-element.20), kind=kLoop, calls=%fused_computation.188 | loop fusion | bytes 98304 | tf_op jit(solution)/shard_map/slice | solution.py:319
  65.4 0.8 %gather_fusion = s32[48]{0:T(128)S(1)} fusion(s32[34]{0:T(128)S(1)} %pad.68, s32[1024]{0:T(1024)S(1)} %pad_clamp_fusion), kind=kCustom, calls=%fused_computation.clone | custom fusion | bytes 576 | tf_op jit(solution)/shard_map/jit(_take)/gather | solution.py:313
  66.2 0.8 %gather_fusion.1 = s32[48]{0:T(128)S(1)} fusion(s32[34]{0:T(128)S(1)} %pad.69, s32[1024]{0:T(1024)S(1)} %pad_clamp_fusion), kind=kCustom, calls=%fused_computation.1.clone | custom fusion | bytes 576 | tf_op jit(solution)/shard_map/jit(_take)/gather | solution.py:313
  67.9 0.9 %select_bitcast_fusion = bf16[4,1,64,256]{3,2,0,1:T(8,128)(2,1)S(1)} fusion(bf16[4,64,256]{2,1,0:T(8,128)(2,1)} %get-tuple-element.19, pred[]{:T(512)S(6)} %lt.26), kind=kLoop, calls=%fused_computation.105 | loop fusion | flops 65536 | bytes 262145 | tf_op jit(solution)/shard_map/broadcast_in_dim | solution.py:308
  68.8 0.9 %select_bitcast_fusion.1 = bf16[4,1,64,256]{3,2,0,1:T(8,128)(2,1)S(1)} fusion(bf16[4,64,256]{2,1,0:T(8,128)(2,1)} %get-tuple-element.18, pred[]{:T(512)S(6)} %gt.8), kind=kLoop, calls=%fused_computation.106 | loop fusion | flops 65536 | bytes 262145 | tf_op jit(solution)/shard_map/broadcast_in_dim | solution.py:307
  69.8 0.7 fusion.35
  70.4 0.8 %copy.122 = bf16[4,1,4,64,256]{4,3,2,1,0:T(8,128)(2,1)} copy(bf16[4,1,4,64,256]{4,3,0,2,1:T(8,128)(2,1)S(1)} %fusion.35) | data formatting | bytes 1048576
  71.4 0.7 slice.150
  72.1 0.6 slice.151
  (75 shorter events, 9.5 us)
Async XLA Ops:
  0.6 20.0 %copy-start = (bf16[4,1,4,64,256]{4,3,2,1,0:T(8,128)(2,1)S(1)}, bf16[4,1,4,64,256]{4,3,2,1,0:T(8,128)(2,1)}, u32[]{:S(2)}) copy-start(bf16[4,1,4,64,256]{4,3,2,1,0:T(8,128)(2,1)} %param.8) | copy-start | bytes 1572868
  0.6 20.0 %copy-start.5 = (bf16[7,64,64]{2,1,0:T(8,128)(2,1)S(1)}, bf16[7,64,64]{2,1,0:T(8,128)(2,1)}, u32[]{:S(2)}) copy-start(bf16[7,64,64]{2,1,0:T(8,128)(2,1)} %param.10) | copy-start | bytes 172036
  23.7 1.8 %copy-start.7 = (bf16[4,64,256]{2,1,0:T(8,128)(2,1)S(1)}, bf16[4,64,256]{2,1,0:T(8,128)(2,1)}, u32[]{:S(2)}) copy-start(bf16[4,64,256]{2,1,0:T(8,128)(2,1)} %get-tuple-element.14) | copy-start | bytes 393220
  23.7 1.8 %copy-start.8 = (bf16[4,64,256]{2,1,0:T(8,128)(2,1)S(1)}, bf16[4,64,256]{2,1,0:T(8,128)(2,1)}, u32[]{:S(2)}) copy-start(bf16[4,64,256]{2,1,0:T(8,128)(2,1)} %get-tuple-element.13) | copy-start | bytes 393220
  23.7 1.8 %copy-start.1 = (bf16[4,1,4,64,256]{4,3,2,1,0:T(8,128)(2,1)S(1)}, bf16[4,1,4,64,256]{4,3,2,1,0:T(8,128)(2,1)}, u32[]{:S(2)}) copy-start(bf16[4,1,4,64,256]{4,3,2,1,0:T(8,128)(2,1)} %param.9) | copy-start | bytes 1572868
  25.5 0.8 %copy-start.9 = (bf16[3,64,64]{2,1,0:T(8,128)(2,1)S(1)}, bf16[3,64,64]{2,1,0:T(8,128)(2,1)}, u32[]{:S(2)}) copy-start(bf16[3,64,64]{2,1,0:T(8,128)(2,1)} %param.11) | copy-start | bytes 73732
  25.5 1.3 %copy-start.4 = (f32[4,4,64,256]{3,2,1,0:T(8,128)S(1)}, f32[4,4,64,256]{3,2,1,0:T(8,128)}, u32[]{:S(2)}) copy-start(f32[4,4,64,256]{3,2,1,0:T(8,128)} %get-tuple-element.51) | copy-start | bytes 3145732
  29.0 1.0 %copy-start.3 = (bf16[4,4,64,256]{3,2,1,0:T(8,128)(2,1)S(1)}, bf16[4,4,64,256]{3,2,1,0:T(8,128)(2,1)}, u32[]{:S(2)}) copy-start(bf16[4,4,64,256]{3,2,1,0:T(8,128)(2,1)} %get-tuple-element.50) | copy-start | bytes 1572868
  35.9 1.0 %copy-start.2 = (bf16[4,6,64,258]{3,2,0,1:T(8,128)(2,1)}, bf16[4,6,64,258]{3,2,0,1:T(8,128)(2,1)S(1)}, u32[]{:S(2)}) copy-start(bf16[4,6,64,258]{3,2,0,1:T(8,128)(2,1)S(1)} %get-tuple-element.30) | copy-start | bytes 2377732
  66.2 5.1 %copy-start.6 = (f32[8,40,128]{2,1,0:T(8,128)S(1)}, f32[8,40,128]{2,1,0:T(8,128)}, u32[]{:S(2)}) copy-start(f32[8,40,128]{2,1,0:T(8,128)} %get-tuple-element.21) | copy-start | bytes 491524

commit v2 on v1

--- a/solution.py
+++ b/solution.py
@@ -43,36 +43,33 @@
     me, tiles = lax.axis_index("tile"), lax.axis_size("tile")
     chart, charts = lax.axis_index("diamond"), lax.axis_size("diamond")
     sides = (lax.rem(chart + 1, charts), lax.rem(chart + charts - 1, charts))
-    copies = []
-    for step in range(tiles):
-        other = lax.rem(me + step, tiles)
-        for side in range(2):
-            copies.append(
-                remote(
-                    strips.at[side],
-                    gathered.at[side, me],
-                    send.at[side, step],
-                    recv.at[side, me],
-                    {"diamond": sides[side], "tile": other},
-                )
-            )
+    parts = (slice(0, 2),) if charts == 2 else (slice(0, 1), slice(1, 2))
+
+    def copy(part, step, source, target):
+        return remote(
+            strips.at[parts[part]],
+            gathered.at[source, parts[part]],
+            send.at[part, step],
+            recv.at[part, source],
+            {"diamond": sides[part], "tile": target},
+        )
+
+    copies = [
+        copy(part, step, me, lax.rem(me + step, tiles))
+        for step in range(tiles)
+        for part in range(len(parts))
+    ]
 
     def start():
-        for copy in copies:
-            copy.start()
+        for one in copies:
+            one.start()
 
     def wait():
-        for copy in copies:
-            copy.wait_send()
-        for side in range(2):
+        for one in copies:
+            one.wait_send()
+        for part in range(len(parts)):
             for number in range(tiles):
-                remote(
-                    strips.at[side],
-                    gathered.at[side, number],
-                    send.at[side, 0],
-                    recv.at[side, number],
-                    {"diamond": sides[side], "tile": me},
-                ).wait_recv()
+                copy(part, 0, number, me).wait_recv()
 
     return start, wait
 
@@ -175,7 +172,7 @@
     return pl.pallas_call(
         first_exchange,
         out_shape=(
-            jax.ShapeDtypeStruct((2, tiles) + strips.shape[1:], kind), line, line, frame, frame,
+            jax.ShapeDtypeStruct((tiles,) + strips.shape, kind), line, line, frame, frame,
         ),
         in_specs=[ANY] * 3,
         out_specs=(ANY,) * 5,
@@ -195,7 +192,7 @@
     return pl.pallas_call(
         last_exchange,
         out_shape=(
-            jax.ShapeDtypeStruct((2, tiles) + strips.shape[1:], strips.dtype), line, line,
+            jax.ShapeDtypeStruct((tiles,) + strips.shape, strips.dtype), line, line,
             jax.ShapeDtypeStruct(terms.shape, terms.dtype),
         ),
         in_specs=[ANY, ANY, ANY, VMEM],
@@ -247,9 +244,34 @@
         term = jnp.einsum(
             "frdx,cd->frcx", grad_wide, hex_weight[number], preferred_element_type=jnp.float32
         )
-        term = jnp.pad(term, ((0, 0), (1 + a, 1 - a), (0, 0), (1 + b, 1 - b)))
+        if b == 1:
+            term = jnp.pad(term[..., :-1], ((0, 0), (0, 0), (0, 0), (1, 0)))
+        if b == -1:
+            term = jnp.pad(term[..., 1:], ((0, 0), (0, 0), (0, 0), (0, 1)))
+        term = jnp.pad(term, ((0, 0), (1 + a, 1 - a), (0, 0), (0, 0)))
         spread = term if spread is None else spread + term
-    return spread, jnp.stack(hex_terms + time_terms)
+    seams = seam_columns(grad_wide)
+    sides = []
+    for side, b in ((0, 1), (1, -1)):
+        seam = None
+        for number, (a, _) in enumerate(OFFSETS):
+            if OFFSETS[number][1] == b:
+                term = jnp.einsum(
+                    "frd,cd->frc", seams[side], hex_weight[number],
+                    preferred_element_type=jnp.float32,
+                )
+                term = jnp.pad(term, ((0, 0), (1 + a, 1 - a), (0, 0)))
+                seam = term if seam is None else seam + term
+        sides.append(seam)
+    return spread, jnp.stack(sides).astype(jnp.bfloat16), jnp.stack(hex_terms + time_terms)
+
+
+def seam_columns(block):
+    columns = block.shape[-1]
+    pick = jnp.array([columns - 1, 0])[:, None] == jnp.arange(columns)[None, :]
+    return jnp.einsum(
+        "sx,frcx->sfrc", pick.astype(block.dtype), block, preferred_element_type=jnp.float32
+    ).astype(block.dtype)
 
 
 def shards(activations, upstream, hex_weight, time_weight, left_map, right_map):
@@ -261,9 +283,7 @@
     line, lines = lax.axis_index("tm"), lax.axis_size("tm")
     first_row = tile * tile_rows
     wide = tile_rows + 2
-    strips = jnp.stack([field[..., columns - 1], field[..., 0]]).reshape(
-        2, frames * tile_rows, channels
-    )
+    strips = seam_columns(field).reshape(2, frames * tile_rows, channels)
     gathered, above, below, before, after = exchange_start(strips, field, cotangent)
     above = jnp.where(tile > 0, above, 0)
     below = jnp.where(tile < tiles - 1, below, 0)
@@ -285,39 +305,40 @@
             jnp.bfloat16
         )
 
-    ghost_left = ghost(gathered[0], left_map)
-    ghost_right = ghost(gathered[1], right_map)
+    ghost_left = ghost(gathered[:, 0], left_map)
+    ghost_right = ghost(gathered[:, 1], right_map)
     rows = jnp.concatenate([above[:, None], field, below[:, None]], axis=1)
     padded = jnp.concatenate([ghost_left[..., None], rows, ghost_right[..., None]], axis=-1)
     framed = jnp.concatenate([before[None], cotangent, after[None]], axis=0)
-    spread, terms = local_math(
+    spread, seams, terms = local_math(
         padded, framed, hex_weight, time_weight, frames, tile_rows, channels, columns
     )
-    sent = spread.astype(jnp.bfloat16)
-    strips = jnp.stack([sent[..., columns + 1], sent[..., 0]]).reshape(2, frames * wide, channels)
+    strips = seams.reshape(2, frames * wide, channels)
     count = terms.size // (tiles * 128)
     gathered, above, below, sums = exchange_end(
-        strips, sent[:, 0, :, 1 : columns + 1], sent[:, wide - 1, :, 1 : columns + 1],
+        strips, spread[:, 0].astype(jnp.bfloat16), spread[:, wide - 1].astype(jnp.bfloat16),
         terms.reshape(tiles, count, 128),
     )
     sums = sums.reshape(terms.shape)
-    total = cotangent.astype(jnp.float32) + spread[:, 1 : tile_rows + 1, :, 1 : columns + 1]
+    total = cotangent.astype(jnp.float32) + spread[:, 1 : tile_rows + 1]
     above = jnp.where(tile > 0, above, 0).astype(jnp.float32)
     below = jnp.where(tile < tiles - 1, below, 0).astype(jnp.float32)
     total = total + jnp.pad(above[:, None], ((0, 0), (0, tile_rows - 1), (0, 0), (0, 0)))
     total = total + jnp.pad(below[:, None], ((0, 0), (tile_rows - 1, 0), (0, 0), (0, 0)))
     own_rows = first_row + jnp.arange(tile_rows)
-    source = (jnp.arange(tiles)[:, None] * tile_rows + jnp.arange(wide)[None, :]).reshape(-1)
 
     def landing(strip, table, number):
-        target = jnp.take(chart_rows(table, number), source)
-        pick = (own_rows[:, None] == target[None, :]).astype(jnp.bfloat16)
-        pick = pick.reshape(tile_rows, tiles, wide)
+        target = chart_rows(table, number)
+        inner = target[1:-1].reshape(tiles, tile_rows)
+        prior = target[:-2].reshape(tiles, tile_rows)[:, :1]
+        later = target[2:].reshape(tiles, tile_rows)[:, -1:]
+        target = jnp.concatenate([prior, inner, later], axis=1)
+        pick = (own_rows[:, None, None] == target[None]).astype(jnp.bfloat16)
         strip = strip.reshape(tiles, frames, wide, channels)
         return jnp.einsum("rtw,tfwc->frc", pick, strip, preferred_element_type=jnp.float32)
 
-    into_first = landing(gathered[0], right_map, lax.rem(chart + charts - 1, charts))
-    into_last = landing(gathered[1], left_map, lax.rem(chart + 1, charts))
+    into_first = landing(gathered[:, 0], right_map, lax.rem(chart + charts - 1, charts))
+    into_last = landing(gathered[:, 1], left_map, lax.rem(chart + 1, charts))
     column = jnp.arange(columns)
     total = total + jnp.where(column == 0, into_first[..., None], 0.0)
     total = total + jnp.where(column == columns - 1, into_last[..., None], 0.0)

time: 73.2 us -> 75.2 us (1.027)
  matrix products: 11.2 us -> 19.4 us
  local copies, waits for them, and re-layouts: 17.3 us -> 12.5 us
  other arithmetic: 7.14 us -> 5.82 us
    dot_general x7, matrix products: 2.42 us -> 6.69 us  [local_math(): jnp.einsum('frcx,frdx->cd', window, grad_wide, preferred_element_type=jnp...]
    squeeze x3 -> x0, local copies, waits for them, and re-layouts: 3.38 us -> none  [the longest x1 1.86 us: shards(): sent[:, wide - 1, :, 1:columns + 1]]
    slice x8 -> x11, local copies, waits for them, and re-layouts: 5.65 us -> 2.65 us  [the longest x2 0.85 us: shards(): gathered[:, 0]]
    dot_general x0 -> x6, matrix products: none -> 2.22 us  [the longest x2 1.7 us: seam_columns(): jnp.einsum('sx,frcx->sfrc', pick.astype(block.dtype), block, preferred_el...]
    convert_element_type x1 -> x0, other arithmetic: 2.09 us -> none  [shards(): sent = spread.astype(jnp.bfloat16)]
    dot_general x3, matrix products: 0.86 us -> 2.68 us  [local_math(): jnp.einsum('frcx,frdx->cd', active, shifted, preferred_element_type=jnp.f...]
    gather x2 -> x0, local copies, waits for them, and re-layouts: 1.56 us -> none  [landing(): target = jnp.take(chart_rows(table, number), source)]
    convert_element_type x0 -> x2, local copies, waits for them, and re-layouts: none -> 1.34 us  [the longest x1 0.71 us: shards(): spread[:, wide - 1].astype(jnp.bfloat16)]
where the time goes in v2:
time: 75.2 us; the launch traced here: 74.7 us
  Pallas kernels  36.1 us (48%)
  matrix products  19.4 us (26%)
  local copies, waits for them, and re-layouts  12.5 us (17%)
  other arithmetic  5.82 us (8%)
  between operations  0.94 us (1%)
    pallas_call x1, Pallas kernels, exchange_end(): pl.pallas_call(last_exchange, out_shape=(jax.ShapeDtypeStruct((tiles,) +...  22.3 us
    pallas_call x1, Pallas kernels, exchange_start(): pl.pallas_call(first_exchange, out_shape=(jax.ShapeDtypeStruct((tiles,) +...  13.8 us
    dot_general x7, matrix products, local_math(): jnp.einsum('frcx,frdx->cd', window, grad_wide, preferred_element_type=jnp...  6.69 us
    dot_general x7, matrix products, local_math(): jnp.einsum('frcx,cd->frdx', windows[number], hex_weight[number], preferre...  3.84 us
    unnamed x24, local copies, waits for them, and re-layouts  2.71 us
    dot_general x3, matrix products, local_math(): jnp.einsum('frcx,frdx->cd', active, shifted, preferred_element_type=jnp.f...  2.68 us
    dot_general x7, matrix products, local_math(): jnp.einsum('frdx,cd->frcx', grad_wide, hex_weight[number], preferred_elem...  1.92 us
    dot_general x2, matrix products, seam_columns(): jnp.einsum('sx,frcx->sfrc', pick.astype(block.dtype), block, preferred_el...  1.7 us

profile of v2, /device:TPU:1, one launch (start us, length us, event | category | flops | bytes accessed | tf_op | source)
XLA Modules:
  0.0 74.7 jit_solution(13500860930041971183)
XLA Ops:
  0.7 0.8 %fusion.123 = (s32[32]{0:T(128)S(1)}, s32[32]{0:T(128)S(1)}, s32[32]{0:T(128)S(1)}, s32[32]{0:T(128)S(1)}, s32[32]{0:T(128)S(1)}, /*index=5*/s32[32]{0:T(128)S(1)}) fusion(s32[2,32]{1,0:T(2,128)} %param.13, s32[]{:T(128)S(6)} %select_n.65, s32[]{:T(128)S(6)} %select_n.61, s32[2,32]{1,0:T(2,128)} %param.12), kind=kLoop, calls=%fused_computation.204 | loop fusion | bytes 1288 | tf_op jit(solution)/shard_map/dynamic_slice | solution.py:294
  3.1 1.4 %convolution_convert_fusion.1 = bf16[2,4,4,64]{3,0,2,1:T(2,128)(2,1)S(1)} fusion(s32[2]{0:T(128)} %constant.50.clone, bf16[4,1,4,64,256]{4,3,2,1,0:T(8,128)(2,1)} %param.8), kind=kOutput, calls=%fused_computation.58 | convolution fusion | flops 1051136 | bytes 528392 | tf_op jit(solution)/shard_map/sx,frcx->sfrc/dot_general | solution.py:272
  4.4 0.6 copy.71
  5.1 1.1 %copy.263 = bf16[4,1,4,64,256]{4,3,0,2,1:T(8,128)(2,1)S(1)} copy(bf16[4,1,4,64,256]{4,3,2,1,0:T(8,128)(2,1)} %param.9) | data formatting | bytes 1048576 | tf_op args[1]
  6.2 13.8 %first_exchange.1 = (bf16[8,2,16,64]{3,2,1,0:T(8,128)(2,1)}, bf16[4,64,256]{2,1,0:T(8,128)(2,1)}, bf16[4,64,256]{2,1,0:T(8,128)(2,1)}, bf16[4,64,256]{2,1,0:T(8,128)(2,1)}, bf16[4,64,256]{2,1,0:T(8,128)(2,1)}) custom-call(bf16[2,16,64]{2,1,0:T(8,128)(2,1)} %bitcast.425, bf16[4,4,64,256]{3,2,1,0:T(8,128)(2,1)} %bitcast.406, bf16[4,4,64,256]{3,2,1,0:T(8,128)(2,1)} %bitcast.419), custom_call_target="tpu_custom_call" | custom-call | tf_op jit(solution)/shard_map/first_exchange/pallas_call | solution.py:172
  20.0 1.0 %select_bitcast_fusion.4 = (bf16[1,4,64,256]{3,2,0,1:T(8,128)(2,1)S(1)}, bf16[1,4,64,256]{3,2,0,1:T(8,128)(2,1)S(1)}) fusion(bf16[4,64,256]{2,1,0:T(8,128)(2,1)} %get-tuple-element.13, pred[]{:T(512)S(6)} %gt.7, bf16[4,64,256]{2,1,0:T(8,128)(2,1)} %get-tuple-element.12, pred[]{:T(512)S(6)} %lt.19), kind=kLoop, calls=%fused_computation.112 | loop fusion | flops 131072 | bytes 524290 | tf_op jit(solution)/shard_map/broadcast_in_dim | solution.py:312
  21.0 0.8 %fusion.138 = (bf16[8,1,16,64]{3,2,1,0:T(8,128)(2,1)S(1)}, bf16[8,1,16,64]{3,2,1,0:T(8,128)(2,1)S(1)}) fusion(bf16[8,2,16,64]{3,2,1,0:T(8,128)(2,1)} %get-tuple-element.16), kind=kLoop, calls=%fused_computation.219 | loop fusion | bytes 65536 | tf_op jit(solution)/shard_map/slice | solution.py:308
  22.2 0.9 %pad_maximum_fusion.9 = (bf16[4,4,64,256]{3,2,0,1:T(8,128)(2,1)}, bf16[4,4,64,256]{3,2,0,1:T(8,128)(2,1)S(1)}) fusion(bf16[1,4,64,256]{3,2,0,1:T(8,128)(2,1)S(1)} %get-tuple-element.56, bf16[4,4,64,256]{3,2,0,1:T(8,128)(2,1)S(1)} %bitcast.422, bf16[1,4,64,256]{3,2,0,1:T(8,128)(2,1)S(1)} %get-tuple-element.55), kind=kLoop, calls=%fused_computation.93 | loop fusion | flops 524288 | bytes 1835008 | tf_op jit(solution)/shard_map/concatenate | solution.py:312
  26.1 1.5 %multiply_convert_fusion = (bf16[4,4,64,256]{3,2,1,0:T(8,128)(2,1)}, f32[4,4,64,256]{3,2,1,0:T(8,128)S(1)}) fusion(f32[4,4,64,256]{3,2,1,0:T(8,128)S(1)} %convolution_bitcast_fusion.7, f32[4,4,64,256]{3,2,1,0:T(8,128)S(1)} %convolution_bitcast_fusion.8, f32[4,4,64,256]{3,2,1,0:T(8,128)S(1)} %convolution_bitcast_fusion.9, ...), kind=kOutput, calls=%fused_computation.69 | convolution fusion | flops 36438016 | bytes 8404992 | tf_op jit(solution)/shard_map/frcx,cd->frdx/dot_general | solution.py:222
  28.6 0.5 fusion.11
  30.2 0.6 pad_maximum_fusion.10.strips
  30.9 0.9 %fusion.21 = f32[10,64,64]{1,2,0:T(8,128)} fusion(bf16[4,4,64,256]{3,2,1,0:T(8,128)(2,1)S(1)} %fusion.11, bf16[4,1,4,64,256]{4,3,2,1,0:T(8,128)(2,1)S(1)} %copy-done), kind=kOutput, calls=%fused_computation.52 | convolution fusion | flops 33554432 | bytes 1081344 | tf_op jit(solution)/shard_map/frcx,frdx->cd/dot_general | solution.py:239
  31.7 1.0 %fusion.20 = f32[10,64,64]{1,2,0:T(8,128)} fusion(f32[10,64,64]{1,2,0:T(8,128)} %fusion.21, bf16[4,4,64,256]{3,2,1,0:T(8,128)(2,1)S(1)} %fusion.11, bf16[4,6,64,1]{3,2,1,0:T(8,128)(2,1)S(1)} %copy.83, bf16[4,1,64,256]{3,2,1,0:T(8,128)(2,1)S(1)} %get-tuple-element.53, bf16[4,4,64,256]{3,2,1,0:T(8,128)(2,1)S(1)} %bitcast.413, ...), kind=kOutput, calls=%fused_computation.50 | convolution fusion | flops 35651584 | bytes 1346560 | tf_op jit(solution)/shard_map/frcx,frdx->cd/dot_general | solution.py:239
  32.8 1.0 %fusion.19 = f32[10,64,64]{1,2,0:T(8,128)} fusion(f32[10,64,64]{1,2,0:T(8,128)} %fusion.20, bf16[4,4,64,256]{3,2,1,0:T(8,128)(2,1)S(1)} %fusion.11, bf16[4,6,64,1]{3,2,1,0:T(8,128)(2,1)S(1)} %copy.87, bf16[4,1,64,256]{3,2,1,0:T(8,128)(2,1)S(1)} %get-tuple-element.53, bf16[4,4,64,256]{3,2,1,0:T(8,128)(2,1)S(1)} %bitcast.414, ...), kind=kOutput, calls=%fused_computation.48 | convolution fusion | flops 35651584 | bytes 1346560 | tf_op jit(solution)/shard_map/frcx,frdx->cd/dot_general | solution.py:239
  33.8 0.9 %fusion.13 = f32[10,64,64]{1,2,0:T(8,128)} fusion(f32[10,64,64]{1,2,0:T(8,128)} %fusion.19, bf16[4,4,64,256]{3,2,1,0:T(8,128)(2,1)S(1)} %fusion.11, bf16[4,1,64,256]{3,2,1,0:T(8,128)(2,1)S(1)} %get-tuple-element.53, bf16[4,4,64,256]{3,2,1,0:T(8,128)(2,1)S(1)} %bitcast.415), kind=kOutput, calls=%fused_computation.36 | convolution fusion | flops 34865152 | bytes 1212416 | tf_op jit(solution)/shard_map/frcx,frdx->cd/dot_general | solution.py:239
  34.7 0.9 %fusion.12 = f32[10,64,64]{1,2,0:T(8,128)} fusion(f32[10,64,64]{1,2,0:T(8,128)} %fusion.13, bf16[4,4,64,256]{3,2,1,0:T(8,128)(2,1)S(1)} %fusion.11, bf16[4,4,64,256]{3,2,1,0:T(8,128)(2,1)S(1)} %bitcast.416, bf16[4,1,64,256]{3,2,1,0:T(8,128)(2,1)S(1)} %get-tuple-element.54), kind=kOutput, calls=%fused_computation.34 | convolution fusion | flops 34865152 | bytes 1212416 | tf_op jit(solution)/shard_map/frcx,frdx->cd/dot_general | solution.py:239
  35.5 1.0 %fusion.18 = f32[10,64,64]{1,2,0:T(8,128)} fusion(f32[10,64,64]{1,2,0:T(8,128)} %fusion.12, bf16[4,4,64,256]{3,2,1,0:T(8,128)(2,1)S(1)} %fusion.11, bf16[4,6,64,1]{3,2,1,0:T(8,128)(2,1)S(1)} %copy.87, bf16[4,1,64,256]{3,2,1,0:T(8,128)(2,1)S(1)} %get-tuple-element.53, bf16[4,4,64,256]{3,2,1,0:T(8,128)(2,1)S(1)} %bitcast.417, ...), kind=kOutput, calls=%fused_computation.46 | convolution fusion | flops 35651584 | bytes 1346560 | tf_op jit(solution)/shard_map/frcx,frdx->cd/dot_general | solution.py:239
  36.5 1.0 %fusion.17 = f32[10,64,64]{1,2,0:T(8,128)} fusion(f32[10,64,64]{1,2,0:T(8,128)} %fusion.18, bf16[4,4,64,256]{3,2,1,0:T(8,128)(2,1)S(1)} %fusion.11, bf16[4,6,64,1]{3,2,1,0:T(8,128)(2,1)S(1)} %copy.83, bf16[4,1,64,256]{3,2,1,0:T(8,128)(2,1)S(1)} %get-tuple-element.53, bf16[4,4,64,256]{3,2,1,0:T(8,128)(2,1)S(1)} %bitcast.418, ...), kind=kOutput, calls=%fused_computation.44 | convolution fusion | flops 35651584 | bytes 1346560 | tf_op jit(solution)/shard_map/frcx,frdx->cd/dot_general | solution.py:239
  37.7 0.9 %fusion.16 = f32[10,64,64]{1,2,0:T(8,128)} fusion(f32[10,64,64]{1,2,0:T(8,128)} %fusion.17, bf16[4,4,64,256]{3,2,1,0:T(8,128)(2,1)S(1)} %copy-done.4, bf16[4,4,64,256]{3,2,0,1:T(8,128)(2,1)S(1)} %copy-done.3), kind=kOutput, calls=%fused_computation.42 | convolution fusion | flops 33554432 | bytes 1081344 | tf_op jit(solution)/shard_map/frcx,frdx->cd/dot_general | solution.py:235
  38.6 0.9 %fusion.15 = f32[10,64,64]{1,2,0:T(8,128)} fusion(f32[10,64,64]{1,2,0:T(8,128)} %fusion.16, bf16[4,4,64,256]{3,2,1,0:T(8,128)(2,1)S(1)} %copy-done.4, bf16[4,1,4,64,256]{4,3,2,1,0:T(8,128)(2,1)S(1)} %copy-done.1), kind=kOutput, calls=%fused_computation.40 | convolution fusion | flops 33554432 | bytes 1081344 | tf_op jit(solution)/shard_map/frcx,frdx->cd/dot_general | solution.py:235
  39.5 0.9 %fusion.14 = f32[10,64,64]{1,2,0:T(8,128)} fusion(f32[10,64,64]{1,2,0:T(8,128)} %fusion.15, bf16[4,4,64,256]{3,2,1,0:T(8,128)(2,1)S(1)} %copy-done.4, bf16[4,4,64,256]{3,2,0,1:T(8,128)(2,1)S(1)} %get-tuple-element.32), kind=kOutput, calls=%fused_computation.38 | convolution fusion | flops 33554432 | bytes 1081344 | tf_op jit(solution)/shard_map/frcx,frdx->cd/dot_general | solution.py:235
  40.4 1.1 %copy.125 = f32[10,64,64]{2,1,0:T(8,128)S(1)} copy(f32[10,64,64]{1,2,0:T(8,128)} %fusion.14) | data formatting | bytes 327680 | tf_op jit(solution)/shard_map/stack | solution.py:266
  41.5 0.8 %reshape.81.terms = f32[8,40,128]{2,1,0:T(8,128)} reshape(f32[10,64,64]{2,1,0:T(8,128)S(1)} %copy.125) | data formatting | bytes 327680 | tf_op jit(solution)/shard_map/reshape | solution.py:320
  44.9 0.8 %fusion.136 = (bf16[4,6,64,256]{3,2,0,1:T(8,128)(2,1)S(1)}, f32[4,6,64,256]{3,2,0,1:T(8,128)S(1)}) fusion(f32[4,4,64,255]{3,2,0,1:T(8,128)S(1)} %bitcast.421, f32[4,4,64,255]{3,2,0,1:T(8,128)S(1)} %slice.191, f32[4,4,64,256]{3,2,0,1:T(8,128)S(1)} %convolution_bitcast_fusion.2, f32[4,4,64,256]{3,2,0,1:T(8,128)S(1)} %convolution_bitcast_fusion.3, ...), kind=kLoop, calls=%fused_computation.217 | loop fusion | flops 2752512 | bytes 9682944 | tf_op jit(solution)/shard_map/convert.7
  45.7 0.7 slice_bitcast_fusion
  46.4 22.3 %last_exchange.1 = (bf16[8,2,24,64]{3,2,1,0:T(8,128)(2,1)}, bf16[4,64,256]{2,1,0:T(8,128)(2,1)}, bf16[4,64,256]{2,1,0:T(8,128)(2,1)}, f32[8,40,128]{2,1,0:T(8,128)}) custom-call(bf16[2,24,64]{2,1,0:T(8,128)(2,1)} %pad_maximum_fusion.10.strips, bf16[4,64,256]{2,1,0:T(8,128)(2,1)} %get-tuple-element.30.up_row, bf16[4,64,256]{2,1,0:T(8,128)(2,1)} %get-tuple-element.29.down_row, ...), custom_call_target="tpu_custom_call" | custom-call | tf_op jit(solution)/shard_map/last_exchange/pallas_call | solution.py:192
  68.7 0.9 %select_bitcast_fusion.1 = bf16[4,1,64,256]{3,2,0,1:T(8,128)(2,1)S(1)} fusion(bf16[4,64,256]{2,1,0:T(8,128)(2,1)} %get-tuple-element.17, pred[]{:T(512)S(6)} %gt.8), kind=kLoop, calls=%fused_computation.109 | loop fusion | flops 65536 | bytes 262145 | tf_op jit(solution)/shard_map/broadcast_in_dim | solution.py:326
  69.6 0.8 %fusion.137 = (bf16[8,1,24,64]{3,2,1,0:T(8,128)(2,1)S(1)}, bf16[8,1,24,64]{3,2,1,0:T(8,128)(2,1)S(1)}) fusion(bf16[8,2,24,64]{3,2,1,0:T(8,128)(2,1)} %get-tuple-element.19), kind=kLoop, calls=%fused_computation.218 | loop fusion | bytes 98304 | tf_op jit(solution)/shard_map/slice | solution.py:340
  71.0 0.9 %select_bitcast_fusion = bf16[4,1,64,256]{3,2,0,1:T(8,128)(2,1)S(1)} fusion(bf16[4,64,256]{2,1,0:T(8,128)(2,1)} %get-tuple-element.18, pred[]{:T(512)S(6)} %lt.20), kind=kLoop, calls=%fused_computation.108 | loop fusion | flops 65536 | bytes 262145 | tf_op jit(solution)/shard_map/broadcast_in_dim | solution.py:327
  72.3 0.8 %copy.132 = bf16[4,1,4,64,256]{4,3,2,1,0:T(8,128)(2,1)} copy(bf16[4,1,4,64,256]{4,3,0,2,1:T(8,128)(2,1)S(1)} %fusion.37) | data formatting | bytes 1048576
  73.3 0.6 slice.199
  74.0 0.7 slice.198
  (84 shorter events, 10.8 us)
Async XLA Ops:
  20.0 3.1 %copy-start.7 = (bf16[4,64,256]{2,1,0:T(8,128)(2,1)S(1)}, bf16[4,64,256]{2,1,0:T(8,128)(2,1)}, u32[]{:S(2)}) copy-start(bf16[4,64,256]{2,1,0:T(8,128)(2,1)} %get-tuple-element.14) | copy-start | bytes 393220
  20.0 3.1 %copy-start.8 = (bf16[4,64,256]{2,1,0:T(8,128)(2,1)S(1)}, bf16[4,64,256]{2,1,0:T(8,128)(2,1)}, u32[]{:S(2)}) copy-start(bf16[4,64,256]{2,1,0:T(8,128)(2,1)} %get-tuple-element.15) | copy-start | bytes 393220
  22.2 1.5 %copy-start = (bf16[4,1,4,64,256]{4,3,2,1,0:T(8,128)(2,1)S(1)}, bf16[4,1,4,64,256]{4,3,2,1,0:T(8,128)(2,1)}, u32[]{:S(2)}) copy-start(bf16[4,1,4,64,256]{4,3,2,1,0:T(8,128)(2,1)} %param.8) | copy-start | bytes 1572868
  22.2 1.5 %copy-start.5 = (bf16[7,64,64]{2,1,0:T(8,128)(2,1)S(1)}, bf16[7,64,64]{2,1,0:T(8,128)(2,1)}, u32[]{:S(2)}) copy-start(bf16[7,64,64]{2,1,0:T(8,128)(2,1)} %param.10) | copy-start | bytes 172036
  26.0 1.5 %copy-start.2 = (bf16[4,4,64,256]{3,2,0,1:T(8,128)(2,1)S(1)}, bf16[4,4,64,256]{3,2,0,1:T(8,128)(2,1)}, u32[]{:S(2)}) copy-start(bf16[4,4,64,256]{3,2,0,1:T(8,128)(2,1)} %get-tuple-element.31) | copy-start | bytes 1572868
  26.0 1.5 %copy-start.9 = (bf16[3,64,64]{2,1,0:T(8,128)(2,1)S(1)}, bf16[3,64,64]{2,1,0:T(8,128)(2,1)}, u32[]{:S(2)}) copy-start(bf16[3,64,64]{2,1,0:T(8,128)(2,1)} %param.11) | copy-start | bytes 73732
  27.6 1.0 %copy-start.1 = (bf16[4,1,4,64,256]{4,3,2,1,0:T(8,128)(2,1)S(1)}, bf16[4,1,4,64,256]{4,3,2,1,0:T(8,128)(2,1)}, u32[]{:S(2)}) copy-start(bf16[4,1,4,64,256]{4,3,2,1,0:T(8,128)(2,1)} %param.9) | copy-start | bytes 1572868
  28.6 0.7 copy-start.10
  36.5 1.0 %copy-start.3 = (bf16[4,4,64,256]{3,2,0,1:T(8,128)(2,1)S(1)}, bf16[4,4,64,256]{3,2,0,1:T(8,128)(2,1)}, u32[]{:S(2)}) copy-start(bf16[4,4,64,256]{3,2,0,1:T(8,128)(2,1)} %get-tuple-element.31) | copy-start | bytes 1572868
  36.5 1.2 %copy-start.4 = (bf16[4,4,64,256]{3,2,1,0:T(8,128)(2,1)S(1)}, bf16[4,4,64,256]{3,2,1,0:T(8,128)(2,1)}, u32[]{:S(2)}) copy-start(bf16[4,4,64,256]{3,2,1,0:T(8,128)(2,1)} %get-tuple-element.51) | copy-start | bytes 1572868
  71.9 1.2 %copy-start.6 = (f32[8,40,128]{2,1,0:T(8,128)S(1)}, f32[8,40,128]{2,1,0:T(8,128)}, u32[]{:S(2)}) copy-start(f32[8,40,128]{2,1,0:T(8,128)} %get-tuple-element.20) | copy-start | bytes 491524

commit v3 on v2

--- a/solution.py
+++ b/solution.py
@@ -21,6 +21,31 @@
     )
 
 
+def meet(whole_tile, whole_group):
+    me, tiles = lax.axis_index("tile"), lax.axis_size("tile")
+    chart, charts = lax.axis_index("diamond"), lax.axis_size("diamond")
+    line, lines = lax.axis_index("tm"), lax.axis_size("tm")
+    mine, size = line * charts + chart, lines * charts
+    partners = [
+        {"diamond": lax.rem(chart + turn, charts), "tile": lax.rem(me + step, tiles)}
+        for turn in sorted({1, charts - 1})
+        for step in range(tiles)
+    ]
+    steps = range(1, tiles) if whole_tile else sorted({1, tiles - 1})
+    partners += [{"tile": lax.rem(me + step, tiles)} for step in steps]
+    if whole_group:
+        others = [lax.rem(mine + step, size) for step in range(1, size)]
+        partners += [{"tm": one // charts, "diamond": lax.rem(one, charts)} for one in others]
+    else:
+        partners += [{"tm": lax.rem(line + step, lines)} for step in sorted({1, lines - 1})]
+    barrier = pltpu.get_barrier_semaphore()
+    for partner in partners:
+        pl.semaphore_signal(
+            barrier, inc=1, device_id=partner, device_id_type=pl.DeviceIdType.MESH
+        )
+    pl.semaphore_wait(barrier, len(partners))
+
+
 def line_copies(axis, to_next, at_next, to_prev, at_prev, send, recv):
     me, size = lax.axis_index(axis), lax.axis_size(axis)
     up = remote(to_next, at_next, send.at[0], recv.at[0], {axis: lax.rem(me + 1, size)})
@@ -78,6 +103,7 @@
     strips, field, cotangent, gathered, above, below, before, after,
     seam_send, seam_recv, row_send, row_recv, frame_send, frame_recv,
 ):
+    meet(False, False)
     rows, frames = field.shape[1], field.shape[0]
     parts = (
         seam_copies(strips, gathered, seam_send, seam_recv),
@@ -97,6 +123,7 @@
     seam_send, seam_recv, row_send, row_recv,
     scattered, scatter_send, scatter_recv, group, group_send, group_recv, out_send, out_recv,
 ):
+    meet(True, True)
     me, tiles = lax.axis_index("tile"), lax.axis_size("tile")
     charts, lines = lax.axis_size("diamond"), lax.axis_size("tm")
     mine = lax.axis_index("tm") * charts + lax.axis_index("diamond")
@@ -179,7 +206,7 @@
         scratch_shapes=[
             dma((2, tiles)), dma((2, tiles)), dma((2,)), dma((2,)), dma((2,)), dma((2,)),
         ],
-        compiler_params=pltpu.CompilerParams(has_side_effects=True),
+        compiler_params=pltpu.CompilerParams(collective_id=0, has_side_effects=True),
         name="first_exchange",
     )(strips, field, cotangent)
 
@@ -203,7 +230,7 @@
             pltpu.VMEM((size,) + terms.shape[1:], terms.dtype), dma((size,)), dma((size,)),
             dma((tiles,)), dma((tiles,)),
         ],
-        compiler_params=pltpu.CompilerParams(has_side_effects=True),
+        compiler_params=pltpu.CompilerParams(collective_id=1, has_side_effects=True),
         name="last_exchange",
     )(strips, up_row, down_row, terms)
 
@@ -263,15 +290,16 @@
                 term = jnp.pad(term, ((0, 0), (1 + a, 1 - a), (0, 0)))
                 seam = term if seam is None else seam + term
         sides.append(seam)
-    return spread, jnp.stack(sides).astype(jnp.bfloat16), jnp.stack(hex_terms + time_terms)
+    return spread, jnp.stack(sides).astype(jnp.bfloat16), jnp.stack(
+        [
+            jnp.concatenate(pair, axis=-1)
+            for pair in zip(hex_terms[:5], hex_terms[5:] + time_terms)
+        ]
+    )
 
 
 def seam_columns(block):
-    columns = block.shape[-1]
-    pick = jnp.array([columns - 1, 0])[:, None] == jnp.arange(columns)[None, :]
-    return jnp.einsum(
-        "sx,frcx->sfrc", pick.astype(block.dtype), block, preferred_element_type=jnp.float32
-    ).astype(block.dtype)
+    return jnp.stack([block[..., block.shape[-1] - 1], block[..., 0]])
 
 
 def shards(activations, upstream, hex_weight, time_weight, left_map, right_map):
@@ -342,7 +370,9 @@
     column = jnp.arange(columns)
     total = total + jnp.where(column == 0, into_first[..., None], 0.0)
     total = total + jnp.where(column == columns - 1, into_last[..., None], 0.0)
-    return total.astype(jnp.bfloat16)[:, None], sums[:7], sums[7:]
+    ahead, behind = sums[..., :channels], sums[..., channels:]
+    grad_hex = jnp.concatenate([ahead, behind[:2]], axis=0)
+    return total.astype(jnp.bfloat16)[:, None], grad_hex, behind[2:]
 
 
 def solution(mesh):

time: 75.2 us -> 61.3 us (0.82)
  matrix products: 19.4 us -> 10.6 us
  Pallas kernels: 36.1 us -> 29.6 us
  other arithmetic: 5.82 us -> 6.74 us
    dot_general x7, matrix products: 6.69 us -> 2.32 us  [local_math(): jnp.einsum('frcx,frdx->cd', window, grad_wide, preferred_element_type=jnp...]
    pallas_call x1, Pallas kernels: 22.3 us -> 18.4 us  [exchange_end(): pl.pallas_call(last_exchange, out_shape=(jax.ShapeDtypeStruct((tiles,) +...]
    slice x3 -> x4, local copies, waits for them, and re-layouts: 1.38 us -> 4.55 us  [the longest x2 2 us: seam_columns(): return jnp.stack([block[..., block.shape[-1] - 1], block[..., 0]])]
    pallas_call x1, Pallas kernels: 13.8 us -> 11.2 us  [exchange_start(): pl.pallas_call(first_exchange, out_shape=(jax.ShapeDtypeStruct((tiles,) +...]
    dot_general x3, matrix products: 2.68 us -> 0.87 us  [local_math(): jnp.einsum('frcx,frdx->cd', active, shifted, preferred_element_type=jnp.f...]
    dot_general x2 -> x0, matrix products: 1.7 us -> none  [seam_columns(): jnp.einsum('sx,frcx->sfrc', pick.astype(block.dtype), block, preferred_el...]
    another operation x1 -> x0, local copies, waits for them, and re-layouts: 1.12 us -> none  [local_math(): jnp.stack(hex_terms + time_terms)]
    dot_general x7, matrix products: 3.84 us -> 2.95 us  [local_math(): jnp.einsum('frcx,cd->frdx', windows[number], hex_weight[number], preferre...]
where the time goes in v3:
time: 61.3 us; the launch traced here: 60.8 us
  Pallas kernels  29.6 us (48%)
  local copies, waits for them, and re-layouts  12.8 us (21%)
  matrix products  10.6 us (17%)
  other arithmetic  6.74 us (11%)
  between operations  1.01 us (2%)
    pallas_call x1, Pallas kernels, exchange_end(): pl.pallas_call(last_exchange, out_shape=(jax.ShapeDtypeStruct((tiles,) +...  18.4 us
    pallas_call x1, Pallas kernels, exchange_start(): pl.pallas_call(first_exchange, out_shape=(jax.ShapeDtypeStruct((tiles,) +...  11.2 us
    dot_general x7, matrix products, local_math(): jnp.einsum('frcx,cd->frdx', windows[number], hex_weight[number], preferre...  2.95 us
    unnamed x18, local copies, waits for them, and re-layouts  2.49 us
    dot_general x7, matrix products, local_math(): jnp.einsum('frcx,frdx->cd', window, grad_wide, preferred_element_type=jnp...  2.32 us
    slice x2, local copies, waits for them, and re-layouts, seam_columns(): return jnp.stack([block[..., block.shape[-1] - 1], block[..., 0]])  2 us
    dot_general x7, matrix products, local_math(): jnp.einsum('frdx,cd->frcx', grad_wide, hex_weight[number], preferred_elem...  1.93 us
    slice x1, local copies, waits for them, and re-layouts, shards(): return (total.astype(jnp.bfloat16)[:, None], grad_hex, behind[2:])  1.64 us

profile of v3, /device:TPU:1, one launch (start us, length us, event | category | flops | bytes accessed | tf_op | source)
XLA Modules:
  0.0 60.8 jit_solution(904155218715861482)
XLA Ops:
  0.7 0.8 %fusion.106 = (s32[32]{0:T(128)S(1)}, s32[32]{0:T(128)S(1)}, s32[32]{0:T(128)S(1)}, s32[32]{0:T(128)S(1)}, s32[32]{0:T(128)S(1)}, /*index=5*/s32[32]{0:T(128)S(1)}) fusion(s32[2,32]{1,0:T(2,128)} %param.11, s32[]{:T(128)S(6)} %select_n.65, s32[]{:T(128)S(6)} %select_n.61, s32[2,32]{1,0:T(2,128)} %param.10), kind=kLoop, calls=%fused_computation.195 | loop fusion | bytes 1288 | tf_op jit(solution)/shard_map/dynamic_slice | solution.py:322
  3.1 1.5 %slice_reduce_fusion.3 = (bf16[4,4,64]{2,1,0:T(4,128)(2,1)S(1)}, bf16[4,4,64]{2,1,0:T(4,128)(2,1)S(1)}) fusion(bf16[4,4,64,256]{3,2,1,0:T(8,128)(2,1)} %bitcast.392), kind=kLoop, calls=%fused_computation.90 | loop fusion | bytes 8192 | tf_op jit(solution)/shard_map/slice | solution.py:302
  4.6 0.6 pad_maximum_fusion.12.strips
  5.2 1.1 %copy.211 = bf16[4,1,4,64,256]{4,3,0,2,1:T(8,128)(2,1)S(1)} copy(bf16[4,1,4,64,256]{4,3,2,1,0:T(8,128)(2,1)} %param.7) | data formatting | bytes 1048576 | tf_op args[1]
  6.3 11.2 %first_exchange.1 = (bf16[8,2,16,64]{3,2,1,0:T(8,128)(2,1)}, bf16[4,64,256]{2,1,0:T(8,128)(2,1)}, bf16[4,64,256]{2,1,0:T(8,128)(2,1)}, bf16[4,64,256]{2,1,0:T(8,128)(2,1)}, bf16[4,64,256]{2,1,0:T(8,128)(2,1)}) custom-call(bf16[2,16,64]{2,1,0:T(8,128)(2,1)} %pad_maximum_fusion.12.strips, bf16[4,4,64,256]{3,2,1,0:T(8,128)(2,1)} %bitcast.393, ...), custom_call_target="tpu_custom_call" | custom-call | tf_op jit(solution)/shard_map/first_exchange/pallas_call | solution.py:199
  17.5 1.0 %select_bitcast_fusion.4 = (bf16[1,4,64,256]{3,2,0,1:T(8,128)(2,1)S(1)}, bf16[1,4,64,256]{3,2,0,1:T(8,128)(2,1)S(1)}) fusion(bf16[4,64,256]{2,1,0:T(8,128)(2,1)} %get-tuple-element.13, pred[]{:T(512)S(6)} %gt.7, bf16[4,64,256]{2,1,0:T(8,128)(2,1)} %get-tuple-element.12, pred[]{:T(512)S(6)} %lt.19), kind=kLoop, calls=%fused_computation.105 | loop fusion | flops 131072 | bytes 524290 | tf_op jit(solution)/shard_map/broadcast_in_dim | solution.py:340
  18.5 0.8 %fusion.120 = (bf16[8,1,16,64]{3,2,1,0:T(8,128)(2,1)S(1)}, bf16[8,1,16,64]{3,2,1,0:T(8,128)(2,1)S(1)}) fusion(bf16[8,2,16,64]{3,2,1,0:T(8,128)(2,1)} %get-tuple-element.16), kind=kLoop, calls=%fused_computation.209 | loop fusion | bytes 65536 | tf_op jit(solution)/shard_map/slice | solution.py:336
  20.8 0.4 convolution_bitcast_fusion.8
  21.2 0.4 convolution_bitcast_fusion.11
  21.6 0.5 convolution_bitcast_fusion.7
  22.0 0.5 convolution_bitcast_fusion.12
  23.1 0.6 %multiply_convert_fusion = (bf16[4,4,64,256]{3,2,1,0:T(8,128)(2,1)S(1)}, f32[4,4,64,256]{3,2,1,0:T(8,128)S(1)}) fusion(f32[4,4,64,256]{3,2,1,0:T(8,128)S(1)} %convolution_bitcast_fusion.7, f32[4,4,64,256]{3,2,1,0:T(8,128)S(1)} %convolution_bitcast_fusion.8, f32[4,4,64,256]{3,2,1,0:T(8,128)S(1)} %convolution_bitcast_fusion.9, ...), kind=kOutput, calls=%fused_computation.57 | convolution fusion | flops 36438016 | bytes 8404992 | tf_op jit(solution)/shard_map/frcx,cd->frdx/dot_general | solution.py:249
  25.3 0.5 fusion.11
  25.9 0.5 slice_reduce_fusion.1
  27.0 0.6 %pad_maximum_fusion.11.strips = bf16[2,24,64]{2,1,0:T(8,128)(2,1)} fusion(bf16[1,24,64]{2,1,0:T(8,128)(2,1)S(1)} %stack.38, bf16[1,24,64]{2,1,0:T(8,128)(2,1)S(1)} %stack.37), kind=kLoop, calls=%fused_computation.167 | loop fusion | flops 3072 | bytes 12288 | tf_op jit(solution)/shard_map/stack | solution.py:293
  27.9 0.3 convolution_bitcast_fusion.25
  28.2 0.3 convolution_bitcast_fusion.22
  28.6 0.4 convolution_bitcast_fusion.24
  29.0 0.4 convolution_bitcast_fusion.23
  31.3 0.3 slice.205
  32.5 0.3 slice.206
  33.1 0.8 %fusion.118 = (bf16[4,6,64,256]{3,2,0,1:T(8,128)(2,1)S(1)}, f32[4,6,64,256]{3,2,0,1:T(8,128)S(1)}) fusion(f32[4,4,64,255]{3,2,0,1:T(8,128)S(1)} %bitcast.408, f32[4,4,64,255]{3,2,0,1:T(8,128)S(1)} %slice.206, f32[4,4,64,256]{3,2,0,1:T(8,128)S(1)} %convolution_bitcast_fusion.2, f32[4,4,64,256]{3,2,0,1:T(8,128)S(1)} %convolution_bitcast_fusion.3, ...), kind=kLoop, calls=%fused_computation.207 | loop fusion | flops 2752512 | bytes 9682944 | tf_op jit(solution)/shard_map/convert.7
  33.9 0.7 %slice_bitcast_fusion = (bf16[4,64,256]{2,1,0:T(8,128)(2,1)}, bf16[4,64,256]{2,1,0:T(8,128)(2,1)}) fusion(bf16[4,6,64,256]{3,2,0,1:T(8,128)(2,1)S(1)} %get-tuple-element.31), kind=kLoop, calls=%fused_computation.99 | loop fusion | bytes 524288 | tf_op jit(solution)/shard_map/convert_element_type | solution.py:347
  34.6 18.4 %last_exchange.1 = (bf16[8,2,24,64]{3,2,1,0:T(8,128)(2,1)}, bf16[4,64,256]{2,1,0:T(8,128)(2,1)}, bf16[4,64,256]{2,1,0:T(8,128)(2,1)}, f32[8,40,128]{2,1,0:T(8,128)}) custom-call(bf16[2,24,64]{2,1,0:T(8,128)(2,1)} %pad_maximum_fusion.11.strips, bf16[4,64,256]{2,1,0:T(8,128)(2,1)} %get-tuple-element.34.up_row, bf16[4,64,256]{2,1,0:T(8,128)(2,1)} %get-tuple-element.33.down_row, ...), custom_call_target="tpu_custom_call" | custom-call | tf_op jit(solution)/shard_map/last_exchange/pallas_call | solution.py:219
  53.0 0.9 %select_bitcast_fusion.1 = bf16[4,1,64,256]{3,2,0,1:T(8,128)(2,1)S(1)} fusion(bf16[4,64,256]{2,1,0:T(8,128)(2,1)} %get-tuple-element.17, pred[]{:T(512)S(6)} %gt.8), kind=kLoop, calls=%fused_computation.102 | loop fusion | flops 65536 | bytes 262145 | tf_op jit(solution)/shard_map/broadcast_in_dim | solution.py:354
  53.9 0.9 %slice.214 = f32[2,64,64]{2,1,0:T(8,128)S(1)} slice(f32[5,64,128]{2,1,0:T(8,128)} %bitcast.410), slice={[0:2], [0:64], [64:128]} | slice | bytes 65536 | tf_op jit(solution)/shard_map/slice | solution.py:374
  54.8 1.6 %slice.215 = f32[3,64,64]{2,1,0:T(8,128)} slice(f32[5,64,128]{2,1,0:T(8,128)} %bitcast.411), slice={[2:5], [0:64], [64:128]} | slice | bytes 98304 | tf_op jit(solution)/shard_map/slice | solution.py:375
  56.5 0.8 %fusion.119 = (bf16[8,1,24,64]{3,2,1,0:T(8,128)(2,1)S(1)}, bf16[8,1,24,64]{3,2,1,0:T(8,128)(2,1)S(1)}) fusion(bf16[8,2,24,64]{3,2,1,0:T(8,128)(2,1)} %get-tuple-element.19), kind=kLoop, calls=%fused_computation.208 | loop fusion | bytes 98304 | tf_op jit(solution)/shard_map/slice | solution.py:368
  57.9 0.9 %select_bitcast_fusion = bf16[4,1,64,256]{3,2,0,1:T(8,128)(2,1)S(1)} fusion(bf16[4,64,256]{2,1,0:T(8,128)(2,1)} %get-tuple-element.18, pred[]{:T(512)S(6)} %lt.20), kind=kLoop, calls=%fused_computation.101 | loop fusion | flops 65536 | bytes 262145 | tf_op jit(solution)/shard_map/broadcast_in_dim | solution.py:355
  58.8 0.4 fusion.27
  59.2 0.8 %copy.108 = bf16[4,1,4,64,256]{4,3,2,1,0:T(8,128)(2,1)} copy(bf16[4,1,4,64,256]{4,3,0,2,1:T(8,128)(2,1)S(1)} %fusion.27) | data formatting | bytes 1048576
  60.0 0.7 %pad_maximum_fusion.10 = f32[7,64,64]{2,1,0:T(8,128)} fusion(f32[2,64,64]{2,1,0:T(8,128)S(1)} %slice.214, f32[5,64,64]{2,1,0:T(8,128)S(1)} %bitcast.412), kind=kLoop, calls=%fused_computation.91 | loop fusion | flops 28672 | bytes 229376 | tf_op jit(solution)/shard_map/concatenate | solution.py:374
  (80 shorter events, 9.6 us)
Async XLA Ops:
  17.5 2.3 %copy-start.5 = (bf16[4,64,256]{2,1,0:T(8,128)(2,1)S(1)}, bf16[4,64,256]{2,1,0:T(8,128)(2,1)}, u32[]{:S(2)}) copy-start(bf16[4,64,256]{2,1,0:T(8,128)(2,1)} %get-tuple-element.14) | copy-start | bytes 393220
  17.5 2.3 %copy-start.6 = (bf16[4,64,256]{2,1,0:T(8,128)(2,1)S(1)}, bf16[4,64,256]{2,1,0:T(8,128)(2,1)}, u32[]{:S(2)}) copy-start(bf16[4,64,256]{2,1,0:T(8,128)(2,1)} %get-tuple-element.15) | copy-start | bytes 393220
  19.7 1.0 %copy-start = (bf16[4,1,4,64,256]{4,3,2,1,0:T(8,128)(2,1)S(1)}, bf16[4,1,4,64,256]{4,3,2,1,0:T(8,128)(2,1)}, u32[]{:S(2)}) copy-start(bf16[4,1,4,64,256]{4,3,2,1,0:T(8,128)(2,1)} %param.6) | copy-start | bytes 1572868
  19.7 1.1 %copy-start.2 = (bf16[7,64,64]{2,1,0:T(8,128)(2,1)S(1)}, bf16[7,64,64]{2,1,0:T(8,128)(2,1)}, u32[]{:S(2)}) copy-start(bf16[7,64,64]{2,1,0:T(8,128)(2,1)} %param.8) | copy-start | bytes 172036
  23.1 1.0 %copy-start.1 = (bf16[4,1,4,64,256]{4,3,2,1,0:T(8,128)(2,1)S(1)}, bf16[4,1,4,64,256]{4,3,2,1,0:T(8,128)(2,1)}, u32[]{:S(2)}) copy-start(bf16[4,1,4,64,256]{4,3,2,1,0:T(8,128)(2,1)} %param.7) | copy-start | bytes 1572868
  23.8 1.0 %copy-start.7 = (bf16[3,64,64]{2,1,0:T(8,128)(2,1)S(1)}, bf16[3,64,64]{2,1,0:T(8,128)(2,1)}, u32[]{:S(2)}) copy-start(bf16[3,64,64]{2,1,0:T(8,128)(2,1)} %param.9) | copy-start | bytes 73732
  30.4 0.7 %copy-start.4 = (f32[5,64,128]{2,1,0:T(8,128)}, f32[5,64,128]{2,1,0:T(8,128)S(1)}, u32[]{:S(2)}) copy-start(f32[5,64,128]{2,1,0:T(8,128)S(1)} %fusion.49) | copy-start | bytes 491524
  58.8 1.3 %copy-start.3 = (f32[8,40,128]{2,1,0:T(8,128)S(1)}, f32[8,40,128]{2,1,0:T(8,128)}, u32[]{:S(2)}) copy-start(f32[8,40,128]{2,1,0:T(8,128)} %get-tuple-element.20) | copy-start | bytes 491524

commit v4 on v3

--- a/solution.py
+++ b/solution.py
@@ -2,6 +2,7 @@
 import jax.numpy as jnp
 from jax import lax
 from jax.experimental import pallas as pl
+from jax.experimental.layout import Layout, with_layout_constraint
 from jax.experimental.pallas import tpu as pltpu
 from jax.sharding import PartitionSpec as P
 
@@ -119,8 +120,8 @@
 
 
 def last_exchange(
-    strips, up_row, down_row, terms, gathered, above, below, sums,
-    seam_send, seam_recv, row_send, row_recv,
+    strips, up_row, down_row, terms, gathered, above, below, grad_hex, grad_time,
+    seam_send, seam_recv, row_send, row_recv, sums,
     scattered, scatter_send, scatter_recv, group, group_send, group_recv, out_send, out_recv,
 ):
     meet(True, True)
@@ -134,7 +135,7 @@
 
     first = [
         tile_copy(
-            terms.at[lax.rem(me + step, tiles)], scattered.at[me], scatter_send,
+            terms.at[:, lax.rem(me + step, tiles)], scattered.at[me], scatter_send,
             scatter_recv.at[me], step,
         )
         for step in range(1, tiles)
@@ -147,11 +148,11 @@
     )
     for start, _ in parts:
         start()
-    total = terms[me]
+    total = terms[:, me]
     for step in range(1, tiles):
         other = lax.rem(me + step, tiles)
         tile_copy(
-            terms.at[other], scattered.at[other], scatter_send, scatter_recv.at[other], step
+            terms.at[:, other], scattered.at[other], scatter_send, scatter_recv.at[other], step
         ).wait_recv()
         total = total + scattered[other]
     group[mine] = total
@@ -183,6 +184,15 @@
     for step in range(1, tiles):
         other = lax.rem(me + step, tiles)
         tile_copy(sums.at[other], sums.at[other], out_send, out_recv.at[other], step).wait_recv()
+    channels = grad_hex.shape[1]
+    pairs, _, span, _ = terms.shape
+    taps = grad_hex.shape[0]
+    for number in range(tiles):
+        chunk = sums[number]
+        rows = pl.ds(number * span, span)
+        grad_hex[:pairs, rows] = chunk[..., :channels]
+        grad_hex[pairs:, rows] = chunk[: taps - pairs, :, channels:]
+        grad_time[:, rows] = chunk[taps - pairs :, :, channels:]
     for copy in first + second + third:
         copy.wait_send()
     for _, wait in parts:
@@ -216,18 +226,22 @@
     size = lax.axis_size("tm") * lax.axis_size("diamond")
     dma = pltpu.SemaphoreType.DMA
     line = jax.ShapeDtypeStruct(up_row.shape, up_row.dtype)
+    chunk = terms.shape[:1] + terms.shape[2:]
+    channels = up_row.shape[1]
     return pl.pallas_call(
         last_exchange,
         out_shape=(
             jax.ShapeDtypeStruct((tiles,) + strips.shape, strips.dtype), line, line,
-            jax.ShapeDtypeStruct(terms.shape, terms.dtype),
+            jax.ShapeDtypeStruct((7, channels, channels), terms.dtype),
+            jax.ShapeDtypeStruct((3, channels, channels), terms.dtype),
         ),
         in_specs=[ANY, ANY, ANY, VMEM],
-        out_specs=(ANY, ANY, ANY, VMEM),
+        out_specs=(ANY, ANY, ANY, VMEM, VMEM),
         scratch_shapes=[
             dma((2, tiles)), dma((2, tiles)), dma((2,)), dma((2,)),
-            pltpu.VMEM(terms.shape, terms.dtype), dma((tiles,)), dma((tiles,)),
-            pltpu.VMEM((size,) + terms.shape[1:], terms.dtype), dma((size,)), dma((size,)),
+            pltpu.VMEM((tiles,) + chunk, terms.dtype),
+            pltpu.VMEM((tiles,) + chunk, terms.dtype), dma((tiles,)), dma((tiles,)),
+            pltpu.VMEM((size,) + chunk, terms.dtype), dma((size,)), dma((size,)),
             dma((tiles,)), dma((tiles,)),
         ],
         compiler_params=pltpu.CompilerParams(collective_id=1, has_side_effects=True),
@@ -241,6 +255,8 @@
 
 
 def local_math(padded, framed, hex_weight, time_weight, frames, tile_rows, channels, columns):
+    row_major = Layout(major_to_minor=(0, 1, 2, 3))
+    padded = with_layout_constraint(padded, row_major)
     hidden = jnp.zeros((frames, tile_rows, channels, columns), jnp.float32)
     windows = [
         padded[:, 1 + a : 1 + a + tile_rows, :, 1 + b : 1 + b + columns] for a, b in OFFSETS
@@ -262,11 +278,12 @@
             jnp.einsum("frcx,frdx->cd", active, shifted, preferred_element_type=jnp.float32)
         )
     grad_wide = (grad_act * silu_slope(hidden)).astype(jnp.bfloat16)
+    grad_wide = with_layout_constraint(grad_wide, row_major)
     hex_terms = [
         jnp.einsum("frcx,frdx->cd", window, grad_wide, preferred_element_type=jnp.float32)
         for window in windows
     ]
-    spread = None
+    spread = up_row = down_row = None
     for number, (a, b) in enumerate(OFFSETS):
         term = jnp.einsum(
             "frdx,cd->frcx", grad_wide, hex_weight[number], preferred_element_type=jnp.float32
@@ -275,8 +292,14 @@
             term = jnp.pad(term[..., :-1], ((0, 0), (0, 0), (0, 0), (1, 0)))
         if b == -1:
             term = jnp.pad(term[..., 1:], ((0, 0), (0, 0), (0, 0), (0, 1)))
-        term = jnp.pad(term, ((0, 0), (1 + a, 1 - a), (0, 0), (0, 0)))
+        if a == 1:
+            down_row = term[:, -1] if down_row is None else down_row + term[:, -1]
+            term = jnp.pad(term[:, :-1], ((0, 0), (1, 0), (0, 0), (0, 0)))
+        if a == -1:
+            up_row = term[:, 0] if up_row is None else up_row + term[:, 0]
+            term = jnp.pad(term[:, 1:], ((0, 0), (0, 1), (0, 0), (0, 0)))
         spread = term if spread is None else spread + term
+    edges = up_row.astype(jnp.bfloat16), down_row.astype(jnp.bfloat16)
     seams = seam_columns(grad_wide)
     sides = []
     for side, b in ((0, 1), (1, -1)):
@@ -290,12 +313,9 @@
                 term = jnp.pad(term, ((0, 0), (1 + a, 1 - a), (0, 0)))
                 seam = term if seam is None else seam + term
         sides.append(seam)
-    return spread, jnp.stack(sides).astype(jnp.bfloat16), jnp.stack(
-        [
-            jnp.concatenate(pair, axis=-1)
-            for pair in zip(hex_terms[:5], hex_terms[5:] + time_terms)
-        ]
-    )
+    pairs = zip(hex_terms[:5], hex_terms[5:] + time_terms)
+    terms = jnp.stack([jnp.concatenate(pair, axis=-1) for pair in pairs])
+    return spread, edges, jnp.stack(sides).astype(jnp.bfloat16), terms
 
 
 def seam_columns(block):
@@ -304,7 +324,8 @@
 
 def shards(activations, upstream, hex_weight, time_weight, left_map, right_map):
     field = activations[:, 0]
-    cotangent = upstream[:, 0]
+    row_major = Layout(major_to_minor=(0, 1, 2, 3))
+    cotangent = with_layout_constraint(upstream[:, 0], row_major)
     frames, tile_rows, channels, columns = field.shape
     chart, charts = lax.axis_index("diamond"), lax.axis_size("diamond")
     tile, tiles = lax.axis_index("tile"), lax.axis_size("tile")
@@ -338,21 +359,21 @@
     rows = jnp.concatenate([above[:, None], field, below[:, None]], axis=1)
     padded = jnp.concatenate([ghost_left[..., None], rows, ghost_right[..., None]], axis=-1)
     framed = jnp.concatenate([before[None], cotangent, after[None]], axis=0)
-    spread, seams, terms = local_math(
+    spread, edges, seams, terms = local_math(
         padded, framed, hex_weight, time_weight, frames, tile_rows, channels, columns
     )
     strips = seams.reshape(2, frames * wide, channels)
-    count = terms.size // (tiles * 128)
-    gathered, above, below, sums = exchange_end(
-        strips, spread[:, 0].astype(jnp.bfloat16), spread[:, wide - 1].astype(jnp.bfloat16),
-        terms.reshape(tiles, count, 128),
-    )
-    sums = sums.reshape(terms.shape)
-    total = cotangent.astype(jnp.float32) + spread[:, 1 : tile_rows + 1]
-    above = jnp.where(tile > 0, above, 0).astype(jnp.float32)
-    below = jnp.where(tile < tiles - 1, below, 0).astype(jnp.float32)
-    total = total + jnp.pad(above[:, None], ((0, 0), (0, tile_rows - 1), (0, 0), (0, 0)))
-    total = total + jnp.pad(below[:, None], ((0, 0), (tile_rows - 1, 0), (0, 0), (0, 0)))
+    gathered, above, below, grad_hex, grad_time = exchange_end(
+        strips, *edges, terms.reshape(terms.shape[0], tiles, channels // tiles, 2 * channels)
+    )
+    row = jnp.arange(tile_rows)[:, None, None]
+    total = cotangent.astype(jnp.float32) + spread
+    total = total + jnp.where(
+        (row == 0) & (tile > 0), above[:, None].astype(jnp.float32), 0.0
+    )
+    total = total + jnp.where(
+        (row == tile_rows - 1) & (tile < tiles - 1), below[:, None].astype(jnp.float32), 0.0
+    )
     own_rows = first_row + jnp.arange(tile_rows)
 
     def landing(strip, table, number):
@@ -370,9 +391,8 @@
     column = jnp.arange(columns)
     total = total + jnp.where(column == 0, into_first[..., None], 0.0)
     total = total + jnp.where(column == columns - 1, into_last[..., None], 0.0)
-    ahead, behind = sums[..., :channels], sums[..., channels:]
-    grad_hex = jnp.concatenate([ahead, behind[:2]], axis=0)
-    return total.astype(jnp.bfloat16)[:, None], grad_hex, behind[2:]
+    total = with_layout_constraint(total.astype(jnp.bfloat16), row_major)
+    return total[:, None], grad_hex, grad_time
 
 
 def solution(mesh):

time: 61.3 us -> 70.4 us (1.15)
  local copies, waits for them, and re-layouts: 12.8 us -> 16.8 us
  matrix products: 10.6 us -> 14.4 us
  other arithmetic: 6.74 us -> 8.02 us
    unnamed x18 -> x32, local copies, waits for them, and re-layouts: 2.49 us -> 6.84 us
    convert_element_type x0 -> x4, other arithmetic: none -> 4.03 us  [the longest x1 1.63 us: shards(): below[:, None].astype(jnp.float32)]
    broadcast_in_dim x3 -> x0, other arithmetic: 2.24 us -> none  [the longest x1 0.93 us: shards(): above[:, None]]
    slice x2 -> x6, local copies, waits for them, and re-layouts: 2.55 us -> 0.86 us  [the longest x3 0.51 us: local_math(): term = jnp.pad(term[:, 1:], ((0, 0), (0, 1), (0, 0), (0, 0)))]
    slice x1, local copies, waits for them, and re-layouts: 0.01 us -> 1.43 us  [shards(): into_last = landing(gathered[:, 1], left_map, lax.rem(chart + 1, charts))]
    dot_general x7, matrix products: 1.93 us -> 3.33 us  [local_math(): jnp.einsum('frdx,cd->frcx', grad_wide, hex_weight[number], preferred_elem...]
    broadcast_in_dim x1, other arithmetic: 0.02 us -> 1.14 us  [shards(): rows = jnp.concatenate([above[:, None], field, below[:, None]], axis=1)]
    dot_general x7, matrix products: 2.95 us -> 3.86 us  [local_math(): jnp.einsum('frcx,cd->frdx', windows[number], hex_weight[number], preferre...]
where the time goes in v4:
time: 70.4 us; the launch traced here: 69.4 us
  Pallas kernels  29.2 us (41%)
  local copies, waits for them, and re-layouts  16.8 us (24%)
  matrix products  14.4 us (20%)
  other arithmetic  8.02 us (11%)
  between operations  1.02 us (1%)
    pallas_call x1, Pallas kernels, exchange_end(): pl.pallas_call(last_exchange, out_shape=(jax.ShapeDtypeStruct((tiles,) +...  18.1 us
    pallas_call x1, Pallas kernels, exchange_start(): pl.pallas_call(first_exchange, out_shape=(jax.ShapeDtypeStruct((tiles,) +...  11.2 us
    unnamed x32, local copies, waits for them, and re-layouts  6.84 us
    dot_general x7, matrix products, local_math(): jnp.einsum('frcx,cd->frdx', windows[number], hex_weight[number], preferre...  3.86 us
    dot_general x7, matrix products, local_math(): jnp.einsum('frdx,cd->frcx', grad_wide, hex_weight[number], preferred_elem...  3.33 us
    dot_general x7, matrix products, local_math(): jnp.einsum('frcx,frdx->cd', window, grad_wide, preferred_element_type=jnp...  2.33 us
    slice x2, local copies, waits for them, and re-layouts, seam_columns(): return jnp.stack([block[..., block.shape[-1] - 1], block[..., 0]])  1.99 us
    dot_general x3, matrix products, local_math(): jnp.einsum('frdx,cd->frcx', shifted, time_weight[number], preferred_eleme...  1.78 us

profile of v4, /device:TPU:1, one launch (start us, length us, event | category | flops | bytes accessed | tf_op | source)
XLA Modules:
  0.0 69.4 jit_solution(11051570191777051988)
XLA Ops:
  0.6 0.8 %fusion.102 = (s32[32]{0:T(128)S(1)}, s32[32]{0:T(128)S(1)}, s32[32]{0:T(128)S(1)}, s32[32]{0:T(128)S(1)}, s32[32]{0:T(128)S(1)}, /*index=5*/s32[32]{0:T(128)S(1)}) fusion(s32[2,32]{1,0:T(2,128)} %param.11, s32[]{:T(128)S(6)} %select_n.64, s32[]{:T(128)S(6)} %select_n.56, s32[2,32]{1,0:T(2,128)} %param.10), kind=kLoop, calls=%fused_computation.185 | loop fusion | bytes 1288 | tf_op jit(solution)/shard_map/dynamic_slice | solution.py:343
  1.8 1.5 %slice_reduce_fusion.3 = (bf16[4,4,64]{2,1,0:T(4,128)(2,1)S(1)}, bf16[4,4,64]{2,1,0:T(4,128)(2,1)S(1)}) fusion(bf16[4,4,64,256]{3,2,1,0:T(8,128)(2,1)} %bitcast.364), kind=kLoop, calls=%fused_computation.87 | loop fusion | bytes 8192 | tf_op jit(solution)/shard_map/slice | solution.py:322
  3.3 0.6 pad_maximum_fusion.15.strips
  3.9 11.2 %first_exchange.1 = (bf16[8,2,16,64]{3,2,1,0:T(8,128)(2,1)}, bf16[4,64,256]{2,1,0:T(8,128)(2,1)}, bf16[4,64,256]{2,1,0:T(8,128)(2,1)}, bf16[4,64,256]{2,1,0:T(8,128)(2,1)}, bf16[4,64,256]{2,1,0:T(8,128)(2,1)}) custom-call(bf16[2,16,64]{2,1,0:T(8,128)(2,1)} %pad_maximum_fusion.15.strips, bf16[4,4,64,256]{3,2,1,0:T(8,128)(2,1)} %bitcast.365, ...), custom_call_target="tpu_custom_call" | custom-call | tf_op jit(solution)/shard_map/first_exchange/pallas_call | solution.py:209
  15.1 0.8 %fusion.119 = (bf16[8,1,16,64]{3,2,1,0:T(8,128)(2,1)S(1)}, bf16[8,1,16,64]{3,2,1,0:T(8,128)(2,1)S(1)}) fusion(bf16[8,2,16,64]{3,2,1,0:T(8,128)(2,1)} %get-tuple-element.15), kind=kLoop, calls=%fused_computation.202 | loop fusion | bytes 65536 | tf_op jit(solution)/shard_map/slice | solution.py:357
  16.4 1.1 %select_bitcast_fusion = (bf16[4,1,64,256]{3,2,1,0:T(8,128)(2,1)S(1)}, bf16[4,1,64,256]{3,2,1,0:T(8,128)(2,1)S(1)}) fusion(bf16[4,64,256]{2,1,0:T(8,128)(2,1)} %get-tuple-element.17, pred[]{:T(512)S(6)} %lt.22, bf16[4,64,256]{2,1,0:T(8,128)(2,1)} %get-tuple-element.16, pred[]{:T(512)S(6)} %gt.8), kind=kLoop, calls=%fused_computation.90 | loop fusion | flops 131072 | bytes 524290 | tf_op jit(solution)/shard_map/broadcast_in_dim | solution.py:359
  17.9 0.5 convolution_add_fusion.5
  18.9 0.4 convolution_add_fusion.4
  20.4 1.6 %multiply_convert_fusion = (bf16[4,4,64,256]{3,2,1,0:T(8,128)(2,1)}, f32[4,4,64,256]{3,2,1,0:T(8,128)}) fusion(f32[4,4,256,64]{2,3,1,0:T(8,128)S(1)} %convolution_add_fusion.1, bf16[4,6,64,1]{3,2,1,0:T(8,128)(2,1)S(1)} %copy.41, bf16[4,1,64,256]{3,2,1,0:T(8,128)(2,1)S(1)} %get-tuple-element.51, bf16[4,4,64,256]{3,2,1,0:T(8,128)(2,1)S(1)} %bitcast.371, ...), kind=kOutput, calls=%fused_computation.52 | convolution fusion | flops 37224448 | bytes 3817472 | tf_op jit(solution)/shard_map/frcx,cd->frdx/dot_general | solution.py:265
  22.1 0.9 %select_bitcast_fusion.2 = (bf16[1,4,64,256]{3,2,1,0:T(8,128)(2,1)S(1)}, bf16[1,4,64,256]{3,2,1,0:T(8,128)(2,1)S(1)}) fusion(bf16[4,64,256]{2,1,0:T(8,128)(2,1)S(1)} %copy-done.11, pred[]{:T(512)S(6)} %gt.7, bf16[4,64,256]{2,1,0:T(8,128)(2,1)} %get-tuple-element.13, pred[]{:T(512)S(6)} %lt.19), kind=kLoop, calls=%fused_computation.92 | loop fusion | flops 131072 | bytes 524290 | tf_op jit(solution)/shard_map/broadcast_in_dim | solution.py:361
  23.0 1.0 %convolution_bitcast_fusion.7 = f32[4,4,64,256]{3,2,1,0:T(8,128)S(1)} fusion(bf16[4,4,64,256]{3,2,1,0:T(8,128)(2,1)S(1)} %bitcast.379, bf16[1,4,64,256]{3,2,1,0:T(8,128)(2,1)S(1)} %get-tuple-element.53, bf16[3,64,64]{2,1,0:T(8,128)(2,1)} %param.9), kind=kOutput, calls=%fused_computation.7 | convolution fusion | flops 34603008 | bytes 1720320 | tf_op jit(solution)/shard_map/frdx,cd->frcx/dot_general | solution.py:274
  24.3 0.9 %copy-done.14 = f32[4,4,64,256]{3,2,1,0:T(8,128)S(1)} copy-done((f32[4,4,64,256]{3,2,1,0:T(8,128)S(1)}, f32[4,4,64,256]{3,2,1,0:T(8,128)}, u32[]{:S(2)}) %copy-start.14) | copy-done | bytes 1048600
  25.2 0.5 fusion.16
  26.5 0.6 copy-done.5
  28.3 0.7 copy-done.8
  30.7 0.7 copy-done.9
  32.3 1.0 %copy-done.2 = f32[4,4,64,256]{3,2,1,0:T(8,128)} copy-done((f32[4,4,64,256]{3,2,1,0:T(8,128)}, f32[4,4,64,256]{3,2,1,0:T(8,128)S(1)}, u32[]{:S(2)}) %copy-start.2) | copy-done | bytes 1048600
  33.2 0.7 fusion.39.down_row
  34.5 1.0 %copy-done.3 = f32[4,4,64,256]{3,2,1,0:T(8,128)} copy-done((f32[4,4,64,256]{3,2,1,0:T(8,128)}, f32[4,4,64,256]{3,2,1,0:T(8,128)S(1)}, u32[]{:S(2)}) %copy-start.3) | copy-done | bytes 1048600
  35.5 0.8 %fusion.38.up_row = bf16[4,64,256]{2,1,0:T(8,128)(2,1)} fusion(f32[4,4,64,255]{3,2,1,0:T(8,128)S(1)} %bitcast.383, f32[4,4,64,256]{3,2,1,0:T(8,128)S(1)} %convolution_bitcast_fusion.2), kind=kLoop, calls=%fused_computation.88 | loop fusion | flops 131072 | bytes 1437696 | tf_op jit(solution)/shard_map/convert_element_type | solution.py:302
  36.3 0.5 slice_reduce_fusion.1
  37.4 0.6 pad_maximum_fusion.14.strips
  38.0 18.1 %last_exchange.1 = (bf16[8,2,24,64]{3,2,1,0:T(8,128)(2,1)}, bf16[4,64,256]{2,1,0:T(8,128)(2,1)}, bf16[4,64,256]{2,1,0:T(8,128)(2,1)}, f32[7,64,64]{2,1,0:T(8,128)}, f32[3,64,64]{2,1,0:T(8,128)}) custom-call(bf16[2,24,64]{2,1,0:T(8,128)(2,1)} %pad_maximum_fusion.14.strips, bf16[4,64,256]{2,1,0:T(8,128)(2,1)} %fusion.38.up_row, ...), custom_call_target="tpu_custom_call" | custom-call | tf_op jit(solution)/shard_map/last_exchange/pallas_call | solution.py:231
  56.0 1.5 %fusion.118 = (bf16[8,1,24,64]{3,2,1,0:T(8,128)(2,1)S(1)}, bf16[8,1,24,64]{3,2,1,0:T(8,128)(2,1)}) fusion(bf16[8,2,24,64]{3,2,1,0:T(8,128)(2,1)} %get-tuple-element.20), kind=kLoop, calls=%fused_computation.201 | loop fusion | bytes 98304 | tf_op jit(solution)/shard_map/slice | solution.py:389
  58.3 0.9 %convert_element_type.83 = f32[4,64,256]{2,1,0:T(8,128)S(1)} convert(bf16[4,64,256]{2,1,0:T(8,128)(2,1)} %get-tuple-element.18) | non-fusion elementwise | flops 65536 | bytes 393216 | tf_op jit(solution)/shard_map/convert_element_type | solution.py:372
  59.3 1.6 %convert_element_type.84 = f32[4,64,256]{2,1,0:T(8,128)} convert(bf16[4,64,256]{2,1,0:T(8,128)(2,1)} %get-tuple-element.19) | non-fusion elementwise | flops 65536 | bytes 393216 | tf_op jit(solution)/shard_map/convert_element_type | solution.py:375
  60.9 1.4 %copy.62 = bf16[8,1,24,64]{3,0,2,1:T(8,128)(2,1)} copy(bf16[8,1,24,64]{3,2,1,0:T(8,128)(2,1)} %get-tuple-element.34) | data formatting | bytes 49152 | tf_op jit(solution)/shard_map/slice | solution.py:390
  62.9 1.1 %convolution_bitcast_fusion.22 = f32[4,4,64]{2,1,0:T(4,128)S(1)} fusion(bf16[8,4,6,64]{3,0,2,1:T(8,128)(2,1)} %bitcast.387, s32[8,6]{0,1:T(8,128)S(1)} %copy.63, s32[4]{0:T(128)S(1)} %iota_add_fusion), kind=kOutput, calls=%fused_computation.50 | convolution fusion | flops 98496 | bytes 28880 | tf_op jit(solution)/shard_map/rtw,tfwc->frc/dot_general | solution.py:387
  65.3 0.6 copy-done.6
  66.4 1.7 %fusion.17 = bf16[4,1,4,64,256]{4,3,2,1,0:T(8,128)(2,1)} fusion(bf16[4,4,64,256]{3,2,1,0:T(8,128)(2,1)S(1)} %fusion.16, f32[4,3,64,256]{3,2,1,0:T(8,128)S(1)} %pad_slice_fusion.1, f32[4,3,64,256]{3,2,1,0:T(8,128)S(1)} %pad_slice_fusion.3, f32[4,3,64,256]{3,2,1,0:T(8,128)S(1)} %slice-done.1, f32[4,3,64,256]{3,2,1,0:T(8,128)S(1)} %slice-done, ...), kind=kOutput, calls=%fused_computation.33 | convolution fusion | flops 38010880 | bytes 7374848 | tf_op jit(solution)/shard_map/frdx,cd->frcx/dot_general | solution.py:288
  68.1 0.7 copy.130
  68.8 0.6 copy.131
  (94 shorter events, 11.9 us)
Async XLA Ops:
  3.9 13.6 %copy-start = (bf16[4,1,4,64,256]{4,3,2,1,0:T(8,128)(2,1)S(1)}, bf16[4,1,4,64,256]{4,3,2,1,0:T(8,128)(2,1)}, u32[]{:S(2)}) copy-start(bf16[4,1,4,64,256]{4,3,2,1,0:T(8,128)(2,1)} %param.6) | copy-start | bytes 1572868
  3.9 13.6 %copy-start.7 = (bf16[7,64,64]{2,1,0:T(8,128)(2,1)S(1)}, bf16[7,64,64]{2,1,0:T(8,128)(2,1)}, u32[]{:S(2)}) copy-start(bf16[7,64,64]{2,1,0:T(8,128)(2,1)} %param.8) | copy-start | bytes 172036
  16.4 4.0 %copy-start.4 = (bf16[4,6,64,1]{3,2,1,0:T(8,128)(2,1)}, bf16[4,6,64,1]{3,2,1,0:T(8,128)(2,1)S(1)}, u32[]{:S(2)}) copy-start(bf16[4,6,64,1]{3,2,1,0:T(8,128)(2,1)S(1)} %copy.41) | copy-start | bytes 9220
  20.4 1.7 %copy-start.11 = (bf16[4,64,256]{2,1,0:T(8,128)(2,1)S(1)}, bf16[4,64,256]{2,1,0:T(8,128)(2,1)}, u32[]{:S(2)}) copy-start(bf16[4,64,256]{2,1,0:T(8,128)(2,1)} %get-tuple-element.14) | copy-start | bytes 393220
  20.4 2.6 %copy-start.1 = (bf16[4,1,4,64,256]{4,3,2,1,0:T(8,128)(2,1)S(1)}, bf16[4,1,4,64,256]{4,3,2,1,0:T(8,128)(2,1)}, u32[]{:S(2)}) copy-start(bf16[4,1,4,64,256]{4,3,2,1,0:T(8,128)(2,1)} %param.7) | copy-start | bytes 1572868
  22.1 2.0 %copy-start.13 = (bf16[3,64,64]{2,1,0:T(8,128)(2,1)S(1)}, bf16[3,64,64]{2,1,0:T(8,128)(2,1)}, u32[]{:S(2)}) copy-start(bf16[3,64,64]{2,1,0:T(8,128)(2,1)} %param.9) | copy-start | bytes 73732
  24.0 1.2 %copy-start.14 = (f32[4,4,64,256]{3,2,1,0:T(8,128)S(1)}, f32[4,4,64,256]{3,2,1,0:T(8,128)}, u32[]{:S(2)}) copy-start(f32[4,4,64,256]{3,2,1,0:T(8,128)} %get-tuple-element.50) | copy-start | bytes 3145732
  26.1 1.0 %copy-start.5 = (bf16[4,6,64,1]{3,2,1,0:T(8,128)(2,1)S(1)}, bf16[4,6,64,1]{3,2,1,0:T(8,128)(2,1)}, u32[]{:S(2)}) copy-start(bf16[4,6,64,1]{3,2,1,0:T(8,128)(2,1)} %copy-done.4) | copy-start | bytes 9220
  28.0 1.0 %copy-start.8 = (bf16[4,4,64,256]{3,2,1,0:T(8,128)(2,1)S(1)}, bf16[4,4,64,256]{3,2,1,0:T(8,128)(2,1)}, u32[]{:S(2)}) copy-start(bf16[4,4,64,256]{3,2,1,0:T(8,128)(2,1)} %get-tuple-element.49) | copy-start | bytes 1572868
  30.7 0.7 copy-start.9
  32.3 1.0 %copy-start.2 = (f32[4,4,64,256]{3,2,1,0:T(8,128)}, f32[4,4,64,256]{3,2,1,0:T(8,128)S(1)}, u32[]{:S(2)}) copy-start(f32[4,4,64,256]{3,2,1,0:T(8,128)S(1)} %convolution_bitcast_fusion.3) | copy-start | bytes 3145732
  34.5 1.0 %copy-start.3 = (f32[4,4,64,256]{3,2,1,0:T(8,128)}, f32[4,4,64,256]{3,2,1,0:T(8,128)S(1)}, u32[]{:S(2)}) copy-start(f32[4,4,64,256]{3,2,1,0:T(8,128)S(1)} %convolution_bitcast_fusion.2) | copy-start | bytes 3145732
  64.9 1.0 %copy-start.6 = (f32[4,64,256]{2,1,0:T(8,128)S(1)}, f32[4,64,256]{2,1,0:T(8,128)}, u32[]{:S(2)}) copy-start(f32[4,64,256]{2,1,0:T(8,128)} %convert_element_type.84) | copy-start | bytes 786436
  64.9 1.2 %slice-start = ((f32[4,4,64,256]{3,2,1,0:T(8,128)}), f32[4,3,64,256]{3,2,1,0:T(8,128)S(1)}, s32[]{:S(2)}) async-start(f32[4,4,64,256]{3,2,1,0:T(8,128)} %copy-done.2), calls=%async_computation | async-start | bytes 1572864 | tf_op jit(solution)/shard_map/slice | solution.py:297
  64.9 1.4 %slice-start.1 = ((f32[4,4,64,256]{3,2,1,0:T(8,128)}), f32[4,3,64,256]{3,2,1,0:T(8,128)S(1)}, s32[]{:S(2)}) async-start(f32[4,4,64,256]{3,2,1,0:T(8,128)} %copy-done.3), calls=%async_computation.1 | async-start | bytes 1572864 | tf_op jit(solution)/shard_map/slice | solution.py:300
  66.4 1.7 %copy-start.10 = (f32[7,64,64]{2,1,0:T(8,128)S(1)}, f32[7,64,64]{2,1,0:T(8,128)}, u32[]{:S(2)}) copy-start(f32[7,64,64]{2,1,0:T(8,128)} %get-tuple-element.66) | copy-start | bytes 344068
  66.4 2.4 %copy-start.12 = (f32[3,64,64]{2,1,0:T(8,128)S(1)}, f32[3,64,64]{2,1,0:T(8,128)}, u32[]{:S(2)}) copy-start(f32[3,64,64]{2,1,0:T(8,128)} %get-tuple-element.67) | copy-start | bytes 147460

commit v5 on v4

--- a/solution.py
+++ b/solution.py
@@ -2,7 +2,6 @@
 import jax.numpy as jnp
 from jax import lax
 from jax.experimental import pallas as pl
-from jax.experimental.layout import Layout, with_layout_constraint
 from jax.experimental.pallas import tpu as pltpu
 from jax.sharding import PartitionSpec as P
 
@@ -255,8 +254,6 @@
 
 
 def local_math(padded, framed, hex_weight, time_weight, frames, tile_rows, channels, columns):
-    row_major = Layout(major_to_minor=(0, 1, 2, 3))
-    padded = with_layout_constraint(padded, row_major)
     hidden = jnp.zeros((frames, tile_rows, channels, columns), jnp.float32)
     windows = [
         padded[:, 1 + a : 1 + a + tile_rows, :, 1 + b : 1 + b + columns] for a, b in OFFSETS
@@ -278,12 +275,11 @@
             jnp.einsum("frcx,frdx->cd", active, shifted, preferred_element_type=jnp.float32)
         )
     grad_wide = (grad_act * silu_slope(hidden)).astype(jnp.bfloat16)
-    grad_wide = with_layout_constraint(grad_wide, row_major)
     hex_terms = [
         jnp.einsum("frcx,frdx->cd", window, grad_wide, preferred_element_type=jnp.float32)
         for window in windows
     ]
-    spread = up_row = down_row = None
+    spread = None
     for number, (a, b) in enumerate(OFFSETS):
         term = jnp.einsum(
             "frdx,cd->frcx", grad_wide, hex_weight[number], preferred_element_type=jnp.float32
@@ -292,14 +288,8 @@
             term = jnp.pad(term[..., :-1], ((0, 0), (0, 0), (0, 0), (1, 0)))
         if b == -1:
             term = jnp.pad(term[..., 1:], ((0, 0), (0, 0), (0, 0), (0, 1)))
-        if a == 1:
-            down_row = term[:, -1] if down_row is None else down_row + term[:, -1]
-            term = jnp.pad(term[:, :-1], ((0, 0), (1, 0), (0, 0), (0, 0)))
-        if a == -1:
-            up_row = term[:, 0] if up_row is None else up_row + term[:, 0]
-            term = jnp.pad(term[:, 1:], ((0, 0), (0, 1), (0, 0), (0, 0)))
+        term = jnp.pad(term, ((0, 0), (1 + a, 1 - a), (0, 0), (0, 0)))
         spread = term if spread is None else spread + term
-    edges = up_row.astype(jnp.bfloat16), down_row.astype(jnp.bfloat16)
     seams = seam_columns(grad_wide)
     sides = []
     for side, b in ((0, 1), (1, -1)):
@@ -315,7 +305,7 @@
         sides.append(seam)
     pairs = zip(hex_terms[:5], hex_terms[5:] + time_terms)
     terms = jnp.stack([jnp.concatenate(pair, axis=-1) for pair in pairs])
-    return spread, edges, jnp.stack(sides).astype(jnp.bfloat16), terms
+    return spread, jnp.stack(sides).astype(jnp.bfloat16), terms
 
 
 def seam_columns(block):
@@ -324,8 +314,7 @@
 
 def shards(activations, upstream, hex_weight, time_weight, left_map, right_map):
     field = activations[:, 0]
-    row_major = Layout(major_to_minor=(0, 1, 2, 3))
-    cotangent = with_layout_constraint(upstream[:, 0], row_major)
+    cotangent = upstream[:, 0]
     frames, tile_rows, channels, columns = field.shape
     chart, charts = lax.axis_index("diamond"), lax.axis_size("diamond")
     tile, tiles = lax.axis_index("tile"), lax.axis_size("tile")
@@ -359,21 +348,19 @@
     rows = jnp.concatenate([above[:, None], field, below[:, None]], axis=1)
     padded = jnp.concatenate([ghost_left[..., None], rows, ghost_right[..., None]], axis=-1)
     framed = jnp.concatenate([before[None], cotangent, after[None]], axis=0)
-    spread, edges, seams, terms = local_math(
+    spread, seams, terms = local_math(
         padded, framed, hex_weight, time_weight, frames, tile_rows, channels, columns
     )
     strips = seams.reshape(2, frames * wide, channels)
     gathered, above, below, grad_hex, grad_time = exchange_end(
-        strips, *edges, terms.reshape(terms.shape[0], tiles, channels // tiles, 2 * channels)
-    )
-    row = jnp.arange(tile_rows)[:, None, None]
-    total = cotangent.astype(jnp.float32) + spread
-    total = total + jnp.where(
-        (row == 0) & (tile > 0), above[:, None].astype(jnp.float32), 0.0
-    )
-    total = total + jnp.where(
-        (row == tile_rows - 1) & (tile < tiles - 1), below[:, None].astype(jnp.float32), 0.0
-    )
+        strips, spread[:, 0].astype(jnp.bfloat16), spread[:, wide - 1].astype(jnp.bfloat16),
+        terms.reshape(terms.shape[0], tiles, channels // tiles, 2 * channels),
+    )
+    total = cotangent.astype(jnp.float32) + spread[:, 1 : tile_rows + 1]
+    above = jnp.where(tile > 0, above, 0).astype(jnp.float32)
+    below = jnp.where(tile < tiles - 1, below, 0).astype(jnp.float32)
+    total = total + jnp.pad(above[:, None], ((0, 0), (0, tile_rows - 1), (0, 0), (0, 0)))
+    total = total + jnp.pad(below[:, None], ((0, 0), (tile_rows - 1, 0), (0, 0), (0, 0)))
     own_rows = first_row + jnp.arange(tile_rows)
 
     def landing(strip, table, number):
@@ -391,8 +378,7 @@
     column = jnp.arange(columns)
     total = total + jnp.where(column == 0, into_first[..., None], 0.0)
     total = total + jnp.where(column == columns - 1, into_last[..., None], 0.0)
-    total = with_layout_constraint(total.astype(jnp.bfloat16), row_major)
-    return total[:, None], grad_hex, grad_time
+    return total.astype(jnp.bfloat16)[:, None], grad_hex, grad_time
 
 
 def solution(mesh):

time: 70.4 us -> 59.4 us (0.84)
  local copies, waits for them, and re-layouts: 16.8 us -> 11.6 us
  matrix products: 14.4 us -> 10.6 us
  other arithmetic: 8.02 us -> 6.03 us
    convert_element_type x4 -> x0, other arithmetic: 4.03 us -> none  [the longest x1 1.63 us: shards(): below[:, None].astype(jnp.float32)]
    unnamed x32 -> x22, local copies, waits for them, and re-layouts: 6.84 us -> 3.82 us
    broadcast_in_dim x0 -> x3, other arithmetic: none -> 2.24 us  [the longest x1 0.93 us: shards(): above[:, None]]
    slice x1, local copies, waits for them, and re-layouts: 1.43 us -> 0.01 us  [shards(): into_last = landing(gathered[:, 1], left_map, lax.rem(chart + 1, charts))]
    dot_general x7, matrix products: 3.33 us -> 1.93 us  [local_math(): jnp.einsum('frdx,cd->frcx', grad_wide, hex_weight[number], preferred_elem...]
    broadcast_in_dim x1, other arithmetic: 1.14 us -> 0.02 us  [shards(): rows = jnp.concatenate([above[:, None], field, below[:, None]], axis=1)]
    dot_general x7, matrix products: 3.86 us -> 2.95 us  [local_math(): jnp.einsum('frcx,cd->frdx', windows[number], hex_weight[number], preferre...]
    slice x6 -> x0, local copies, waits for them, and re-layouts: 0.86 us -> none  [the longest x3 0.51 us: local_math(): term = jnp.pad(term[:, 1:], ((0, 0), (0, 1), (0, 0), (0, 0)))]
where the time goes in v5:
time: 59.4 us; the launch traced here: 59 us
  Pallas kernels  29.8 us (50%)
  local copies, waits for them, and re-layouts  11.6 us (20%)
  matrix products  10.6 us (18%)
  other arithmetic  6.03 us (10%)
  between operations  1.02 us (2%)
    pallas_call x1, Pallas kernels, exchange_end(): pl.pallas_call(last_exchange, out_shape=(jax.ShapeDtypeStruct((tiles,) +...  18.5 us
    pallas_call x1, Pallas kernels, exchange_start(): pl.pallas_call(first_exchange, out_shape=(jax.ShapeDtypeStruct((tiles,) +...  11.2 us
    unnamed x22, local copies, waits for them, and re-layouts  3.82 us
    dot_general x7, matrix products, local_math(): jnp.einsum('frcx,cd->frdx', windows[number], hex_weight[number], preferre...  2.95 us
    dot_general x7, matrix products, local_math(): jnp.einsum('frcx,frdx->cd', window, grad_wide, preferred_element_type=jnp...  2.32 us
    slice x2, local copies, waits for them, and re-layouts, seam_columns(): return jnp.stack([block[..., block.shape[-1] - 1], block[..., 0]])  2 us
    dot_general x7, matrix products, local_math(): jnp.einsum('frdx,cd->frcx', grad_wide, hex_weight[number], preferred_elem...  1.93 us

profile of v5, /device:TPU:1, one launch (start us, length us, event | category | flops | bytes accessed | tf_op | source)
XLA Modules:
  0.0 59.0 jit_solution(2047626077355089285)
XLA Ops:
  0.7 0.8 %fusion.106 = (s32[32]{0:T(128)S(1)}, s32[32]{0:T(128)S(1)}, s32[32]{0:T(128)S(1)}, s32[32]{0:T(128)S(1)}, s32[32]{0:T(128)S(1)}, /*index=5*/s32[32]{0:T(128)S(1)}) fusion(s32[2,32]{1,0:T(2,128)} %param.11, s32[]{:T(128)S(6)} %select_n.65, s32[]{:T(128)S(6)} %select_n.61, s32[2,32]{1,0:T(2,128)} %param.10), kind=kLoop, calls=%fused_computation.194 | loop fusion | bytes 1288 | tf_op jit(solution)/shard_map/dynamic_slice | solution.py:332
  3.1 1.5 %slice_reduce_fusion.3 = (bf16[4,4,64]{2,1,0:T(4,128)(2,1)S(1)}, bf16[4,4,64]{2,1,0:T(4,128)(2,1)S(1)}) fusion(bf16[4,4,64,256]{3,2,1,0:T(8,128)(2,1)} %bitcast.389), kind=kLoop, calls=%fused_computation.90 | loop fusion | bytes 8192 | tf_op jit(solution)/shard_map/slice | solution.py:312
  4.6 0.6 %pad_maximum_fusion.11.strips = bf16[2,16,64]{2,1,0:T(8,128)(2,1)} fusion(bf16[1,16,64]{2,1,0:T(8,128)(2,1)S(1)} %bitcast.412, bf16[1,16,64]{2,1,0:T(8,128)(2,1)S(1)} %bitcast.411), kind=kLoop, calls=%fused_computation.171 | loop fusion | flops 2048 | bytes 8192 | tf_op jit(solution)/shard_map/stack | solution.py:312
  5.2 1.1 %copy.211 = bf16[4,1,4,64,256]{4,3,0,2,1:T(8,128)(2,1)S(1)} copy(bf16[4,1,4,64,256]{4,3,2,1,0:T(8,128)(2,1)} %param.7) | data formatting | bytes 1048576 | tf_op args[1]
  6.3 11.2 %first_exchange.1 = (bf16[8,2,16,64]{3,2,1,0:T(8,128)(2,1)}, bf16[4,64,256]{2,1,0:T(8,128)(2,1)}, bf16[4,64,256]{2,1,0:T(8,128)(2,1)}, bf16[4,64,256]{2,1,0:T(8,128)(2,1)}, bf16[4,64,256]{2,1,0:T(8,128)(2,1)}) custom-call(bf16[2,16,64]{2,1,0:T(8,128)(2,1)} %pad_maximum_fusion.11.strips, bf16[4,4,64,256]{3,2,1,0:T(8,128)(2,1)} %bitcast.390, ...), custom_call_target="tpu_custom_call" | custom-call | tf_op jit(solution)/shard_map/first_exchange/pallas_call | solution.py:208
  17.5 1.0 %select_bitcast_fusion.4 = (bf16[1,4,64,256]{3,2,0,1:T(8,128)(2,1)S(1)}, bf16[1,4,64,256]{3,2,0,1:T(8,128)(2,1)S(1)}) fusion(bf16[4,64,256]{2,1,0:T(8,128)(2,1)} %get-tuple-element.14, pred[]{:T(512)S(6)} %gt.7, bf16[4,64,256]{2,1,0:T(8,128)(2,1)} %get-tuple-element.13, pred[]{:T(512)S(6)} %lt.19), kind=kLoop, calls=%fused_computation.104 | loop fusion | flops 131072 | bytes 524290 | tf_op jit(solution)/shard_map/broadcast_in_dim | solution.py:350
  18.5 0.8 %fusion.120 = (bf16[8,1,16,64]{3,2,1,0:T(8,128)(2,1)S(1)}, bf16[8,1,16,64]{3,2,1,0:T(8,128)(2,1)S(1)}) fusion(bf16[8,2,16,64]{3,2,1,0:T(8,128)(2,1)} %get-tuple-element.17), kind=kLoop, calls=%fused_computation.208 | loop fusion | bytes 65536 | tf_op jit(solution)/shard_map/slice | solution.py:346
  20.4 0.3 copy-done
  20.8 0.4 convolution_bitcast_fusion.8
  21.2 0.4 convolution_bitcast_fusion.11
  21.6 0.5 convolution_bitcast_fusion.7
  22.0 0.5 convolution_bitcast_fusion.12
  23.1 0.6 %multiply_convert_fusion = (bf16[4,4,64,256]{3,2,1,0:T(8,128)(2,1)S(1)}, f32[4,4,64,256]{3,2,1,0:T(8,128)S(1)}) fusion(f32[4,4,64,256]{3,2,1,0:T(8,128)S(1)} %convolution_bitcast_fusion.7, f32[4,4,64,256]{3,2,1,0:T(8,128)S(1)} %convolution_bitcast_fusion.8, f32[4,4,64,256]{3,2,1,0:T(8,128)S(1)} %convolution_bitcast_fusion.9, ...), kind=kOutput, calls=%fused_computation.57 | convolution fusion | flops 36438016 | bytes 8404992 | tf_op jit(solution)/shard_map/frcx,cd->frdx/dot_general | solution.py:262
  25.3 0.5 fusion.11
  25.9 0.5 slice_reduce_fusion.1
  27.0 0.6 %pad_maximum_fusion.10.strips = bf16[2,24,64]{2,1,0:T(8,128)(2,1)} fusion(bf16[1,24,64]{2,1,0:T(8,128)(2,1)S(1)} %stack.38, bf16[1,24,64]{2,1,0:T(8,128)(2,1)S(1)} %stack.37), kind=kLoop, calls=%fused_computation.166 | loop fusion | flops 3072 | bytes 12288 | tf_op jit(solution)/shard_map/stack | solution.py:308
  27.9 0.3 convolution_bitcast_fusion.25
  28.2 0.3 convolution_bitcast_fusion.22
  28.6 0.4 convolution_bitcast_fusion.24
  29.0 0.4 convolution_bitcast_fusion.23
  31.3 0.3 slice.190
  32.5 0.3 slice.191
  33.1 0.8 %fusion.118 = (bf16[4,6,64,256]{3,2,0,1:T(8,128)(2,1)S(1)}, f32[4,6,64,256]{3,2,0,1:T(8,128)S(1)}) fusion(f32[4,4,64,255]{3,2,0,1:T(8,128)S(1)} %bitcast.405, f32[4,4,64,255]{3,2,0,1:T(8,128)S(1)} %slice.191, f32[4,4,64,256]{3,2,0,1:T(8,128)S(1)} %convolution_bitcast_fusion.2, f32[4,4,64,256]{3,2,0,1:T(8,128)S(1)} %convolution_bitcast_fusion.3, ...), kind=kLoop, calls=%fused_computation.206 | loop fusion | flops 2752512 | bytes 9682944 | tf_op jit(solution)/shard_map/convert.7
  33.9 0.7 %slice_bitcast_fusion = (bf16[4,64,256]{2,1,0:T(8,128)(2,1)}, bf16[4,64,256]{2,1,0:T(8,128)(2,1)}) fusion(bf16[4,6,64,256]{3,2,0,1:T(8,128)(2,1)S(1)} %get-tuple-element.33), kind=kLoop, calls=%fused_computation.98 | loop fusion | bytes 524288 | tf_op jit(solution)/shard_map/convert_element_type | solution.py:356
  34.6 18.5 %last_exchange.1 = (bf16[8,2,24,64]{3,2,1,0:T(8,128)(2,1)}, bf16[4,64,256]{2,1,0:T(8,128)(2,1)}, bf16[4,64,256]{2,1,0:T(8,128)(2,1)}, f32[7,64,64]{2,1,0:T(8,128)}, f32[3,64,64]{2,1,0:T(8,128)}) custom-call(bf16[2,24,64]{2,1,0:T(8,128)(2,1)} %pad_maximum_fusion.10.strips, bf16[4,64,256]{2,1,0:T(8,128)(2,1)} %get-tuple-element.36.up_row, ...), custom_call_target="tpu_custom_call" | custom-call | tf_op jit(solution)/shard_map/last_exchange/pallas_call | solution.py:230
  53.1 0.9 %select_bitcast_fusion.1 = bf16[4,1,64,256]{3,2,0,1:T(8,128)(2,1)S(1)} fusion(bf16[4,64,256]{2,1,0:T(8,128)(2,1)} %get-tuple-element.18, pred[]{:T(512)S(6)} %gt.8), kind=kLoop, calls=%fused_computation.101 | loop fusion | flops 65536 | bytes 262145 | tf_op jit(solution)/shard_map/broadcast_in_dim | solution.py:362
  54.1 0.8 %fusion.119 = (bf16[8,1,24,64]{3,2,1,0:T(8,128)(2,1)S(1)}, bf16[8,1,24,64]{3,2,1,0:T(8,128)(2,1)S(1)}) fusion(bf16[8,2,24,64]{3,2,1,0:T(8,128)(2,1)} %get-tuple-element.20), kind=kLoop, calls=%fused_computation.207 | loop fusion | bytes 98304 | tf_op jit(solution)/shard_map/slice | solution.py:376
  55.5 0.9 %select_bitcast_fusion = bf16[4,1,64,256]{3,2,0,1:T(8,128)(2,1)S(1)} fusion(bf16[4,64,256]{2,1,0:T(8,128)(2,1)} %get-tuple-element.19, pred[]{:T(512)S(6)} %lt.20), kind=kLoop, calls=%fused_computation.100 | loop fusion | flops 65536 | bytes 262145 | tf_op jit(solution)/shard_map/broadcast_in_dim | solution.py:363
  56.4 0.4 fusion.27
  56.8 0.8 %copy.108 = bf16[4,1,4,64,256]{4,3,2,1,0:T(8,128)(2,1)} copy(bf16[4,1,4,64,256]{4,3,0,2,1:T(8,128)(2,1)S(1)} %fusion.27) | data formatting | bytes 1048576
  57.7 0.7 %copy.218 = f32[7,64,64]{2,1,0:T(8,128)} copy(f32[7,64,64]{2,1,0:T(8,128)S(1)} %copy-done.4) | data formatting | bytes 229376
  58.4 0.6 %copy.219 = f32[3,64,64]{2,1,0:T(8,128)} copy(f32[3,64,64]{2,1,0:T(8,128)S(1)} %copy-done.7) | data formatting | bytes 98304
  (81 shorter events, 9.3 us)
Async XLA Ops:
  17.5 2.3 %copy-start.5 = (bf16[4,64,256]{2,1,0:T(8,128)(2,1)S(1)}, bf16[4,64,256]{2,1,0:T(8,128)(2,1)}, u32[]{:S(2)}) copy-start(bf16[4,64,256]{2,1,0:T(8,128)(2,1)} %get-tuple-element.15) | copy-start | bytes 393220
  17.5 2.3 %copy-start.6 = (bf16[4,64,256]{2,1,0:T(8,128)(2,1)S(1)}, bf16[4,64,256]{2,1,0:T(8,128)(2,1)}, u32[]{:S(2)}) copy-start(bf16[4,64,256]{2,1,0:T(8,128)(2,1)} %get-tuple-element.16) | copy-start | bytes 393220
  19.7 1.0 %copy-start = (bf16[4,1,4,64,256]{4,3,2,1,0:T(8,128)(2,1)S(1)}, bf16[4,1,4,64,256]{4,3,2,1,0:T(8,128)(2,1)}, u32[]{:S(2)}) copy-start(bf16[4,1,4,64,256]{4,3,2,1,0:T(8,128)(2,1)} %param.6) | copy-start | bytes 1572868
  19.7 1.1 %copy-start.2 = (bf16[7,64,64]{2,1,0:T(8,128)(2,1)S(1)}, bf16[7,64,64]{2,1,0:T(8,128)(2,1)}, u32[]{:S(2)}) copy-start(bf16[7,64,64]{2,1,0:T(8,128)(2,1)} %param.8) | copy-start | bytes 172036
  23.1 1.0 %copy-start.1 = (bf16[4,1,4,64,256]{4,3,2,1,0:T(8,128)(2,1)S(1)}, bf16[4,1,4,64,256]{4,3,2,1,0:T(8,128)(2,1)}, u32[]{:S(2)}) copy-start(bf16[4,1,4,64,256]{4,3,2,1,0:T(8,128)(2,1)} %param.7) | copy-start | bytes 1572868
  23.8 1.0 %copy-start.8 = (bf16[3,64,64]{2,1,0:T(8,128)(2,1)S(1)}, bf16[3,64,64]{2,1,0:T(8,128)(2,1)}, u32[]{:S(2)}) copy-start(bf16[3,64,64]{2,1,0:T(8,128)(2,1)} %param.9) | copy-start | bytes 73732
  30.4 0.7 %copy-start.3 = (f32[5,8,8,128]{3,2,1,0:T(8,128)}, f32[5,8,8,128]{3,2,1,0:T(8,128)S(1)}, u32[]{:S(2)}) copy-start(f32[5,8,8,128]{3,2,1,0:T(8,128)S(1)} %fusion.49.terms) | copy-start | bytes 491524
  56.4 1.3 %copy-start.4 = (f32[7,64,64]{2,1,0:T(8,128)S(1)}, f32[7,64,64]{2,1,0:T(8,128)}, u32[]{:S(2)}) copy-start(f32[7,64,64]{2,1,0:T(8,128)} %get-tuple-element.70) | copy-start | bytes 344068
  56.4 1.9 %copy-start.7 = (f32[3,64,64]{2,1,0:T(8,128)S(1)}, f32[3,64,64]{2,1,0:T(8,128)}, u32[]{:S(2)}) copy-start(f32[3,64,64]{2,1,0:T(8,128)} %get-tuple-element.71) | copy-start | bytes 147460

commit v6 on v5

--- a/solution.py
+++ b/solution.py
@@ -106,11 +106,11 @@
     meet(False, False)
     rows, frames = field.shape[1], field.shape[0]
     parts = (
-        seam_copies(strips, gathered, seam_send, seam_recv),
-        line_copies("tile", field.at[:, rows - 1], above, field.at[:, 0], below, row_send, row_recv),
         line_copies(
             "tm", cotangent.at[frames - 1], before, cotangent.at[0], after, frame_send, frame_recv
         ),
+        line_copies("tile", field.at[:, rows - 1], above, field.at[:, 0], below, row_send, row_recv),
+        seam_copies(strips, gathered, seam_send, seam_recv),
     )
     for start, _ in parts:
         start()
@@ -145,8 +145,6 @@
         seam_copies(strips, gathered, seam_send, seam_recv),
         line_copies("tile", down_row, above, up_row, below, row_send, row_recv),
     )
-    for start, _ in parts:
-        start()
     total = terms[:, me]
     for step in range(1, tiles):
         other = lax.rem(me + step, tiles)
@@ -164,6 +162,8 @@
         )
         copy.start()
         second.append(copy)
+    for start, _ in parts:
+        start()
     for step in range(1, size):
         other = lax.rem(mine + step, size)
         target = {"tm": other // charts, "diamond": lax.rem(other, charts)}

time: 59.4 us -> 60 us (1.010)
  no operation moved by 1% of the time
where the time goes in v6:
time: 60 us; the launch traced here: 59.6 us
  Pallas kernels  30.4 us (51%)
  local copies, waits for them, and re-layouts  11.6 us (19%)
  matrix products  10.6 us (18%)
  other arithmetic  6.03 us (10%)
  between operations  1.02 us (2%)
    pallas_call x1, Pallas kernels, exchange_end(): pl.pallas_call(last_exchange, out_shape=(jax.ShapeDtypeStruct((tiles,) +...  19.1 us
    pallas_call x1, Pallas kernels, exchange_start(): pl.pallas_call(first_exchange, out_shape=(jax.ShapeDtypeStruct((tiles,) +...  11.3 us
    unnamed x22, local copies, waits for them, and re-layouts  3.82 us
    dot_general x7, matrix products, local_math(): jnp.einsum('frcx,cd->frdx', windows[number], hex_weight[number], preferre...  2.95 us
    dot_general x7, matrix products, local_math(): jnp.einsum('frcx,frdx->cd', window, grad_wide, preferred_element_type=jnp...  2.32 us
    slice x2, local copies, waits for them, and re-layouts, seam_columns(): return jnp.stack([block[..., block.shape[-1] - 1], block[..., 0]])  2 us
    dot_general x7, matrix products, local_math(): jnp.einsum('frdx,cd->frcx', grad_wide, hex_weight[number], preferred_elem...  1.93 us

profile of v6, /device:TPU:1, one launch (start us, length us, event | category | flops | bytes accessed | tf_op | source)
XLA Modules:
  0.0 59.6 jit_solution(17662220894094592640)
XLA Ops:
  0.7 0.8 %fusion.106 = (s32[32]{0:T(128)S(1)}, s32[32]{0:T(128)S(1)}, s32[32]{0:T(128)S(1)}, s32[32]{0:T(128)S(1)}, s32[32]{0:T(128)S(1)}, /*index=5*/s32[32]{0:T(128)S(1)}) fusion(s32[2,32]{1,0:T(2,128)} %param.11, s32[]{:T(128)S(6)} %select_n.65, s32[]{:T(128)S(6)} %select_n.61, s32[2,32]{1,0:T(2,128)} %param.10), kind=kLoop, calls=%fused_computation.194 | loop fusion | bytes 1288 | tf_op jit(solution)/shard_map/dynamic_slice | solution.py:332
  3.1 1.5 %slice_reduce_fusion.3 = (bf16[4,4,64]{2,1,0:T(4,128)(2,1)S(1)}, bf16[4,4,64]{2,1,0:T(4,128)(2,1)S(1)}) fusion(bf16[4,4,64,256]{3,2,1,0:T(8,128)(2,1)} %bitcast.389), kind=kLoop, calls=%fused_computation.90 | loop fusion | bytes 8192 | tf_op jit(solution)/shard_map/slice | solution.py:312
  4.6 0.6 %pad_maximum_fusion.11.strips = bf16[2,16,64]{2,1,0:T(8,128)(2,1)} fusion(bf16[1,16,64]{2,1,0:T(8,128)(2,1)S(1)} %bitcast.412, bf16[1,16,64]{2,1,0:T(8,128)(2,1)S(1)} %bitcast.411), kind=kLoop, calls=%fused_computation.171 | loop fusion | flops 2048 | bytes 8192 | tf_op jit(solution)/shard_map/stack | solution.py:312
  5.2 1.1 %copy.211 = bf16[4,1,4,64,256]{4,3,0,2,1:T(8,128)(2,1)S(1)} copy(bf16[4,1,4,64,256]{4,3,2,1,0:T(8,128)(2,1)} %param.7) | data formatting | bytes 1048576 | tf_op args[1]
  6.3 11.3 %first_exchange.1 = (bf16[8,2,16,64]{3,2,1,0:T(8,128)(2,1)}, bf16[4,64,256]{2,1,0:T(8,128)(2,1)}, bf16[4,64,256]{2,1,0:T(8,128)(2,1)}, bf16[4,64,256]{2,1,0:T(8,128)(2,1)}, bf16[4,64,256]{2,1,0:T(8,128)(2,1)}) custom-call(bf16[2,16,64]{2,1,0:T(8,128)(2,1)} %pad_maximum_fusion.11.strips, bf16[4,4,64,256]{3,2,1,0:T(8,128)(2,1)} %bitcast.390, ...), custom_call_target="tpu_custom_call" | custom-call | tf_op jit(solution)/shard_map/first_exchange/pallas_call | solution.py:208
  17.6 1.0 %select_bitcast_fusion.4 = (bf16[1,4,64,256]{3,2,0,1:T(8,128)(2,1)S(1)}, bf16[1,4,64,256]{3,2,0,1:T(8,128)(2,1)S(1)}) fusion(bf16[4,64,256]{2,1,0:T(8,128)(2,1)} %get-tuple-element.14, pred[]{:T(512)S(6)} %gt.7, bf16[4,64,256]{2,1,0:T(8,128)(2,1)} %get-tuple-element.13, pred[]{:T(512)S(6)} %lt.19), kind=kLoop, calls=%fused_computation.104 | loop fusion | flops 131072 | bytes 524290 | tf_op jit(solution)/shard_map/broadcast_in_dim | solution.py:350
  18.6 0.8 %fusion.120 = (bf16[8,1,16,64]{3,2,1,0:T(8,128)(2,1)S(1)}, bf16[8,1,16,64]{3,2,1,0:T(8,128)(2,1)S(1)}) fusion(bf16[8,2,16,64]{3,2,1,0:T(8,128)(2,1)} %get-tuple-element.17), kind=kLoop, calls=%fused_computation.208 | loop fusion | bytes 65536 | tf_op jit(solution)/shard_map/slice | solution.py:346
  20.4 0.3 copy-done
  20.8 0.4 convolution_bitcast_fusion.8
  21.2 0.4 convolution_bitcast_fusion.11
  21.6 0.5 convolution_bitcast_fusion.7
  22.0 0.5 convolution_bitcast_fusion.12
  23.2 0.6 %multiply_convert_fusion = (bf16[4,4,64,256]{3,2,1,0:T(8,128)(2,1)S(1)}, f32[4,4,64,256]{3,2,1,0:T(8,128)S(1)}) fusion(f32[4,4,64,256]{3,2,1,0:T(8,128)S(1)} %convolution_bitcast_fusion.7, f32[4,4,64,256]{3,2,1,0:T(8,128)S(1)} %convolution_bitcast_fusion.8, f32[4,4,64,256]{3,2,1,0:T(8,128)S(1)} %convolution_bitcast_fusion.9, ...), kind=kOutput, calls=%fused_computation.57 | convolution fusion | flops 36438016 | bytes 8404992 | tf_op jit(solution)/shard_map/frcx,cd->frdx/dot_general | solution.py:262
  25.4 0.5 fusion.11
  25.9 0.5 slice_reduce_fusion.1
  27.0 0.6 %pad_maximum_fusion.10.strips = bf16[2,24,64]{2,1,0:T(8,128)(2,1)} fusion(bf16[1,24,64]{2,1,0:T(8,128)(2,1)S(1)} %stack.38, bf16[1,24,64]{2,1,0:T(8,128)(2,1)S(1)} %stack.37), kind=kLoop, calls=%fused_computation.166 | loop fusion | flops 3072 | bytes 12288 | tf_op jit(solution)/shard_map/stack | solution.py:308
  27.9 0.3 convolution_bitcast_fusion.25
  28.3 0.3 convolution_bitcast_fusion.22
  28.6 0.4 convolution_bitcast_fusion.24
  29.0 0.4 convolution_bitcast_fusion.23
  31.3 0.3 slice.190
  32.5 0.3 slice.191
  33.1 0.8 %fusion.118 = (bf16[4,6,64,256]{3,2,0,1:T(8,128)(2,1)S(1)}, f32[4,6,64,256]{3,2,0,1:T(8,128)S(1)}) fusion(f32[4,4,64,255]{3,2,0,1:T(8,128)S(1)} %bitcast.405, f32[4,4,64,255]{3,2,0,1:T(8,128)S(1)} %slice.191, f32[4,4,64,256]{3,2,0,1:T(8,128)S(1)} %convolution_bitcast_fusion.2, f32[4,4,64,256]{3,2,0,1:T(8,128)S(1)} %convolution_bitcast_fusion.3, ...), kind=kLoop, calls=%fused_computation.206 | loop fusion | flops 2752512 | bytes 9682944 | tf_op jit(solution)/shard_map/convert.7
  33.9 0.7 %slice_bitcast_fusion = (bf16[4,64,256]{2,1,0:T(8,128)(2,1)}, bf16[4,64,256]{2,1,0:T(8,128)(2,1)}) fusion(bf16[4,6,64,256]{3,2,0,1:T(8,128)(2,1)S(1)} %get-tuple-element.33), kind=kLoop, calls=%fused_computation.98 | loop fusion | bytes 524288 | tf_op jit(solution)/shard_map/convert_element_type | solution.py:356
  34.6 19.1 %last_exchange.1 = (bf16[8,2,24,64]{3,2,1,0:T(8,128)(2,1)}, bf16[4,64,256]{2,1,0:T(8,128)(2,1)}, bf16[4,64,256]{2,1,0:T(8,128)(2,1)}, f32[7,64,64]{2,1,0:T(8,128)}, f32[3,64,64]{2,1,0:T(8,128)}) custom-call(bf16[2,24,64]{2,1,0:T(8,128)(2,1)} %pad_maximum_fusion.10.strips, bf16[4,64,256]{2,1,0:T(8,128)(2,1)} %get-tuple-element.36.up_row, ...), custom_call_target="tpu_custom_call" | custom-call | tf_op jit(solution)/shard_map/last_exchange/pallas_call | solution.py:230
  53.8 0.9 %select_bitcast_fusion.1 = bf16[4,1,64,256]{3,2,0,1:T(8,128)(2,1)S(1)} fusion(bf16[4,64,256]{2,1,0:T(8,128)(2,1)} %get-tuple-element.18, pred[]{:T(512)S(6)} %gt.8), kind=kLoop, calls=%fused_computation.101 | loop fusion | flops 65536 | bytes 262145 | tf_op jit(solution)/shard_map/broadcast_in_dim | solution.py:362
  54.7 0.8 %fusion.119 = (bf16[8,1,24,64]{3,2,1,0:T(8,128)(2,1)S(1)}, bf16[8,1,24,64]{3,2,1,0:T(8,128)(2,1)S(1)}) fusion(bf16[8,2,24,64]{3,2,1,0:T(8,128)(2,1)} %get-tuple-element.20), kind=kLoop, calls=%fused_computation.207 | loop fusion | bytes 98304 | tf_op jit(solution)/shard_map/slice | solution.py:376
  56.1 0.9 %select_bitcast_fusion = bf16[4,1,64,256]{3,2,0,1:T(8,128)(2,1)S(1)} fusion(bf16[4,64,256]{2,1,0:T(8,128)(2,1)} %get-tuple-element.19, pred[]{:T(512)S(6)} %lt.20), kind=kLoop, calls=%fused_computation.100 | loop fusion | flops 65536 | bytes 262145 | tf_op jit(solution)/shard_map/broadcast_in_dim | solution.py:363
  57.0 0.4 fusion.27
  57.4 0.8 %copy.108 = bf16[4,1,4,64,256]{4,3,2,1,0:T(8,128)(2,1)} copy(bf16[4,1,4,64,256]{4,3,0,2,1:T(8,128)(2,1)S(1)} %fusion.27) | data formatting | bytes 1048576
  58.3 0.7 %copy.218 = f32[7,64,64]{2,1,0:T(8,128)} copy(f32[7,64,64]{2,1,0:T(8,128)S(1)} %copy-done.4) | data formatting | bytes 229376
  59.0 0.6 %copy.219 = f32[3,64,64]{2,1,0:T(8,128)} copy(f32[3,64,64]{2,1,0:T(8,128)S(1)} %copy-done.7) | data formatting | bytes 98304
  (81 shorter events, 9.3 us)
Async XLA Ops:
  17.5 2.3 %copy-start.5 = (bf16[4,64,256]{2,1,0:T(8,128)(2,1)S(1)}, bf16[4,64,256]{2,1,0:T(8,128)(2,1)}, u32[]{:S(2)}) copy-start(bf16[4,64,256]{2,1,0:T(8,128)(2,1)} %get-tuple-element.15) | copy-start | bytes 393220
  17.5 2.3 %copy-start.6 = (bf16[4,64,256]{2,1,0:T(8,128)(2,1)S(1)}, bf16[4,64,256]{2,1,0:T(8,128)(2,1)}, u32[]{:S(2)}) copy-start(bf16[4,64,256]{2,1,0:T(8,128)(2,1)} %get-tuple-element.16) | copy-start | bytes 393220
  19.7 1.0 %copy-start = (bf16[4,1,4,64,256]{4,3,2,1,0:T(8,128)(2,1)S(1)}, bf16[4,1,4,64,256]{4,3,2,1,0:T(8,128)(2,1)}, u32[]{:S(2)}) copy-start(bf16[4,1,4,64,256]{4,3,2,1,0:T(8,128)(2,1)} %param.6) | copy-start | bytes 1572868
  19.7 1.1 %copy-start.2 = (bf16[7,64,64]{2,1,0:T(8,128)(2,1)S(1)}, bf16[7,64,64]{2,1,0:T(8,128)(2,1)}, u32[]{:S(2)}) copy-start(bf16[7,64,64]{2,1,0:T(8,128)(2,1)} %param.8) | copy-start | bytes 172036
  23.1 1.0 %copy-start.1 = (bf16[4,1,4,64,256]{4,3,2,1,0:T(8,128)(2,1)S(1)}, bf16[4,1,4,64,256]{4,3,2,1,0:T(8,128)(2,1)}, u32[]{:S(2)}) copy-start(bf16[4,1,4,64,256]{4,3,2,1,0:T(8,128)(2,1)} %param.7) | copy-start | bytes 1572868
  23.8 1.0 %copy-start.8 = (bf16[3,64,64]{2,1,0:T(8,128)(2,1)S(1)}, bf16[3,64,64]{2,1,0:T(8,128)(2,1)}, u32[]{:S(2)}) copy-start(bf16[3,64,64]{2,1,0:T(8,128)(2,1)} %param.9) | copy-start | bytes 73732
  30.4 0.7 %copy-start.3 = (f32[5,8,8,128]{3,2,1,0:T(8,128)}, f32[5,8,8,128]{3,2,1,0:T(8,128)S(1)}, u32[]{:S(2)}) copy-start(f32[5,8,8,128]{3,2,1,0:T(8,128)S(1)} %fusion.49.terms) | copy-start | bytes 491524
  57.0 1.3 %copy-start.4 = (f32[7,64,64]{2,1,0:T(8,128)S(1)}, f32[7,64,64]{2,1,0:T(8,128)}, u32[]{:S(2)}) copy-start(f32[7,64,64]{2,1,0:T(8,128)} %get-tuple-element.70) | copy-start | bytes 344068
  57.0 1.9 %copy-start.7 = (f32[3,64,64]{2,1,0:T(8,128)S(1)}, f32[3,64,64]{2,1,0:T(8,128)}, u32[]{:S(2)}) copy-start(f32[3,64,64]{2,1,0:T(8,128)} %get-tuple-element.71) | copy-start | bytes 147460

commit v7 on v5

--- a/solution.py
+++ b/solution.py
@@ -210,8 +210,8 @@
         out_shape=(
             jax.ShapeDtypeStruct((tiles,) + strips.shape, kind), line, line, frame, frame,
         ),
-        in_specs=[ANY] * 3,
-        out_specs=(ANY,) * 5,
+        in_specs=[VMEM, ANY, ANY],
+        out_specs=(VMEM,) * 5,
         scratch_shapes=[
             dma((2, tiles)), dma((2, tiles)), dma((2,)), dma((2,)), dma((2,)), dma((2,)),
         ],
@@ -234,8 +234,8 @@
             jax.ShapeDtypeStruct((7, channels, channels), terms.dtype),
             jax.ShapeDtypeStruct((3, channels, channels), terms.dtype),
         ),
-        in_specs=[ANY, ANY, ANY, VMEM],
-        out_specs=(ANY, ANY, ANY, VMEM, VMEM),
+        in_specs=[VMEM] * 4,
+        out_specs=(VMEM,) * 5,
         scratch_shapes=[
             dma((2, tiles)), dma((2, tiles)), dma((2,)), dma((2,)),
             pltpu.VMEM((tiles,) + chunk, terms.dtype),

time: 59.4 us -> 60.7 us (1.022)
  Pallas kernels: 29.8 us -> 31 us
    pallas_call x1, Pallas kernels: 11.2 us -> 12.6 us  [exchange_start(): pl.pallas_call(first_exchange, out_shape=(jax.ShapeDtypeStruct((tiles,) +...]
where the time goes in v7:
time: 60.7 us; the launch traced here: 60.3 us
  Pallas kernels  31 us (51%)
  local copies, waits for them, and re-layouts  11.6 us (19%)
  matrix products  10.6 us (17%)
  other arithmetic  6.03 us (10%)
  between operations  1.02 us (2%)
    pallas_call x1, Pallas kernels, exchange_end(): pl.pallas_call(last_exchange, out_shape=(jax.ShapeDtypeStruct((tiles,) +...  18.4 us
    pallas_call x1, Pallas kernels, exchange_start(): pl.pallas_call(first_exchange, out_shape=(jax.ShapeDtypeStruct((tiles,) +...  12.6 us
    unnamed x22, local copies, waits for them, and re-layouts  3.82 us
    dot_general x7, matrix products, local_math(): jnp.einsum('frcx,cd->frdx', windows[number], hex_weight[number], preferre...  2.95 us
    dot_general x7, matrix products, local_math(): jnp.einsum('frcx,frdx->cd', window, grad_wide, preferred_element_type=jnp...  2.32 us
    slice x2, local copies, waits for them, and re-layouts, seam_columns(): return jnp.stack([block[..., block.shape[-1] - 1], block[..., 0]])  2 us
    dot_general x7, matrix products, local_math(): jnp.einsum('frdx,cd->frcx', grad_wide, hex_weight[number], preferred_elem...  1.93 us

profile of v7, /device:TPU:1, one launch (start us, length us, event | category | flops | bytes accessed | tf_op | source)
XLA Modules:
  0.0 60.3 jit_solution(12259809240728124719)
XLA Ops:
  0.7 0.8 %fusion.106 = (s32[32]{0:T(128)S(1)}, s32[32]{0:T(128)S(1)}, s32[32]{0:T(128)S(1)}, s32[32]{0:T(128)S(1)}, s32[32]{0:T(128)S(1)}, /*index=5*/s32[32]{0:T(128)S(1)}) fusion(s32[2,32]{1,0:T(2,128)} %param.11, s32[]{:T(128)S(6)} %select_n.65, s32[]{:T(128)S(6)} %select_n.61, s32[2,32]{1,0:T(2,128)} %param.10), kind=kLoop, calls=%fused_computation.194 | loop fusion | bytes 1288 | tf_op jit(solution)/shard_map/dynamic_slice | solution.py:332
  3.1 1.5 %slice_reduce_fusion.3 = (bf16[4,4,64]{2,1,0:T(4,128)(2,1)S(1)}, bf16[4,4,64]{2,1,0:T(4,128)(2,1)S(1)}) fusion(bf16[4,4,64,256]{3,2,1,0:T(8,128)(2,1)} %bitcast.389), kind=kLoop, calls=%fused_computation.90 | loop fusion | bytes 8192 | tf_op jit(solution)/shard_map/slice | solution.py:312
  4.6 0.6 %pad_maximum_fusion.11.strips = bf16[2,16,64]{2,1,0:T(8,128)(2,1)} fusion(bf16[1,16,64]{2,1,0:T(8,128)(2,1)S(1)} %bitcast.412, bf16[1,16,64]{2,1,0:T(8,128)(2,1)S(1)} %bitcast.411), kind=kLoop, calls=%fused_computation.171 | loop fusion | flops 2048 | bytes 8192 | tf_op jit(solution)/shard_map/stack | solution.py:312
  5.2 1.1 %copy.211 = bf16[4,1,4,64,256]{4,3,0,2,1:T(8,128)(2,1)S(1)} copy(bf16[4,1,4,64,256]{4,3,2,1,0:T(8,128)(2,1)} %param.7) | data formatting | bytes 1048576 | tf_op args[1]
  6.3 12.6 %first_exchange.1 = (bf16[8,2,16,64]{3,2,1,0:T(8,128)(2,1)}, bf16[4,64,256]{2,1,0:T(8,128)(2,1)}, bf16[4,64,256]{2,1,0:T(8,128)(2,1)}, bf16[4,64,256]{2,1,0:T(8,128)(2,1)}, bf16[4,64,256]{2,1,0:T(8,128)(2,1)}) custom-call(bf16[2,16,64]{2,1,0:T(8,128)(2,1)} %pad_maximum_fusion.11.strips, bf16[4,4,64,256]{3,2,1,0:T(8,128)(2,1)} %bitcast.390, ...), custom_call_target="tpu_custom_call" | custom-call | tf_op jit(solution)/shard_map/first_exchange/pallas_call | solution.py:208
  18.9 1.0 %select_bitcast_fusion.4 = (bf16[1,4,64,256]{3,2,0,1:T(8,128)(2,1)S(1)}, bf16[1,4,64,256]{3,2,0,1:T(8,128)(2,1)S(1)}) fusion(bf16[4,64,256]{2,1,0:T(8,128)(2,1)} %get-tuple-element.14, pred[]{:T(512)S(6)} %gt.7, bf16[4,64,256]{2,1,0:T(8,128)(2,1)} %get-tuple-element.13, pred[]{:T(512)S(6)} %lt.19), kind=kLoop, calls=%fused_computation.104 | loop fusion | flops 131072 | bytes 524290 | tf_op jit(solution)/shard_map/broadcast_in_dim | solution.py:350
  19.9 0.8 %fusion.120 = (bf16[8,1,16,64]{3,2,1,0:T(8,128)(2,1)S(1)}, bf16[8,1,16,64]{3,2,1,0:T(8,128)(2,1)S(1)}) fusion(bf16[8,2,16,64]{3,2,1,0:T(8,128)(2,1)} %get-tuple-element.17), kind=kLoop, calls=%fused_computation.208 | loop fusion | bytes 65536 | tf_op jit(solution)/shard_map/slice | solution.py:346
  21.8 0.3 copy-done
  22.1 0.4 convolution_bitcast_fusion.8
  22.5 0.4 convolution_bitcast_fusion.11
  22.9 0.5 convolution_bitcast_fusion.7
  23.4 0.5 convolution_bitcast_fusion.12
  24.5 0.6 %multiply_convert_fusion = (bf16[4,4,64,256]{3,2,1,0:T(8,128)(2,1)S(1)}, f32[4,4,64,256]{3,2,1,0:T(8,128)S(1)}) fusion(f32[4,4,64,256]{3,2,1,0:T(8,128)S(1)} %convolution_bitcast_fusion.7, f32[4,4,64,256]{3,2,1,0:T(8,128)S(1)} %convolution_bitcast_fusion.8, f32[4,4,64,256]{3,2,1,0:T(8,128)S(1)} %convolution_bitcast_fusion.9, ...), kind=kOutput, calls=%fused_computation.57 | convolution fusion | flops 36438016 | bytes 8404992 | tf_op jit(solution)/shard_map/frcx,cd->frdx/dot_general | solution.py:262
  26.7 0.5 fusion.11
  27.2 0.5 slice_reduce_fusion.1
  28.4 0.6 %pad_maximum_fusion.10.strips = bf16[2,24,64]{2,1,0:T(8,128)(2,1)} fusion(bf16[1,24,64]{2,1,0:T(8,128)(2,1)S(1)} %stack.38, bf16[1,24,64]{2,1,0:T(8,128)(2,1)S(1)} %stack.37), kind=kLoop, calls=%fused_computation.166 | loop fusion | flops 3072 | bytes 12288 | tf_op jit(solution)/shard_map/stack | solution.py:308
  29.2 0.3 convolution_bitcast_fusion.25
  29.6 0.3 convolution_bitcast_fusion.22
  30.0 0.4 convolution_bitcast_fusion.24
  30.4 0.4 convolution_bitcast_fusion.23
  32.7 0.3 slice.190
  33.9 0.3 slice.191
  34.5 0.8 %fusion.118 = (bf16[4,6,64,256]{3,2,0,1:T(8,128)(2,1)S(1)}, f32[4,6,64,256]{3,2,0,1:T(8,128)S(1)}) fusion(f32[4,4,64,255]{3,2,0,1:T(8,128)S(1)} %bitcast.405, f32[4,4,64,255]{3,2,0,1:T(8,128)S(1)} %slice.191, f32[4,4,64,256]{3,2,0,1:T(8,128)S(1)} %convolution_bitcast_fusion.2, f32[4,4,64,256]{3,2,0,1:T(8,128)S(1)} %convolution_bitcast_fusion.3, ...), kind=kLoop, calls=%fused_computation.206 | loop fusion | flops 2752512 | bytes 9682944 | tf_op jit(solution)/shard_map/convert.7
  35.3 0.7 %slice_bitcast_fusion = (bf16[4,64,256]{2,1,0:T(8,128)(2,1)}, bf16[4,64,256]{2,1,0:T(8,128)(2,1)}) fusion(bf16[4,6,64,256]{3,2,0,1:T(8,128)(2,1)S(1)} %get-tuple-element.33), kind=kLoop, calls=%fused_computation.98 | loop fusion | bytes 524288 | tf_op jit(solution)/shard_map/convert_element_type | solution.py:356
  36.0 18.4 %last_exchange.1 = (bf16[8,2,24,64]{3,2,1,0:T(8,128)(2,1)}, bf16[4,64,256]{2,1,0:T(8,128)(2,1)}, bf16[4,64,256]{2,1,0:T(8,128)(2,1)}, f32[7,64,64]{2,1,0:T(8,128)}, f32[3,64,64]{2,1,0:T(8,128)}) custom-call(bf16[2,24,64]{2,1,0:T(8,128)(2,1)} %pad_maximum_fusion.10.strips, bf16[4,64,256]{2,1,0:T(8,128)(2,1)} %get-tuple-element.36.up_row, ...), custom_call_target="tpu_custom_call" | custom-call | tf_op jit(solution)/shard_map/last_exchange/pallas_call | solution.py:230
  54.4 0.9 %select_bitcast_fusion.1 = bf16[4,1,64,256]{3,2,0,1:T(8,128)(2,1)S(1)} fusion(bf16[4,64,256]{2,1,0:T(8,128)(2,1)} %get-tuple-element.18, pred[]{:T(512)S(6)} %gt.8), kind=kLoop, calls=%fused_computation.101 | loop fusion | flops 65536 | bytes 262145 | tf_op jit(solution)/shard_map/broadcast_in_dim | solution.py:362
  55.3 0.8 %fusion.119 = (bf16[8,1,24,64]{3,2,1,0:T(8,128)(2,1)S(1)}, bf16[8,1,24,64]{3,2,1,0:T(8,128)(2,1)S(1)}) fusion(bf16[8,2,24,64]{3,2,1,0:T(8,128)(2,1)} %get-tuple-element.20), kind=kLoop, calls=%fused_computation.207 | loop fusion | bytes 98304 | tf_op jit(solution)/shard_map/slice | solution.py:376
  56.7 0.9 %select_bitcast_fusion = bf16[4,1,64,256]{3,2,0,1:T(8,128)(2,1)S(1)} fusion(bf16[4,64,256]{2,1,0:T(8,128)(2,1)} %get-tuple-element.19, pred[]{:T(512)S(6)} %lt.20), kind=kLoop, calls=%fused_computation.100 | loop fusion | flops 65536 | bytes 262145 | tf_op jit(solution)/shard_map/broadcast_in_dim | solution.py:363
  57.7 0.4 fusion.27
  58.1 0.8 %copy.108 = bf16[4,1,4,64,256]{4,3,2,1,0:T(8,128)(2,1)} copy(bf16[4,1,4,64,256]{4,3,0,2,1:T(8,128)(2,1)S(1)} %fusion.27) | data formatting | bytes 1048576
  58.9 0.7 %copy.218 = f32[7,64,64]{2,1,0:T(8,128)} copy(f32[7,64,64]{2,1,0:T(8,128)S(1)} %copy-done.4) | data formatting | bytes 229376
  59.6 0.6 %copy.219 = f32[3,64,64]{2,1,0:T(8,128)} copy(f32[3,64,64]{2,1,0:T(8,128)S(1)} %copy-done.7) | data formatting | bytes 98304
  (81 shorter events, 9.3 us)
Async XLA Ops:
  18.9 2.3 %copy-start.5 = (bf16[4,64,256]{2,1,0:T(8,128)(2,1)S(1)}, bf16[4,64,256]{2,1,0:T(8,128)(2,1)}, u32[]{:S(2)}) copy-start(bf16[4,64,256]{2,1,0:T(8,128)(2,1)} %get-tuple-element.15) | copy-start | bytes 393220
  18.9 2.3 %copy-start.6 = (bf16[4,64,256]{2,1,0:T(8,128)(2,1)S(1)}, bf16[4,64,256]{2,1,0:T(8,128)(2,1)}, u32[]{:S(2)}) copy-start(bf16[4,64,256]{2,1,0:T(8,128)(2,1)} %get-tuple-element.16) | copy-start | bytes 393220
  21.1 1.0 %copy-start = (bf16[4,1,4,64,256]{4,3,2,1,0:T(8,128)(2,1)S(1)}, bf16[4,1,4,64,256]{4,3,2,1,0:T(8,128)(2,1)}, u32[]{:S(2)}) copy-start(bf16[4,1,4,64,256]{4,3,2,1,0:T(8,128)(2,1)} %param.6) | copy-start | bytes 1572868
  21.1 1.1 %copy-start.2 = (bf16[7,64,64]{2,1,0:T(8,128)(2,1)S(1)}, bf16[7,64,64]{2,1,0:T(8,128)(2,1)}, u32[]{:S(2)}) copy-start(bf16[7,64,64]{2,1,0:T(8,128)(2,1)} %param.8) | copy-start | bytes 172036
  24.5 1.0 %copy-start.1 = (bf16[4,1,4,64,256]{4,3,2,1,0:T(8,128)(2,1)S(1)}, bf16[4,1,4,64,256]{4,3,2,1,0:T(8,128)(2,1)}, u32[]{:S(2)}) copy-start(bf16[4,1,4,64,256]{4,3,2,1,0:T(8,128)(2,1)} %param.7) | copy-start | bytes 1572868
  25.1 1.0 %copy-start.8 = (bf16[3,64,64]{2,1,0:T(8,128)(2,1)S(1)}, bf16[3,64,64]{2,1,0:T(8,128)(2,1)}, u32[]{:S(2)}) copy-start(bf16[3,64,64]{2,1,0:T(8,128)(2,1)} %param.9) | copy-start | bytes 73732
  31.7 0.7 %copy-start.3 = (f32[5,8,8,128]{3,2,1,0:T(8,128)}, f32[5,8,8,128]{3,2,1,0:T(8,128)S(1)}, u32[]{:S(2)}) copy-start(f32[5,8,8,128]{3,2,1,0:T(8,128)S(1)} %fusion.49.terms) | copy-start | bytes 491524
  57.7 1.3 %copy-start.4 = (f32[7,64,64]{2,1,0:T(8,128)S(1)}, f32[7,64,64]{2,1,0:T(8,128)}, u32[]{:S(2)}) copy-start(f32[7,64,64]{2,1,0:T(8,128)} %get-tuple-element.70) | copy-start | bytes 344068
  57.7 1.9 %copy-start.7 = (f32[3,64,64]{2,1,0:T(8,128)S(1)}, f32[3,64,64]{2,1,0:T(8,128)}, u32[]{:S(2)}) copy-start(f32[3,64,64]{2,1,0:T(8,128)} %get-tuple-element.71) | copy-start | bytes 147460

commit v8 on v4

--- a/solution.py
+++ b/solution.py
@@ -2,7 +2,6 @@
 import jax.numpy as jnp
 from jax import lax
 from jax.experimental import pallas as pl
-from jax.experimental.layout import Layout, with_layout_constraint
 from jax.experimental.pallas import tpu as pltpu
 from jax.sharding import PartitionSpec as P
 
@@ -255,8 +254,6 @@
 
 
 def local_math(padded, framed, hex_weight, time_weight, frames, tile_rows, channels, columns):
-    row_major = Layout(major_to_minor=(0, 1, 2, 3))
-    padded = with_layout_constraint(padded, row_major)
     hidden = jnp.zeros((frames, tile_rows, channels, columns), jnp.float32)
     windows = [
         padded[:, 1 + a : 1 + a + tile_rows, :, 1 + b : 1 + b + columns] for a, b in OFFSETS
@@ -278,7 +275,6 @@
             jnp.einsum("frcx,frdx->cd", active, shifted, preferred_element_type=jnp.float32)
         )
     grad_wide = (grad_act * silu_slope(hidden)).astype(jnp.bfloat16)
-    grad_wide = with_layout_constraint(grad_wide, row_major)
     hex_terms = [
         jnp.einsum("frcx,frdx->cd", window, grad_wide, preferred_element_type=jnp.float32)
         for window in windows
@@ -324,8 +320,7 @@
 
 def shards(activations, upstream, hex_weight, time_weight, left_map, right_map):
     field = activations[:, 0]
-    row_major = Layout(major_to_minor=(0, 1, 2, 3))
-    cotangent = with_layout_constraint(upstream[:, 0], row_major)
+    cotangent = upstream[:, 0]
     frames, tile_rows, channels, columns = field.shape
     chart, charts = lax.axis_index("diamond"), lax.axis_size("diamond")
     tile, tiles = lax.axis_index("tile"), lax.axis_size("tile")
@@ -391,8 +386,7 @@
     column = jnp.arange(columns)
     total = total + jnp.where(column == 0, into_first[..., None], 0.0)
     total = total + jnp.where(column == columns - 1, into_last[..., None], 0.0)
-    total = with_layout_constraint(total.astype(jnp.bfloat16), row_major)
-    return total[:, None], grad_hex, grad_time
+    return total.astype(jnp.bfloat16)[:, None], grad_hex, grad_time
 
 
 def solution(mesh):

time: 70.4 us -> 67.8 us (0.963)
  matrix products: 14.4 us -> 12.4 us
  other arithmetic: 8.02 us -> 6.35 us
    slice x1, local copies, waits for them, and re-layouts: 1.43 us -> 0.01 us  [shards(): into_last = landing(gathered[:, 1], left_map, lax.rem(chart + 1, charts))]
    dynamic_slice x1, local copies, waits for them, and re-layouts: 0.78 us -> 1.91 us  [chart_rows(): own = lax.dynamic_slice(table, (number, 0), (1, table.shape[1]))[0]]
    unnamed x32 -> x44, local copies, waits for them, and re-layouts: 6.84 us -> 7.83 us
    broadcast_in_dim x1, other arithmetic: 0.93 us -> 0.02 us  [shards(): framed = jnp.concatenate([before[None], cotangent, after[None]], axis=0)]
    dot_general x2, matrix products: 1.32 us -> 0.52 us  [landing(): jnp.einsum('rtw,tfwc->frc', pick, strip, preferred_element_type=jnp.float32)]
    dot_general x3, matrix products: 1.78 us -> 1.04 us  [local_math(): jnp.einsum('frdx,cd->frcx', shifted, time_weight[number], preferred_eleme...]
where the time goes in v8:
time: 67.8 us; the launch traced here: 67.2 us
  Pallas kernels  29.9 us (44%)
  local copies, waits for them, and re-layouts  17.4 us (26%)
  matrix products  12.4 us (18%)
  other arithmetic  6.35 us (9%)
  between operations  1.11 us (2%)
    pallas_call x1, Pallas kernels, exchange_end(): pl.pallas_call(last_exchange, out_shape=(jax.ShapeDtypeStruct((tiles,) +...  18.7 us
    pallas_call x1, Pallas kernels, exchange_start(): pl.pallas_call(first_exchange, out_shape=(jax.ShapeDtypeStruct((tiles,) +...  11.2 us
    unnamed x44, local copies, waits for them, and re-layouts  7.83 us
    dot_general x7, matrix products, local_math(): jnp.einsum('frcx,cd->frdx', windows[number], hex_weight[number], preferre...  4.09 us
    dot_general x7, matrix products, local_math(): jnp.einsum('frdx,cd->frcx', grad_wide, hex_weight[number], preferred_elem...  2.7 us
    dot_general x7, matrix products, local_math(): jnp.einsum('frcx,frdx->cd', window, grad_wide, preferred_element_type=jnp...  2.33 us
    slice x2, local copies, waits for them, and re-layouts, seam_columns(): return jnp.stack([block[..., block.shape[-1] - 1], block[..., 0]])  1.99 us
    dynamic_slice x1, local copies, waits for them, and re-layouts, chart_rows(): own = lax.dynamic_slice(table, (number, 0), (1, table.shape[1]))[0]  1.91 us

profile of v8, /device:TPU:1, one launch (start us, length us, event | category | flops | bytes accessed | tf_op | source)
XLA Modules:
  0.0 67.2 jit_solution(10736855405175851996)
XLA Ops:
  0.6 1.9 %fusion.117 = (s32[32]{0:T(128)}, s32[32]{0:T(128)}, s32[32]{0:T(128)S(1)}, s32[32]{0:T(128)S(1)}, s32[32]{0:T(128)}, /*index=5*/s32[32]{0:T(128)}) fusion(s32[2,32]{1,0:T(2,128)} %param.11, s32[]{:T(128)S(6)} %select_n.64, s32[]{:T(128)S(6)} %select_n.60, s32[2,32]{1,0:T(2,128)} %param.10), kind=kLoop, calls=%fused_computation.202 | loop fusion | bytes 1288 | tf_op jit(solution)/shard_map/dynamic_slice | solution.py:338
  2.9 1.5 %slice_reduce_fusion.3 = (bf16[4,4,64]{2,1,0:T(4,128)(2,1)S(1)}, bf16[4,4,64]{2,1,0:T(4,128)(2,1)S(1)}) fusion(bf16[4,4,64,256]{3,2,1,0:T(8,128)(2,1)} %bitcast.409), kind=kLoop, calls=%fused_computation.98 | loop fusion | bytes 8192 | tf_op jit(solution)/shard_map/slice | solution.py:318
  4.4 0.6 pad_maximum_fusion.11.strips
  5.0 11.2 %first_exchange.1 = (bf16[8,2,16,64]{3,2,1,0:T(8,128)(2,1)}, bf16[4,64,256]{2,1,0:T(8,128)(2,1)}, bf16[4,64,256]{2,1,0:T(8,128)(2,1)}, bf16[4,64,256]{2,1,0:T(8,128)(2,1)}, bf16[4,64,256]{2,1,0:T(8,128)(2,1)}) custom-call(bf16[2,16,64]{2,1,0:T(8,128)(2,1)} %pad_maximum_fusion.11.strips, bf16[4,4,64,256]{3,2,1,0:T(8,128)(2,1)} %bitcast.410, ...), custom_call_target="tpu_custom_call" | custom-call | tf_op jit(solution)/shard_map/first_exchange/pallas_call | solution.py:208
  16.2 0.8 %fusion.130 = (bf16[8,1,16,64]{3,2,1,0:T(8,128)(2,1)S(1)}, bf16[8,1,16,64]{3,2,1,0:T(8,128)(2,1)S(1)}) fusion(bf16[8,2,16,64]{3,2,1,0:T(8,128)(2,1)} %get-tuple-element.17), kind=kLoop, calls=%fused_computation.215 | loop fusion | bytes 65536 | tf_op jit(solution)/shard_map/slice | solution.py:352
  17.5 1.0 %select_bitcast_fusion = (bf16[4,1,64,256]{3,2,1,0:T(8,128)(2,1)S(1)}, bf16[4,1,64,256]{3,2,1,0:T(8,128)(2,1)S(1)}) fusion(bf16[4,64,256]{2,1,0:T(8,128)(2,1)} %get-tuple-element.16, pred[]{:T(512)S(6)} %lt.20, bf16[4,64,256]{2,1,0:T(8,128)(2,1)} %get-tuple-element.15, pred[]{:T(512)S(6)} %gt.8), kind=kLoop, calls=%fused_computation.108 | loop fusion | flops 131072 | bytes 524290 | tf_op jit(solution)/shard_map/broadcast_in_dim | solution.py:354
  18.5 0.4 convolution_bitcast_fusion.11
  19.5 0.5 convolution_bitcast_fusion.12
  20.3 0.5 convolution_bitcast_fusion.7
  21.8 1.8 %multiply_convert_fusion = (bf16[4,4,64,256]{3,2,1,0:T(8,128)(2,1)}, f32[4,4,64,256]{3,2,1,0:T(8,128)}) fusion(f32[4,4,64,256]{3,2,1,0:T(8,128)S(1)} %convolution_bitcast_fusion.7, f32[4,4,64,256]{3,2,1,0:T(8,128)S(1)} %convolution_bitcast_fusion.8, f32[4,4,64,256]{3,2,1,0:T(8,128)S(1)} %convolution_bitcast_fusion.9, ...), kind=kOutput, calls=%fused_computation.58 | convolution fusion | flops 36438016 | bytes 8404992 | tf_op jit(solution)/shard_map/frcx,cd->frdx/dot_general | solution.py:262
  23.8 0.7 %copy-done.15 = bf16[3,64,64]{2,1,0:T(8,128)(2,1)S(1)} copy-done((bf16[3,64,64]{2,1,0:T(8,128)(2,1)S(1)}, bf16[3,64,64]{2,1,0:T(8,128)(2,1)}, u32[]{:S(2)}) %copy-start.15) | copy-done | bytes 24600
  25.0 0.9 %copy-done.8 = f32[4,4,64,256]{3,2,1,0:T(8,128)S(1)} copy-done((f32[4,4,64,256]{3,2,1,0:T(8,128)S(1)}, f32[4,4,64,256]{3,2,1,0:T(8,128)}, u32[]{:S(2)}) %copy-start.8) | copy-done | bytes 1048600
  26.0 0.5 fusion.21
  27.2 0.6 copy-done.6
  27.8 0.4 convolution_bitcast_fusion.23
  28.2 0.4 convolution_bitcast_fusion.24
  29.1 0.7 %copy-done.7 = bf16[4,4,64,256]{3,2,1,0:T(8,128)(2,1)S(1)} copy-done((bf16[4,4,64,256]{3,2,1,0:T(8,128)(2,1)S(1)}, bf16[4,4,64,256]{3,2,1,0:T(8,128)(2,1)}, u32[]{:S(2)}) %copy-start.7) | copy-done | bytes 524312
  32.4 1.0 %copy-done.3 = f32[4,4,64,256]{3,2,0,1:T(8,128)} copy-done((f32[4,4,64,256]{3,2,0,1:T(8,128)}, f32[4,4,64,256]{3,2,0,1:T(8,128)S(1)}, u32[]{:S(2)}) %copy-start.3) | copy-done | bytes 1048600
  33.4 0.7 %fusion.55.down_row = bf16[4,64,256]{2,1,0:T(8,128)(2,1)} fusion(f32[4,4,64,255]{3,2,0,1:T(8,128)S(1)} %slice.211, f32[4,4,64,256]{3,2,0,1:T(8,128)S(1)} %convolution_bitcast_fusion.3), kind=kLoop, calls=%fused_computation.107 | loop fusion | flops 131072 | bytes 1437696 | tf_op jit(solution)/shard_map/convert_element_type | solution.py:298
  34.6 1.0 %copy-done.4 = f32[4,4,64,256]{3,2,0,1:T(8,128)} copy-done((f32[4,4,64,256]{3,2,0,1:T(8,128)}, f32[4,4,64,256]{3,2,0,1:T(8,128)S(1)}, u32[]{:S(2)}) %copy-start.4) | copy-done | bytes 1048600
  35.6 0.8 %fusion.54.up_row = bf16[4,64,256]{2,1,0:T(8,128)(2,1)} fusion(f32[4,4,64,255]{3,2,0,1:T(8,128)S(1)} %bitcast.423, f32[4,4,64,256]{3,2,0,1:T(8,128)S(1)} %convolution_bitcast_fusion.2), kind=kLoop, calls=%fused_computation.106 | loop fusion | flops 131072 | bytes 1437696 | tf_op jit(solution)/shard_map/convert_element_type | solution.py:298
  36.4 0.5 slice_reduce_fusion.1
  37.5 0.6 pad_maximum_fusion.10.strips
  38.1 18.7 %last_exchange.1 = (bf16[8,2,24,64]{3,2,1,0:T(8,128)(2,1)}, bf16[4,64,256]{2,1,0:T(8,128)(2,1)}, bf16[4,64,256]{2,1,0:T(8,128)(2,1)}, f32[7,64,64]{2,1,0:T(8,128)}, f32[3,64,64]{2,1,0:T(8,128)}) custom-call(bf16[2,24,64]{2,1,0:T(8,128)(2,1)} %pad_maximum_fusion.10.strips, bf16[4,64,256]{2,1,0:T(8,128)(2,1)} %fusion.54.up_row, ...), custom_call_target="tpu_custom_call" | custom-call | tf_op jit(solution)/shard_map/last_exchange/pallas_call | solution.py:230
  56.8 0.8 %fusion.129 = (bf16[8,1,24,64]{3,2,1,0:T(8,128)(2,1)S(1)}, bf16[8,1,24,64]{3,2,1,0:T(8,128)(2,1)S(1)}) fusion(bf16[8,2,24,64]{3,2,1,0:T(8,128)(2,1)} %get-tuple-element.20), kind=kLoop, calls=%fused_computation.214 | loop fusion | bytes 98304 | tf_op jit(solution)/shard_map/slice | solution.py:384
  58.5 0.9 %convert_element_type.83 = f32[4,64,256]{2,1,0:T(8,128)S(1)} convert(bf16[4,64,256]{2,1,0:T(8,128)(2,1)} %get-tuple-element.18) | non-fusion elementwise | flops 65536 | bytes 393216 | tf_op jit(solution)/shard_map/convert_element_type | solution.py:367
  59.5 0.9 %convert_element_type.84 = f32[4,64,256]{2,1,0:T(8,128)S(1)} convert(bf16[4,64,256]{2,1,0:T(8,128)(2,1)} %get-tuple-element.19) | non-fusion elementwise | flops 65536 | bytes 393216 | tf_op jit(solution)/shard_map/convert_element_type | solution.py:370
  62.6 0.8 %slice-done.1 = f32[4,3,64,256]{3,2,0,1:T(8,128)S(1)} async-done(((f32[4,4,64,256]{3,2,0,1:T(8,128)}), f32[4,3,64,256]{3,2,0,1:T(8,128)S(1)}, s32[]{:S(2)}) %slice-start.1) | async-done | bytes 786456 | tf_op jit(solution)/shard_map/slice | solution.py:296
  63.8 1.0 %fusion.22 = bf16[4,1,4,64,256]{4,3,0,2,1:T(8,128)(2,1)S(1)} fusion(f32[4,3,64,256]{3,2,0,1:T(8,128)S(1)} %pad_slice_fusion.1, f32[4,3,64,256]{3,2,0,1:T(8,128)S(1)} %pad_slice_fusion.3, f32[4,3,64,256]{3,2,0,1:T(8,128)S(1)} %slice-done.1, f32[4,3,64,256]{3,2,0,1:T(8,128)S(1)} %slice-done, f32[4,4,64,255]{3,2,0,1:T(8,128)S(1)} %slice.208, ...), kind=kOutput, calls=%fused_computation.39 | convolution fusion | flops 38010880 | bytes 7374848 | tf_op jit(solution)/shard_map/frdx,cd->frcx/dot_general | solution.py:284
  64.8 0.8 %copy.106 = bf16[4,1,4,64,256]{4,3,2,1,0:T(8,128)(2,1)} copy(bf16[4,1,4,64,256]{4,3,0,2,1:T(8,128)(2,1)S(1)} %fusion.22) | data formatting | bytes 1048576
  65.9 0.7 %copy.216 = f32[7,64,64]{2,1,0:T(8,128)} copy(f32[7,64,64]{2,1,0:T(8,128)S(1)} %copy-done.11) | data formatting | bytes 229376
  66.6 0.6 copy.217
  (109 shorter events, 11.9 us)
Async XLA Ops:
  5.0 13.5 %copy-start = (bf16[4,1,4,64,256]{4,3,2,1,0:T(8,128)(2,1)S(1)}, bf16[4,1,4,64,256]{4,3,2,1,0:T(8,128)(2,1)}, u32[]{:S(2)}) copy-start(bf16[4,1,4,64,256]{4,3,2,1,0:T(8,128)(2,1)} %param.6) | copy-start | bytes 1572868
  5.0 13.5 %copy-start.9 = (bf16[7,64,64]{2,1,0:T(8,128)(2,1)S(1)}, bf16[7,64,64]{2,1,0:T(8,128)(2,1)}, u32[]{:S(2)}) copy-start(bf16[7,64,64]{2,1,0:T(8,128)(2,1)} %param.8) | copy-start | bytes 172036
  19.5 0.8 %copy-start.5 = (bf16[4,6,64,1]{3,2,1,0:T(8,128)(2,1)}, bf16[4,6,64,1]{3,2,1,0:T(8,128)(2,1)S(1)}, u32[]{:S(2)}) copy-start(bf16[4,6,64,1]{3,2,1,0:T(8,128)(2,1)S(1)} %copy.67) | copy-start | bytes 9220
  21.8 1.8 %copy-start.12 = (bf16[4,64,256]{2,1,0:T(8,128)(2,1)S(1)}, bf16[4,64,256]{2,1,0:T(8,128)(2,1)}, u32[]{:S(2)}) copy-start(bf16[4,64,256]{2,1,0:T(8,128)(2,1)} %get-tuple-element.14) | copy-start | bytes 393220
  21.8 1.8 %copy-start.13 = (bf16[4,64,256]{2,1,0:T(8,128)(2,1)S(1)}, bf16[4,64,256]{2,1,0:T(8,128)(2,1)}, u32[]{:S(2)}) copy-start(bf16[4,64,256]{2,1,0:T(8,128)(2,1)} %get-tuple-element.13) | copy-start | bytes 393220
  21.8 1.8 %copy-start.1 = (bf16[4,1,4,64,256]{4,3,2,1,0:T(8,128)(2,1)S(1)}, bf16[4,1,4,64,256]{4,3,2,1,0:T(8,128)(2,1)}, u32[]{:S(2)}) copy-start(bf16[4,1,4,64,256]{4,3,2,1,0:T(8,128)(2,1)} %param.7) | copy-start | bytes 1572868
  23.7 0.8 %copy-start.15 = (bf16[3,64,64]{2,1,0:T(8,128)(2,1)S(1)}, bf16[3,64,64]{2,1,0:T(8,128)(2,1)}, u32[]{:S(2)}) copy-start(bf16[3,64,64]{2,1,0:T(8,128)(2,1)} %param.9) | copy-start | bytes 73732
  24.7 1.2 %copy-start.8 = (f32[4,4,64,256]{3,2,1,0:T(8,128)S(1)}, f32[4,4,64,256]{3,2,1,0:T(8,128)}, u32[]{:S(2)}) copy-start(f32[4,4,64,256]{3,2,1,0:T(8,128)} %get-tuple-element.52) | copy-start | bytes 3145732
  26.8 1.0 %copy-start.6 = (bf16[4,6,64,1]{3,2,1,0:T(8,128)(2,1)S(1)}, bf16[4,6,64,1]{3,2,1,0:T(8,128)(2,1)}, u32[]{:S(2)}) copy-start(bf16[4,6,64,1]{3,2,1,0:T(8,128)(2,1)} %copy-done.5) | copy-start | bytes 9220
  28.7 1.0 %copy-start.7 = (bf16[4,4,64,256]{3,2,1,0:T(8,128)(2,1)S(1)}, bf16[4,4,64,256]{3,2,1,0:T(8,128)(2,1)}, u32[]{:S(2)}) copy-start(bf16[4,4,64,256]{3,2,1,0:T(8,128)(2,1)} %get-tuple-element.51) | copy-start | bytes 1572868
  31.4 0.7 copy-start.10
  32.4 1.0 %copy-start.3 = (f32[4,4,64,256]{3,2,0,1:T(8,128)}, f32[4,4,64,256]{3,2,0,1:T(8,128)S(1)}, u32[]{:S(2)}) copy-start(f32[4,4,64,256]{3,2,0,1:T(8,128)S(1)} %convolution_bitcast_fusion.3) | copy-start | bytes 3145732
  34.6 1.0 %copy-start.4 = (f32[4,4,64,256]{3,2,0,1:T(8,128)}, f32[4,4,64,256]{3,2,0,1:T(8,128)S(1)}, u32[]{:S(2)}) copy-start(f32[4,4,64,256]{3,2,0,1:T(8,128)S(1)} %convolution_bitcast_fusion.2) | copy-start | bytes 3145732
  36.4 21.3 %copy-start.19 = (s32[32]{0:T(128)S(1)}, s32[32]{0:T(128)}, u32[]{:S(2)}) copy-start(s32[32]{0:T(128)} %get-tuple-element.42) | copy-start | bytes 388
  36.4 21.6 %copy-start.17 = (s32[32]{0:T(128)S(1)}, s32[32]{0:T(128)}, u32[]{:S(2)}) copy-start(s32[32]{0:T(128)} %get-tuple-element.41) | copy-start | bytes 388
  36.9 23.5 %copy-start.18 = (s32[32]{0:T(128)S(1)}, s32[32]{0:T(128)}, u32[]{:S(2)}) copy-start(s32[32]{0:T(128)} %get-tuple-element.58) | copy-start | bytes 388
  36.9 23.9 %copy-start.16 = (s32[32]{0:T(128)S(1)}, s32[32]{0:T(128)}, u32[]{:S(2)}) copy-start(s32[32]{0:T(128)} %get-tuple-element.59) | copy-start | bytes 388
  62.2 1.1 %slice-start.1 = ((f32[4,4,64,256]{3,2,0,1:T(8,128)}), f32[4,3,64,256]{3,2,0,1:T(8,128)S(1)}, s32[]{:S(2)}) async-start(f32[4,4,64,256]{3,2,0,1:T(8,128)} %copy-done.4), calls=%async_computation.1 | async-start | bytes 1572864 | tf_op jit(solution)/shard_map/slice | solution.py:296
  62.2 1.3 %copy-start.2 = (bf16[4,1,4,64,256]{4,3,2,1,0:T(8,128)(2,1)S(1)}, bf16[4,1,4,64,256]{4,3,2,1,0:T(8,128)(2,1)}, u32[]{:S(2)}) copy-start(bf16[4,1,4,64,256]{4,3,2,1,0:T(8,128)(2,1)} %param.7) | copy-start | bytes 1572868
  62.3 1.5 %slice-start = ((f32[4,4,64,256]{3,2,0,1:T(8,128)}), f32[4,3,64,256]{3,2,0,1:T(8,128)S(1)}, s32[]{:S(2)}) async-start(f32[4,4,64,256]{3,2,0,1:T(8,128)} %copy-done.3), calls=%async_computation | async-start | bytes 1572864 | tf_op jit(solution)/shard_map/slice | solution.py:293
  64.8 1.0 %copy-start.11 = (f32[7,64,64]{2,1,0:T(8,128)S(1)}, f32[7,64,64]{2,1,0:T(8,128)}, u32[]{:S(2)}) copy-start(f32[7,64,64]{2,1,0:T(8,128)} %get-tuple-element.68) | copy-start | bytes 344068
  64.8 1.7 %copy-start.14 = (f32[3,64,64]{2,1,0:T(8,128)S(1)}, f32[3,64,64]{2,1,0:T(8,128)}, u32[]{:S(2)}) copy-start(f32[3,64,64]{2,1,0:T(8,128)} %get-tuple-element.69) | copy-start | bytes 147460
